TPU v7x, 256 devices: a whole 4x4x8 slice. The times are simulated.
256 devices in a mesh: row: 8 (over z_hi, y), col: 32 (over z_lo, x, core).
Axes of the slice: x: 4, y: 4, z: 8 (z_hi: 2, z_lo: 4; z = z_hi * 4 + z_lo), core: 2. Of those that a mesh axis runs over, the one named last changes fastest.
Arguments:
- queries: bfloat16 [32768, 256], P(('row', 'col')), may hold values from -6 to 6
- keys: bfloat16 [32768, 256], P('col', 'row'), may hold values from -6 to 6
- values: bfloat16 [32768, 256], P('col', 'row'), may hold values from -0.59765625 to 0.59765625
- outputs: bfloat16 [32768, 256], P(('row', 'col')), may hold values from -0.59765625 to 0.59765625
- d_out: bfloat16 [32768, 256], P(('row', 'col')), may hold values from -6 to 6
- lse: float32 [2, 32768], P(None, ('row', 'col')), may hold values from 4 to 6
Outputs:
- d_queries: bfloat16 [32768, 256], P(('row', 'col'))
- d_keys: bfloat16 [32768, 256], P('col', 'row')
- d_values: bfloat16 [32768, 256], P('col', 'row')
All inputs are finite; a program needn't handle non-finite values.
Results may differ from a plain program's by a relative error of at most 0.0049.
Values may be sent and summed in bfloat16 or wider, within the bound.
No kernel may reach another device: no remote copies, remote signals or barrier semaphores. Data moves between devices by JAX's collectives and lax.ppermute only.
A program may use at most 64 MiB of HBM per device.

v0:
```python
import jax
import jax.numpy as jnp
from jax import lax
from jax.sharding import PartitionSpec as P


def block_size(row_total):
    block_rows = row_total
    while block_rows > 512 and block_rows % 2 == 0:
        block_rows = block_rows // 2
    return block_rows


def head_slice(matrix, head_index, head_dim):
    return matrix[:, head_index * head_dim : (head_index + 1) * head_dim]


def contract_rows(left, right):
    return lax.dot_general(
        left, right, (((0,), (0,)), ((), ())), preferred_element_type=jnp.float32
    )


def score_terms(query_head, grad_head, lse_row, delta_row, key_head, value_head, scaling):
    scores = jnp.dot(query_head, key_head.T, preferred_element_type=jnp.float32)
    probs = jnp.exp(scores * scaling - lse_row[:, None])
    probs_low = probs.astype(jnp.bfloat16)
    grad_probs = jnp.dot(grad_head, value_head.T, preferred_element_type=jnp.float32)
    grad_scores = (probs * (grad_probs - delta_row[:, None])).astype(jnp.bfloat16)
    return (probs_low, grad_scores)


def block_grads(query_rows, grad_rows, lse_rows, delta_rows, key_all, value_all, head_dim):
    head_total = lse_rows.shape[0]
    scaling = head_dim ** (-0.5)
    key_terms = []
    value_terms = []
    query_terms = []
    for head_index in range(head_total):
        query_head = head_slice(query_rows, head_index, head_dim)
        grad_head = head_slice(grad_rows, head_index, head_dim)
        key_head = head_slice(key_all, head_index, head_dim)
        value_head = head_slice(value_all, head_index, head_dim)
        probs_low, grad_scores = score_terms(
            query_head,
            grad_head,
            lse_rows[head_index],
            delta_rows[head_index],
            key_head,
            value_head,
            scaling,
        )
        value_terms.append(contract_rows(probs_low, grad_head))
        key_terms.append(contract_rows(grad_scores, query_head))
        query_terms.append(jnp.dot(grad_scores, key_head, preferred_element_type=jnp.float32))
    key_term = jnp.concatenate(key_terms, axis=1)
    value_term = jnp.concatenate(value_terms, axis=1)
    query_term = jnp.concatenate(query_terms, axis=1)
    return (key_term, value_term, query_term)


def split_blocks(query_all, grad_all, lse_all, delta_all):
    row_total, features = query_all.shape
    block_rows = block_size(row_total)
    steps_total = row_total // block_rows
    head_total = lse_all.shape[0]
    query_blocks = query_all.reshape(steps_total, block_rows, features)
    grad_blocks = grad_all.reshape(steps_total, block_rows, features)
    lse_blocks = lse_all.reshape(head_total, steps_total, block_rows).transpose(1, 0, 2)
    delta_blocks = delta_all.reshape(head_total, steps_total, block_rows).transpose(1, 0, 2)
    return (query_blocks, grad_blocks, lse_blocks, delta_blocks)


def query_pass(query_all, grad_all, lse_all, delta_all, key_all, value_all, head_dim):
    row_total, features = query_all.shape
    block_inputs = split_blocks(query_all, grad_all, lse_all, delta_all)
    empty_sums = jnp.zeros((key_all.shape[0], features), jnp.float32)

    def advance(running, inputs):
        key_sum, value_sum = running
        query_rows, grad_rows, lse_rows, delta_rows = inputs
        key_term, value_term, query_term = block_grads(
            query_rows, grad_rows, lse_rows, delta_rows, key_all, value_all, head_dim
        )
        return ((key_sum + key_term, value_sum + value_term), query_term)

    (key_sum, value_sum), query_terms = lax.scan(advance, (empty_sums, empty_sums), block_inputs)
    query_terms = query_terms.reshape(row_total, features)
    return (key_sum, value_sum, query_terms)


def head_delta(d_out, outputs, head_total, head_dim):
    product = d_out.astype(jnp.float32) * outputs.astype(jnp.float32)
    return jnp.sum(product.reshape(product.shape[0], head_total, head_dim), axis=2).T


def per_device(queries, keys, values, outputs, d_out, lse):
    head_total = lse.shape[0]
    head_dim = queries.shape[1] // head_total
    scaling = head_dim ** (-0.5)
    delta = head_delta(d_out, outputs, head_total, head_dim)
    key_all, value_all = (
        lax.all_gather(keys, "row", axis=1, tiled=True),
        lax.all_gather(values, "row", axis=1, tiled=True),
    )
    query_all, grad_all = (
        lax.all_gather(queries, "col", axis=0, tiled=True),
        lax.all_gather(d_out, "col", axis=0, tiled=True),
    )
    lse_all, delta_all = (
        lax.all_gather(lse, "col", axis=1, tiled=True),
        lax.all_gather(delta, "col", axis=1, tiled=True),
    )
    key_sum, value_sum, query_terms = query_pass(
        query_all, grad_all, lse_all, delta_all, key_all, value_all, head_dim
    )
    query_grad = lax.psum_scatter(query_terms, "col", scatter_dimension=0, tiled=True)
    key_grad, value_grad = (
        lax.psum_scatter(key_sum, "row", scatter_dimension=1, tiled=True),
        lax.psum_scatter(value_sum, "row", scatter_dimension=1, tiled=True),
    )
    d_queries = (query_grad * scaling).astype(jnp.bfloat16)
    d_keys = (key_grad * scaling).astype(jnp.bfloat16)
    d_values = value_grad.astype(jnp.bfloat16)
    return (d_queries, d_keys, d_values)


def solution(mesh):
    placed = (
        P(("row", "col"), None),
        P("col", "row"),
        P("col", "row"),
        P(("row", "col"), None),
        P(("row", "col"), None),
        P(None, ("row", "col")),
    )
    return jax.shard_map(
        per_device,
        mesh=mesh,
        in_specs=placed,
        out_specs=(P(("row", "col"), None), P("col", "row"), P("col", "row")),
        check_vma=False,
    )
```

profile of v0, /device:TPU:1, one launch (start us, length us, event | category | flops | bytes accessed | tf_op | source)
XLA Modules:
  0.0 608.8 jit_solution(17690217975706771563)
XLA Ops:
  9.7 42.3 %all_gather.19 = bf16[1024,256]{0,1:T(8,128)(2,1)S(1)} all-gather(bf16[1024,32]{0,1:T(8,128)(2,1)} %param.9), channel_id=1, replica_groups=mesh['row'=8,'col'=32] {'row'}, dimensions={1}, use_global_device_ids=true | all-gather | bytes 589824 | tf_op jit(solution)/shard_map/all_gather | solution.py:103
  52.2 39.7 %all_gather.22 = bf16[1024,256]{0,1:T(8,128)(2,1)S(1)} all-gather(bf16[1024,32]{0,1:T(8,128)(2,1)S(1)} %copy-done.1), channel_id=1, replica_groups=mesh['row'=8,'col'=32] {'row'}, dimensions={1}, use_global_device_ids=true | all-gather | bytes 589824 | tf_op jit(solution)/shard_map/all_gather | solution.py:104
  92.3 64.6 %all_gather.23 = f32[2,4096]{0,1:T(8,128)} all-gather(f32[2,128]{0,1:T(8,128)S(1)} %bitcast.55), channel_id=1, replica_groups=mesh['row'=8,'col'=32] {'col'}, dimensions={1}, use_global_device_ids=true | all-gather | bytes 33792 | tf_op jit(solution)/shard_map/all_gather | solution.py:112
  157.0 2.2 copy.19
  159.2 37.9 %all_gather.20 = f32[2,4096]{1,0:T(2,128)S(1)} all-gather(f32[2,128]{1,0:T(2,128)S(1)} %copy-done.2), channel_id=1, replica_groups=mesh['row'=8,'col'=32] {'col'}, dimensions={1}, use_global_device_ids=true | all-gather | bytes 33792 | tf_op jit(solution)/shard_map/all_gather | solution.py:111
  197.1 87.0 %while.15 = (s32[]{:T(128)}, f32[1024,256]{0,1:T(8,128)}, f32[1024,256]{0,1:T(8,128)S(1)}, f32[8,512,256]{2,1,0:T(8,128)}, bf16[8,512,256]{2,1,0:T(8,128)(2,1)},...) while((s32[]{:T(128)}, f32[1024,256]{0,1:T(8,128)}, ...), condition=%wide.region_2.3_spmd.clone, body=%wide.region_1.2_spmd.clone.sunk | while | flops 1352269824 | bytes 34631860 | solution.py:87
  197.1 1.0 dynamic-slice_bitcast_fusion.5
  198.1 1.0 dynamic-slice_bitcast_fusion.4
  204.0 1.8 maximum_add_fusion.3
  206.9 1.0 dynamic-slice_bitcast_fusion.5
  207.9 1.0 dynamic-slice_bitcast_fusion.4
  213.8 3.0 maximum_add_fusion.3
  217.9 1.0 dynamic-slice_bitcast_fusion.5
  218.9 1.0 dynamic-slice_bitcast_fusion.4
  224.8 3.0 maximum_add_fusion.3
  229.0 1.0 dynamic-slice_bitcast_fusion.5
  229.9 1.0 dynamic-slice_bitcast_fusion.4
  235.9 3.0 maximum_add_fusion.3
  241.0 1.0 dynamic-slice_bitcast_fusion.4
  246.9 3.0 maximum_add_fusion.3
  251.0 1.0 dynamic-slice_bitcast_fusion.5
  258.0 3.0 maximum_add_fusion.3
  263.0 1.0 dynamic-slice_bitcast_fusion.4
  269.0 3.0 maximum_add_fusion.3
  273.1 1.0 dynamic-slice_bitcast_fusion.5
  280.0 3.0 maximum_add_fusion.3
  286.2 82.3 %reduce-scatter.8.cloned.1.call-done = f32[1024,32]{0,1:T(8,128)} async-done(((f32[1024,256]{0,1:T(8,128)}), f32[1024,32]{0,1:T(8,128)}) %reduce-scatter.8.cloned.1.call-update) | async-done | bytes 131088 | tf_op jit(solution)/shard_map/reduce_scatter | solution.py:120
  368.5 1.5 convert_element_type.31
  370.0 85.5 %reduce-scatter.6.cloned.1.call-done = f32[1024,32]{0,1:T(8,128)} async-done(((f32[1024,256]{0,1:T(8,128)}), f32[1024,32]{0,1:T(8,128)}) %reduce-scatter.6.cloned.1.call-update) | async-done | bytes 131088 | tf_op jit(solution)/shard_map/reduce_scatter | solution.py:119
  455.6 1.5 multiply_convert_fusion.2
  457.1 143.7 %reduce-scatter.4.cloned.1.call-done = f32[128,256]{1,0:T(8,128)} async-done(((f32[4096,256]{1,0:T(8,128)}), f32[128,256]{1,0:T(8,128)}) %reduce-scatter.4.cloned.1.call-update) | async-done | bytes 131088 | tf_op jit(solution)/shard_map/reduce_scatter | solution.py:117
  600.8 1.5 multiply_convert_fusion.3
  (150 shorter events, 57.2 us)
Async XLA Ops:
  7.2 45.1 %copy-start.1 = (bf16[1024,32]{0,1:T(8,128)(2,1)S(1)}, bf16[1024,32]{0,1:T(8,128)(2,1)}, u32[]{:S(2)}) copy-start(bf16[1024,32]{0,1:T(8,128)(2,1)} %param.10) | copy-start | bytes 196612
  7.2 189.9 %all-gather.3.cloned.1.call-start = ((), (), s32[]{:S(2)}) async-start(), calls=%async_computation.3 | async-start | bytes 2162688 | tf_op jit(solution)/shard_map/all_gather | solution.py:107
  7.9 189.2 %all-gather.5.cloned.1.call-start = ((), (), s32[]{:S(2)}) async-start(), calls=%async_computation.4 | async-start | bytes 2162688 | tf_op jit(solution)/shard_map/all_gather | solution.py:108
  8.7 359.8 %reduce-scatter.8.cloned.1.call-start = ((), (), s32[]{:S(2)}) async-start(), calls=%async_computation.7 | async-start | bytes 1179648 | tf_op jit(solution)/shard_map/reduce_scatter | solution.py:120
  92.3 66.8 %copy-start.2 = (f32[2,128]{1,0:T(2,128)S(1)}, f32[2,128]{1,0:T(2,128)}, u32[]{:S(2)}) copy-start(f32[2,128]{1,0:T(2,128)} %param.13) | copy-start | bytes 3076
  284.1 1.0 copy-start
  285.0 170.5 %reduce-scatter.6.cloned.1.call-start = ((), (), s32[]{:S(2)}) async-start(), calls=%async_computation.6 | async-start | bytes 1179648 | tf_op jit(solution)/shard_map/reduce_scatter | solution.py:119
  285.6 315.1 %reduce-scatter.4.cloned.1.call-start = ((), (), s32[]{:S(2)}) async-start(), calls=%async_computation.5 | async-start | bytes 4325376 | tf_op jit(solution)/shard_map/reduce_scatter | solution.py:117
Sparse Core Ops, SparseCore 0:
  9.9 65.1 all-gather.2
  76.9 59.4 all-gather.4
  285.2 83.2 reduce-scatter.7
  372.8 82.7 reduce-scatter.5
  457.9 142.7 reduce-scatter.3
where the time goes:
time: 614 us; the launch traced here: 609 us
  waiting for transfers between devices  314 us (51%)
  blocking collectives  185 us (30%)
  matrix products  39.4 us (6%)
  other arithmetic  28.6 us (5%)
  local copies, waits for them, and re-layouts  27.7 us (5%)
  between operations  13.9 us (2%)
    reduce_scatter x1, waiting for transfers between devices, per_device(): lax.psum_scatter(query_terms, 'col', scatter_dimension=0, tiled=True)  144 us
    reduce_scatter x1, waiting for transfers between devices, per_device(): lax.psum_scatter(key_sum, 'row', scatter_dimension=1, tiled=True)  85.5 us
    reduce_scatter x1, waiting for transfers between devices, per_device(): lax.psum_scatter(value_sum, 'row', scatter_dimension=1, tiled=True)  82.3 us
    all_gather x1, blocking collectives, per_device(): lax.all_gather(delta, 'col', axis=1, tiled=True)  64.6 us
    all_gather x1, blocking collectives, per_device(): lax.all_gather(keys, 'row', axis=1, tiled=True)  42.3 us
    all_gather x1, blocking collectives, per_device(): lax.all_gather(values, 'row', axis=1, tiled=True)  39.7 us
    all_gather x1, blocking collectives, per_device(): lax.all_gather(lse, 'col', axis=1, tiled=True)  37.9 us
    add x8, other arithmetic, advance(): return ((key_sum + key_term, value_sum + value_term), query_term)  22.6 us
  transfers between devices with their start and end apart: 5, of which 3 were waited for; matrix products, arithmetic and copies ran while one was open for 1% of the time, Pallas kernels for 0%

commit v1 on v0

v1 whole, which is shorter than its diff:
```python
import functools
import math

import jax
import jax.numpy as jnp
from jax import lax
from jax.experimental import pallas as pl
from jax.experimental.pallas import tpu as pltpu
from jax.sharding import Mesh
from jax.sharding import PartitionSpec as P

F32 = jnp.float32
BF16 = jnp.bfloat16
HEAD_DIM = 128
ROWS = 128
KEYS = 1024
FEATS = 32
SIDE = 16
MSG = 2 * ROWS + SIDE
SCALING = HEAD_DIM ** (-0.5)
LOG2E = math.log2(math.e)
NT = (((1,), (1,)), ((), ()))
NN = (((1,), (0,)), ((), ()))
TN = (((0,), (0,)), ((), ()))
VMEM = pl.BlockSpec(memory_space=pltpu.VMEM)


def dot(left, right, dims):
    return lax.dot_general(left, right, dims, preferred_element_type=F32)


def split3(value):
    high = value.astype(BF16).astype(F32)
    middle = (value - high).astype(BF16).astype(F32)
    return high, middle, value - high - middle


def call(body, out_shape, operands, name, flops=0, moved=4 * 2**20, scratch=(), aliases=None):
    return pl.pallas_call(
        body,
        out_shape=out_shape,
        in_specs=[VMEM] * len(operands),
        out_specs=jax.tree.map(lambda _: VMEM, out_shape),
        scratch_shapes=list(scratch),
        input_output_aliases=aliases or {},
        compiler_params=pltpu.CompilerParams(vmem_limit_bytes=48 * 2**20),
        cost_estimate=pl.CostEstimate(flops=flops, bytes_accessed=moved, transcendentals=0),
        name=name,
    )(*operands)


def pack_queries(q_ref, do_ref, o_ref, lse_ref, msg_ref):
    product = do_ref[...].astype(F32) * o_ref[...].astype(F32)
    row = lax.broadcasted_iota(jnp.int32, (SIDE, ROWS), 0)
    for head in range(2):
        cols = pl.ds(head * HEAD_DIM, HEAD_DIM)
        part = product[:, head * HEAD_DIM : (head + 1) * HEAD_DIM]
        delta = jnp.sum(part.T, axis=0, keepdims=True)
        terms = split3(lse_ref[head : head + 1, :] * LOG2E) + split3(delta)
        side = jnp.zeros((SIDE, ROWS), F32)
        for index, term in enumerate(terms):
            side = jnp.where(row == index, jnp.broadcast_to(term, (SIDE, ROWS)), side)
        side = side.astype(BF16)
        for place in range(4):
            target = head * 4 + place
            msg_ref[target, 0:ROWS, :] = q_ref[:, cols]
            msg_ref[target, ROWS : 2 * ROWS, :] = do_ref[:, cols]
            msg_ref[target, 2 * ROWS : MSG, :] = side


def pack_keys(k_ref, v_ref, kv_ref):
    kv_ref[0:FEATS, :] = k_ref[...]
    kv_ref[FEATS : 2 * FEATS, :] = v_ref[...]


def join_keys(y_ref, own_ref, next_ref, prev_ref, far_ref, kv_ref, kt, vt):
    y = y_ref[0]
    for shift, ref in ((0, own_ref), (3, prev_ref), (1, next_ref), (2, far_ref)):
        source = lax.rem(y + shift, 4)
        rows = pl.ds(pl.multiple_of(source * FEATS, FEATS), FEATS)
        kt[rows, :] = ref[0:FEATS, :].astype(F32)
        vt[rows, :] = ref[FEATS : 2 * FEATS, :].astype(F32)
    kv_ref[0] = kt[...].T.astype(BF16)
    kv_ref[1] = vt[...].T.astype(BF16)


def attend(halves, tile, with_dq, last, fresh, *refs):
    refs = list(refs)
    msg_ref = refs.pop(0)
    kv_refs = [refs.pop(0) for _ in range(halves)]
    acc_in = [None if fresh else refs.pop(0) for _ in range(halves)]
    dq_in = refs.pop(0) if with_dq else None
    dq_out = refs.pop(0)
    acc_out = [refs.pop(0) for _ in range(halves)]
    q_s, do_s, st_s, dq_s = refs
    for place in range(8):
        rows = pl.ds(place * ROWS, ROWS)
        q_s[rows, :] = msg_ref[place, 0:ROWS, :]
        do_s[rows, :] = msg_ref[place, ROWS : 2 * ROWS, :]
        side = msg_ref[place, 2 * ROWS : MSG, :].astype(F32)
        st_s[0:1, rows] = side[0:1] + side[1:2] + side[2:3]
        st_s[1:2, rows] = side[3:4] + side[4:5] + side[5:6]
    if with_dq:
        dq_s[...] = dq_in[...]
    else:
        dq_s[...] = jnp.zeros_like(dq_s)
    total = 8 * ROWS
    for half in range(halves):
        kv_ref, accum_in, accum_out = kv_refs[half], acc_in[half], acc_out[half]

        def step(index, _, kv_ref=kv_ref, accum_in=accum_in, accum_out=accum_out):
            ks = pl.ds(pl.multiple_of(index * tile, tile), tile)
            key, value = kv_ref[0, ks, :], kv_ref[1, ks, :]
            if accum_in is None:
                dk = dv = jnp.zeros((tile, HEAD_DIM), F32)
            else:
                dk, dv = accum_in[0, ks, :], accum_in[1, ks, :]
            for start in range(0, total, 256):
                qs = pl.ds(start, 256)
                query, grad = q_s[qs, :], do_s[qs, :]
                scores = dot(key, query, NT)
                probs = jnp.exp2(scores * (SCALING * LOG2E) - st_s[0:1, qs])
                grad_probs = dot(value, grad, NT)
                grad_scores = (probs * (grad_probs - st_s[1:2, qs])).astype(BF16)
                dv = dv + dot(probs.astype(BF16), grad, NN)
                dk = dk + dot(grad_scores, query, NN)
                dq_s[qs, :] += dot(grad_scores, key, TN)
            accum_out[0, ks, :] = dk
            accum_out[1, ks, :] = dv
            return 0

        lax.fori_loop(0, KEYS // tile, step, 0)
    if last:
        for place in range(8):
            dq_out[place] = dq_s[pl.ds(place * ROWS, ROWS), :].astype(BF16)
    else:
        dq_out[...] = dq_s[...]


def attend_call(msg, kvs, accs, dq_in, last, name):
    halves = len(kvs)
    fresh = accs is None
    operands = [msg] + list(kvs) + ([] if fresh else list(accs))
    aliases = {} if fresh else {1 + halves + i: 1 + i for i in range(halves)}
    if dq_in is not None:
        operands.append(dq_in)
    if last:
        dq_shape = jax.ShapeDtypeStruct((8, ROWS, HEAD_DIM), BF16)
    else:
        dq_shape = jax.ShapeDtypeStruct((8 * ROWS, HEAD_DIM), F32)
    out = (dq_shape,) + (jax.ShapeDtypeStruct((2, KEYS, HEAD_DIM), F32),) * halves
    body = functools.partial(attend, halves, 1024, dq_in is not None, last, fresh)
    results = call(
        body,
        out,
        operands,
        name,
        flops=halves * 10 * 1024 * 1024 * 128,
        moved=halves * 8 * 2**20,
        scratch=[
            pltpu.VMEM((8 * ROWS, HEAD_DIM), BF16),
            pltpu.VMEM((8 * ROWS, HEAD_DIM), BF16),
            pltpu.VMEM((8, 8 * ROWS), F32),
            pltpu.VMEM((8 * ROWS, HEAD_DIM), F32),
        ],
        aliases=aliases,
    )
    return results[0], results[1:]


def add_queries(own_ref, a_ref, b_ref, c_ref, out_ref):
    total = own_ref[...].astype(F32) + a_ref[...].astype(F32)
    total = total + b_ref[...].astype(F32) + c_ref[...].astype(F32)
    out_ref[...] = total.astype(BF16)


def finish_queries(in_ref, out_ref):
    for head in range(2):
        total = in_ref[head * 4].astype(F32)
        for place in range(1, 4):
            total = total + in_ref[head * 4 + place].astype(F32)
        out_ref[:, head * HEAD_DIM : (head + 1) * HEAD_DIM] = (total * SCALING).astype(BF16)


def pack_sums(core_ref, own_ref, other_ref, out_ref):
    core = core_ref[0]
    for index, ref in ((core, own_ref), (1 - core, other_ref)):
        dk = (ref[0] * SCALING).T.astype(BF16)
        dv = ref[1].T.astype(BF16)
        for y in range(4):
            rows = slice(y * FEATS, (y + 1) * FEATS)
            out_ref[2 * y + index, 0:FEATS, :] = dk[rows]
            out_ref[2 * y + index, FEATS : 2 * FEATS, :] = dv[rows]


def finish_keys(in_ref, dk_ref, dv_ref):
    total = in_ref[0].astype(F32)
    for place in range(1, 8):
        total = total + in_ref[place].astype(F32)
    dk_ref[...] = total[0:FEATS].astype(BF16)
    dv_ref[...] = total[FEATS : 2 * FEATS].astype(BF16)


def shift(value, axis, size, amount):
    return lax.ppermute(value, axis, [(i, (i + amount) % size) for i in range(size)])


def per_device(queries, keys, values, outputs, d_out, lse):
    sds = jax.ShapeDtypeStruct
    y = lax.axis_index("y").astype(jnp.int32).reshape(1)
    core = lax.axis_index("c").astype(jnp.int32).reshape(1)
    smem = pl.BlockSpec(memory_space=pltpu.SMEM)

    kvt = call(pack_keys, sds((2 * FEATS, KEYS), BF16), [keys.T, values.T], "pack_keys")
    kv_next = shift(kvt, "y", 4, 3)
    kv_prev = shift(kvt, "y", 4, 1)
    kv_far = shift(kvt, "y", 4, 2)

    msg = call(
        pack_queries, sds((8, MSG, HEAD_DIM), BF16), [queries, d_out, outputs, lse], "pack_queries"
    )
    q_own = lax.all_to_all(msg, ("zh", "zl"), 0, 0, tiled=True)
    q_prev = shift(q_own, "x", 4, 1)
    q_next = shift(q_own, "x", 4, 3)
    cut = MSG // 2
    q_far = jnp.concatenate(
        [shift(q_prev[:, :cut], "x", 4, 1), shift(q_next[:, cut:], "x", 4, 3)], axis=1
    )

    kv_own = pl.pallas_call(
        join_keys,
        out_shape=sds((2, KEYS, HEAD_DIM), BF16),
        in_specs=[smem] + [VMEM] * 4,
        out_specs=VMEM,
        scratch_shapes=[pltpu.VMEM((HEAD_DIM, KEYS), F32)] * 2,
        name="join_keys",
    )(y, kvt, kv_next, kv_prev, kv_far)
    kv_other = shift(kv_own, "c", 2, 1)

    dq0, (acc_own,) = attend_call(q_own, [kv_own], None, None, False, "attend_own_a")
    dq0, (acc_other,) = attend_call(q_own, [kv_other], None, dq0, True, "attend_own_b")
    kvs = [kv_own, kv_other]
    dq_p, accs = attend_call(q_prev, kvs, [acc_own, acc_other], None, True, "attend_prev")
    dq_n, accs = attend_call(q_next, kvs, accs, None, True, "attend_next")
    dq_f, accs = attend_call(q_far, kvs, accs, None, True, "attend_far")
    back_p = shift(dq_p, "x", 4, 3)
    back_n = shift(dq_n, "x", 4, 1)
    back_f = shift(dq_f, "x", 4, 2)

    sums = pl.pallas_call(
        pack_sums,
        out_shape=sds((8, 2 * FEATS, KEYS), BF16),
        in_specs=[smem] + [VMEM] * 2,
        out_specs=VMEM,
        name="pack_sums",
    )(core, *accs)
    sums = lax.all_to_all(sums, ("y", "c"), 0, 0, tiled=True)
    dq = call(
        add_queries, sds((8, ROWS, HEAD_DIM), BF16), [dq0, back_p, back_n, back_f], "add_queries"
    )
    dq = lax.all_to_all(dq, ("zh", "zl"), 0, 0, tiled=True)
    d_queries = call(finish_queries, sds((ROWS, 2 * HEAD_DIM), BF16), [dq], "finish_queries")
    d_keys, d_values = call(
        finish_keys, (sds((FEATS, KEYS), BF16),) * 2, [sums], "finish_keys"
    )
    return d_queries, d_keys.T, d_values.T


def solution(mesh):
    every = ("zh", "y", "zl", "x", "c")
    fine = Mesh(mesh.devices.reshape(2, 4, 4, 4, 2), every)
    placed = (
        P(every, None),
        P(("zl", "x", "c"), ("zh", "y")),
        P(("zl", "x", "c"), ("zh", "y")),
        P(every, None),
        P(every, None),
        P(None, every),
    )
    return jax.shard_map(
        per_device,
        mesh=fine,
        in_specs=placed,
        out_specs=(placed[0], placed[1], placed[2]),
        check_vma=False,
    )
```

time: 614 us -> 117 us (0.19)
  waiting for transfers between devices: 314 us -> 41.2 us
  blocking collectives: 185 us -> 0 us
  matrix products: 39.4 us -> 0 us
  starting transfers between devices: 0.19 us -> 37.3 us
  Pallas kernels: 0 us -> 31.5 us
  other arithmetic: 28.6 us -> 0.04 us
  local copies, waits for them, and re-layouts: 27.7 us -> 5.93 us
  between operations: 13.9 us -> 0.81 us
    reduce_scatter x3 -> x0, waiting for transfers between devices: 311 us -> none  [the longest x1 144 us: per_device(): lax.psum_scatter(query_terms, 'col', scatter_dimension=0, tiled=True)]
    all_gather x4 -> x0, blocking collectives: 185 us -> none  [the longest x1 64.6 us: per_device(): lax.all_gather(delta, 'col', axis=1, tiled=True)]
    dot_general x80 -> x0, matrix products: 39.4 us -> none  [the longest x32 14.9 us: contract_rows(): lax.dot_general(left, right, (((0,), (0,)), ((), ())), preferred_element_...]
    pallas_call x0 -> x12, Pallas kernels: none -> 31.5 us  [the longest x10 26.5 us: call(): pl.pallas_call(body, out_shape=out_shape, in_specs=[VMEM] * len(operands)...]
    all_to_all x0 -> x3, waiting for transfers between devices: none -> 24 us  [the longest x1 14.4 us: per_device(): sums = lax.all_to_all(sums, ('y', 'c'), 0, 0, tiled=True)]
    add x8 -> x0, other arithmetic: 22.6 us -> none  [advance(): return ((key_sum + key_term, value_sum + value_term), query_term)]
    all_to_all x0 -> x3, starting transfers between devices: none -> 21.1 us  [the longest x1 9.01 us: per_device(): q_own = lax.all_to_all(msg, ('zh', 'zl'), 0, 0, tiled=True)]
    ppermute x0 -> x11, waiting for transfers between devices: none -> 17.3 us  [shift(): lax.ppermute(value, axis, [(i, (i + amount) % size) for i in range(size)])]
  transfers between devices with their start and end apart: 5 -> 14, of which waited for: 3 -> 7; matrix products, arithmetic and copies ran while one was open for 1% -> 0% of each run, Pallas kernels for 0% -> 25%
where the time goes in v1:
time: 117 us
  waiting for transfers between devices  41.2 us (35%)
  starting transfers between devices  37.3 us (32%)
  Pallas kernels  31.5 us (27%)
  local copies, waits for them, and re-layouts  5.93 us (5%)
    pallas_call x10, Pallas kernels, call(): pl.pallas_call(body, out_shape=out_shape, in_specs=[VMEM] * len(operands)...  26.5 us
    ppermute x11, waiting for transfers between devices, shift(): lax.ppermute(value, axis, [(i, (i + amount) % size) for i in range(size)])  17.3 us
    ppermute x11, starting transfers between devices, shift(): lax.ppermute(value, axis, [(i, (i + amount) % size) for i in range(size)])  16.2 us
    all_to_all x1, waiting for transfers between devices, per_device(): sums = lax.all_to_all(sums, ('y', 'c'), 0, 0, tiled=True)  14.4 us
    all_to_all x1, starting transfers between devices, per_device(): q_own = lax.all_to_all(msg, ('zh', 'zl'), 0, 0, tiled=True)  9.01 us
    all_to_all x1, starting transfers between devices, per_device(): sums = lax.all_to_all(sums, ('y', 'c'), 0, 0, tiled=True)  7.46 us
    all_to_all x1, waiting for transfers between devices, per_device(): dq = lax.all_to_all(dq, ('zh', 'zl'), 0, 0, tiled=True)  6.51 us
    unnamed x28, local copies, waits for them, and re-layouts  5.88 us
  transfers between devices with their start and end apart: 14, of which 7 were waited for; matrix products, arithmetic and copies ran while one was open for 0% of the time, Pallas kernels for 25%

profile of v1, /device:TPU:1, one launch (start us, length us, event | category | flops | bytes accessed | tf_op | source)
XLA Modules:
  0.0 116.8 jit_solution(12326727338520160433)
XLA Ops:
  0.6 0.8 copy-done.5
  1.5 0.8 copy-done.6
  2.3 0.8 copy-done.7
  3.2 0.7 copy-done.10
  3.8 0.9 pack_queries.1
  4.8 9.0 %all-to-all-start = ((bf16[8,272,128]{2,1,0:T(8,128)(2,1)}), bf16[8,272,128]{2,1,0:T(8,128)(2,1)S(1)}, u32[]{:S(2)}, u32[]{:S(2)}) async-start(bf16[8,272,128]{2,1,0:T(8,128)(2,1)} %pack_queries.1), calls=%async_computation | async-start | bytes 1114112 | tf_op jit(solution)/shard_map/all_to_all | solution.py:222
  13.8 2.8 %collective-permute-start = (bf16[64,1024]{1,0:T(8,128)(2,1)S(1)}, bf16[64,1024]{1,0:T(8,128)(2,1)S(1)}, u32[]{:S(2)}, u32[]{:S(2)}) collective-permute-start(bf16[64,1024]{1,0:T(8,128)(2,1)S(1)} %pack_keys.1.own_ref), channel_id=1, source_target_pairs={{0,96},{32,0},{64,32},{96,64},{1,97},{33,1},{65,33},{97,65},{2,98}... | collective-permute-start | bytes 393224 | tf_op jit(solution)/shard_map/ppermute | solution.py:205
  16.6 1.6 %collective-permute-start.2 = (bf16[64,1024]{1,0:T(8,128)(2,1)S(1)}, bf16[64,1024]{1,0:T(8,128)(2,1)S(1)}, u32[]{:S(2)}, u32[]{:S(2)}) collective-permute-start(bf16[64,1024]{1,0:T(8,128)(2,1)S(1)} %pack_keys.1.own_ref), channel_id=1, source_target_pairs={{0,64},{32,96},{64,0},{96,32},{1,65},{33,97},{65,1},{97,33},{2,66}... | collective-permute-start | bytes 393224 | tf_op jit(solution)/shard_map/ppermute | solution.py:205
  18.6 6.7 %collective-permute-done.1.prev_ref = bf16[64,1024]{1,0:T(8,128)(2,1)S(1)} collective-permute-done((bf16[64,1024]{1,0:T(8,128)(2,1)S(1)}, bf16[64,1024]{1,0:T(8,128)(2,1)S(1)}, u32[]{:S(2)}, u32[]{:S(2)}) %collective-permute-start.1) | collective-permute-done | bytes 131104 | tf_op jit(solution)/shard_map/ppermute | solution.py:205
  25.9 2.2 %join_keys.1.refs_1_ = bf16[2,1024,128]{2,1,0:T(8,128)(2,1)} custom-call(s32[1]{0:T(128)} %bitcast.y_ref, bf16[64,1024]{1,0:T(8,128)(2,1)} %copy-done.4, bf16[64,1024]{1,0:T(8,128)(2,1)} %copy-done.11, bf16[64,1024]{1,0:T(8,128)(2,1)} %copy-done.12, bf16[64,1024]{1,0:T(8,128)(2,1)} %copy-done.13), custom_call_target="tpu_custom_call" | custom-call | tf_op jit(solution)/shard_map/join_keys/pallas_call | solution.py:230
  28.1 1.3 %collective-permute-start.3 = (bf16[2,1024,128]{2,1,0:T(8,128)(2,1)}, bf16[2,1024,128]{2,1,0:T(8,128)(2,1)S(1)}, u32[]{:S(2)}, u32[]{:S(2)}) collective-permute-start(bf16[2,1024,128]{2,1,0:T(8,128)(2,1)} %join_keys.1.refs_1_), channel_id=1, source_target_pairs={{0,1},{1,0},{2,3},{3,2},{4,5},{5,4},{6,7},{7,6},{8,9},{9,8},{10,11... | collective-permute-start | bytes 1572872 | tf_op jit(solution)/shard_map/ppermute | solution.py:205
  29.4 3.0 %all-to-all-done.refs_0_ = bf16[8,272,128]{2,1,0:T(8,128)(2,1)S(1)} async-done(((bf16[8,272,128]{2,1,0:T(8,128)(2,1)}), bf16[8,272,128]{2,1,0:T(8,128)(2,1)S(1)}, u32[]{:S(2)}, u32[]{:S(2)}) %all-to-all-start) | async-done | bytes 557088 | tf_op jit(solution)/shard_map/all_to_all | solution.py:222
  32.4 2.5 %collective-permute-start.6 = (bf16[8,272,128]{2,1,0:T(8,128)(2,1)S(1)}, bf16[8,272,128]{2,1,0:T(8,128)(2,1)S(1)}, u32[]{:S(2)}, u32[]{:S(2)}) collective-permute-start(bf16[8,272,128]{2,1,0:T(8,128)(2,1)S(1)} %all-to-all-done.refs_0_), channel_id=1, source_target_pairs={{0,6},{2,0},{4,2},{6,4},{1,7},{3,1},{5,3},{7,5},{8,14},{10,8},{12,... | collective-permute-start | bytes 1671176 | tf_op jit(solution)/shard_map/ppermute | solution.py:205
  34.9 1.0 copy-done.2
  36.0 3.0 %attend_own_a.1 = (f32[1024,128]{1,0:T(8,128)S(1)}, f32[2,1024,128]{2,1,0:T(8,128)S(1)}) custom-call(bf16[8,272,128]{2,1,0:T(8,128)(2,1)S(1)} %all-to-all-done.refs_0_, bf16[2,1024,128]{2,1,0:T(8,128)(2,1)S(1)} %copy-done.2), custom_call_target="tpu_custom_call" | custom-call | flops 1342177280 | bytes 8388608 | tf_op jit(solution)/shard_map/attend_own_a/pallas_call | solution.py:39
  39.0 3.0 %attend_own_b.1 = (bf16[8,128,128]{2,1,0:T(8,128)(2,1)S(1)}, f32[2,1024,128]{2,1,0:T(8,128)S(1)}) custom-call(bf16[8,272,128]{2,1,0:T(8,128)(2,1)S(1)} %all-to-all-done.refs_0_, bf16[2,1024,128]{2,1,0:T(8,128)(2,1)S(1)} %collective-permute-done.3.refs_1_.refs_2_, f32[1024,128]{1,0:T(8,128)S(1)} %get-tuple-element.18.refs_2_), custom_call_target="tpu_custom_call" | custom-call | flops 1342177280 | bytes 8388608 | tf_op jit(solution)/shard_map/attend_own_b/pallas_call | solution.py:39
  42.1 4.4 %collective-permute-done.6.refs_0_ = bf16[8,272,128]{2,1,0:T(8,128)(2,1)S(1)} collective-permute-done((bf16[8,272,128]{2,1,0:T(8,128)(2,1)S(1)}, bf16[8,272,128]{2,1,0:T(8,128)(2,1)S(1)}, u32[]{:S(2)}, u32[]{:S(2)}) %collective-permute-start.6) | collective-permute-done | bytes 557088 | tf_op jit(solution)/shard_map/ppermute | solution.py:205
  46.4 3.5 %collective-permute-start.9 = (bf16[8,136,128]{2,1,0:T(8,128)(2,1)S(1)}, bf16[8,136,128]{2,1,0:T(8,128)(2,1)S(1)}, u32[]{:S(2)}, u32[]{:S(2)}) collective-permute-start(bf16[8,136,128]{2,1,0:T(8,128)(2,1)S(1)} %slice.9), channel_id=1, source_target_pairs={{0,6},{2,0},{4,2},{6,4},{1,7},{3,1},{5,3},{7,5},{8,14},{10,8},{12,... | collective-permute-start | bytes 835592 | tf_op jit(solution)/shard_map/ppermute | solution.py:205
  50.2 5.7 %attend_prev.1 = (bf16[8,128,128]{2,1,0:T(8,128)(2,1)S(1)}, f32[2,1024,128]{2,1,0:T(8,128)S(1)}, f32[2,1024,128]{2,1,0:T(8,128)S(1)}) custom-call(bf16[8,272,128]{2,1,0:T(8,128)(2,1)S(1)} %collective-permute-done.4.refs_0_, bf16[2,1024,128]{2,1,0:T(8,128)(2,1)S(1)} %copy-done.3, ...), custom_call_target="tpu_custom_call", output_to_operand_aliasing={{1}: (3, {}), {2}: (4, {})} | custom-call | flops 2684354560 | bytes 16777216 | tf_op jit(solution)/shard_map/attend_prev/pallas_call | solution.py:39
  56.0 2.7 %collective-permute-start.5 = (bf16[8,128,128]{2,1,0:T(8,128)(2,1)S(1)}, bf16[8,128,128]{2,1,0:T(8,128)(2,1)S(1)}, u32[]{:S(2)}, u32[]{:S(2)}) collective-permute-start(bf16[8,128,128]{2,1,0:T(8,128)(2,1)S(1)} %get-tuple-element.22), channel_id=1, source_target_pairs={{0,6},{2,0},{4,2},{6,4},{1,7},{3,1},{5,3},{7,5},{8,14},{10,8},{12,... | collective-permute-start | bytes 786440 | tf_op jit(solution)/shard_map/ppermute | solution.py:205
  58.7 5.7 %attend_next.1 = (bf16[8,128,128]{2,1,0:T(8,128)(2,1)S(1)}, f32[2,1024,128]{2,1,0:T(8,128)S(1)}, f32[2,1024,128]{2,1,0:T(8,128)S(1)}) custom-call(bf16[8,272,128]{2,1,0:T(8,128)(2,1)S(1)} %collective-permute-done.6.refs_0_, bf16[2,1024,128]{2,1,0:T(8,128)(2,1)S(1)} %copy-done.3, ...), custom_call_target="tpu_custom_call", output_to_operand_aliasing={{1}: (3, {}), {2}: (4, {})} | custom-call | flops 2684354560 | bytes 16777216 | tf_op jit(solution)/shard_map/attend_next/pallas_call | solution.py:39
  64.8 5.7 %attend_far.1 = (bf16[8,128,128]{2,1,0:T(8,128)(2,1)S(1)}, f32[2,1024,128]{2,1,0:T(8,128)S(1)}, f32[2,1024,128]{2,1,0:T(8,128)S(1)}) custom-call(bf16[8,272,128]{2,1,0:T(8,128)(2,1)S(1)} %pad_maximum_fusion.refs_0_, bf16[2,1024,128]{2,1,0:T(8,128)(2,1)S(1)} %copy-done.3, ...), custom_call_target="tpu_custom_call", output_to_operand_aliasing={{1}: (3, {}), {2}: (4, {})} | custom-call | flops 2684354560 | bytes 16777216 | tf_op jit(solution)/shard_map/attend_far/pallas_call | solution.py:39
  70.6 0.9 copy-done.1
  71.5 1.2 %collective-permute-start.10 = (bf16[8,128,128]{2,1,0:T(8,128)(2,1)S(1)}, bf16[8,128,128]{2,1,0:T(8,128)(2,1)S(1)}, u32[]{:S(2)}, u32[]{:S(2)}) collective-permute-start(bf16[8,128,128]{2,1,0:T(8,128)(2,1)S(1)} %get-tuple-element.28), channel_id=1, source_target_pairs={{0,4},{2,6},{4,0},{6,2},{1,5},{3,7},{5,1},{7,3},{8,12},{10,14},{12... | collective-permute-start | bytes 786440 | tf_op jit(solution)/shard_map/ppermute | solution.py:205
  72.7 5.9 %collective-permute-done.10.c_ref = bf16[8,128,128]{2,1,0:T(8,128)(2,1)S(1)} collective-permute-done((bf16[8,128,128]{2,1,0:T(8,128)(2,1)S(1)}, bf16[8,128,128]{2,1,0:T(8,128)(2,1)S(1)}, u32[]{:S(2)}, u32[]{:S(2)}) %collective-permute-start.10) | collective-permute-done | bytes 262176 | tf_op jit(solution)/shard_map/ppermute | solution.py:205
  78.6 0.8 add_queries.1
  79.5 4.6 %all-to-all-start.1 = ((bf16[8,128,128]{2,1,0:T(8,128)(2,1)}), bf16[8,128,128]{2,1,0:T(8,128)(2,1)S(1)}, u32[]{:S(2)}, u32[]{:S(2)}) async-start(bf16[8,128,128]{2,1,0:T(8,128)(2,1)} %add_queries.1), calls=%async_computation.1 | async-start | bytes 524288 | tf_op jit(solution)/shard_map/all_to_all | solution.py:261
  84.1 2.9 %pack_sums.1 = bf16[8,64,1024]{2,1,0:T(8,128)(2,1)} custom-call(s32[1]{0:T(128)} %bitcast.3.core_ref, f32[2,1024,128]{2,1,0:T(8,128)} %copy-done, f32[2,1024,128]{2,1,0:T(8,128)} %copy-done.1), custom_call_target="tpu_custom_call" | custom-call | tf_op jit(solution)/shard_map/pack_sums/pallas_call | solution.py:250
  86.9 6.5 %all-to-all-done.1.in_ref = bf16[8,128,128]{2,1,0:T(8,128)(2,1)S(1)} async-done(((bf16[8,128,128]{2,1,0:T(8,128)(2,1)}), bf16[8,128,128]{2,1,0:T(8,128)(2,1)S(1)}, u32[]{:S(2)}, u32[]{:S(2)}) %all-to-all-start.1) | async-done | bytes 262176 | tf_op jit(solution)/shard_map/all_to_all | solution.py:261
  93.4 7.5 %all-to-all-start.2 = ((bf16[8,64,1024]{2,1,0:T(8,128)(2,1)}), bf16[8,64,1024]{2,1,0:T(8,128)(2,1)S(1)}, u32[]{:S(2)}, u32[]{:S(2)}) async-start(bf16[8,64,1024]{2,1,0:T(8,128)(2,1)} %pack_sums.1), calls=%async_computation.2 | async-start | bytes 2097152 | tf_op jit(solution)/shard_map/all_to_all | solution.py:257
  101.6 14.4 %all-to-all-done.2.in_ref = bf16[8,64,1024]{2,1,0:T(8,128)(2,1)S(1)} async-done(((bf16[8,64,1024]{2,1,0:T(8,128)(2,1)}), bf16[8,64,1024]{2,1,0:T(8,128)(2,1)S(1)}, u32[]{:S(2)}, u32[]{:S(2)}) %all-to-all-start.2) | async-done | bytes 1048608 | tf_op jit(solution)/shard_map/all_to_all | solution.py:257
  116.0 0.8 finish_keys.1
  (39 shorter events, 2.4 us)
Async XLA Ops:
  0.6 0.8 copy-start.5
  1.5 0.8 copy-start.6
  2.3 0.8 copy-start.7
  3.2 0.7 copy-start.10
  3.8 9.9 %copy-start.8 = (bf16[1024,32]{0,1:T(8,128)(2,1)S(1)}, bf16[1024,32]{0,1:T(8,128)(2,1)}, u32[]{:S(2)}) copy-start(bf16[1024,32]{0,1:T(8,128)(2,1)} %param.7) | copy-start | bytes 196612
  3.8 9.9 %copy-start.9 = (bf16[1024,32]{0,1:T(8,128)(2,1)S(1)}, bf16[1024,32]{0,1:T(8,128)(2,1)}, u32[]{:S(2)}) copy-start(bf16[1024,32]{0,1:T(8,128)(2,1)} %param.8) | copy-start | bytes 196612
  4.8 27.7 %all-to-all-start = ((bf16[8,272,128]{2,1,0:T(8,128)(2,1)}), bf16[8,272,128]{2,1,0:T(8,128)(2,1)S(1)}, u32[]{:S(2)}, u32[]{:S(2)}) async-start(bf16[8,272,128]{2,1,0:T(8,128)(2,1)} %pack_queries.1), calls=%async_computation | async-start | bytes 1114112 | tf_op jit(solution)/shard_map/all_to_all | solution.py:222
  13.8 11.4 %copy-start.4 = (bf16[64,1024]{1,0:T(8,128)(2,1)}, bf16[64,1024]{1,0:T(8,128)(2,1)S(1)}, u32[]{:S(2)}) copy-start(bf16[64,1024]{1,0:T(8,128)(2,1)S(1)} %pack_keys.1.own_ref) | copy-start | bytes 393220
  13.8 4.8 %collective-permute-start = (bf16[64,1024]{1,0:T(8,128)(2,1)S(1)}, bf16[64,1024]{1,0:T(8,128)(2,1)S(1)}, u32[]{:S(2)}, u32[]{:S(2)}) collective-permute-start(bf16[64,1024]{1,0:T(8,128)(2,1)S(1)} %pack_keys.1.own_ref), channel_id=1, source_target_pairs={{0,96},{32,0},{64,32},{96,64},{1,97},{33,1},{65,33},{97,65},{2,98}... | collective-permute-start | bytes 393224 | tf_op jit(solution)/shard_map/ppermute | solution.py:205
  16.6 8.6 %collective-permute-start.1 = (bf16[64,1024]{1,0:T(8,128)(2,1)S(1)}, bf16[64,1024]{1,0:T(8,128)(2,1)S(1)}, u32[]{:S(2)}, u32[]{:S(2)}) collective-permute-start(bf16[64,1024]{1,0:T(8,128)(2,1)S(1)} %pack_keys.1.own_ref), channel_id=1, source_target_pairs={{0,32},{32,64},{64,96},{96,0},{1,33},{33,65},{65,97},{97,1},{2,34}... | collective-permute-start | bytes 393224 | tf_op jit(solution)/shard_map/ppermute | solution.py:205
  16.6 8.6 %collective-permute-start.2 = (bf16[64,1024]{1,0:T(8,128)(2,1)S(1)}, bf16[64,1024]{1,0:T(8,128)(2,1)S(1)}, u32[]{:S(2)}, u32[]{:S(2)}) collective-permute-start(bf16[64,1024]{1,0:T(8,128)(2,1)S(1)} %pack_keys.1.own_ref), channel_id=1, source_target_pairs={{0,64},{32,96},{64,0},{96,32},{1,65},{33,97},{65,1},{97,33},{2,66}... | collective-permute-start | bytes 393224 | tf_op jit(solution)/shard_map/ppermute | solution.py:205
  18.6 6.7 %copy-start.11 = (bf16[64,1024]{1,0:T(8,128)(2,1)}, bf16[64,1024]{1,0:T(8,128)(2,1)S(1)}, u32[]{:S(2)}) copy-start(bf16[64,1024]{1,0:T(8,128)(2,1)S(1)} %collective-permute-done.next_ref) | copy-start | bytes 393220
  25.2 0.7 copy-start.12
  25.2 0.7 copy-start.13
  28.1 10.9 %collective-permute-start.3 = (bf16[2,1024,128]{2,1,0:T(8,128)(2,1)}, bf16[2,1024,128]{2,1,0:T(8,128)(2,1)S(1)}, u32[]{:S(2)}, u32[]{:S(2)}) collective-permute-start(bf16[2,1024,128]{2,1,0:T(8,128)(2,1)} %join_keys.1.refs_1_), channel_id=1, source_target_pairs={{0,1},{1,0},{2,3},{3,2},{4,5},{5,4},{6,7},{7,6},{8,9},{9,8},{10,11... | collective-permute-start | bytes 1572872 | tf_op jit(solution)/shard_map/ppermute | solution.py:205
  32.4 14.0 %collective-permute-start.6 = (bf16[8,272,128]{2,1,0:T(8,128)(2,1)S(1)}, bf16[8,272,128]{2,1,0:T(8,128)(2,1)S(1)}, u32[]{:S(2)}, u32[]{:S(2)}) collective-permute-start(bf16[8,272,128]{2,1,0:T(8,128)(2,1)S(1)} %all-to-all-done.refs_0_), channel_id=1, source_target_pairs={{0,6},{2,0},{4,2},{6,4},{1,7},{3,1},{5,3},{7,5},{8,14},{10,8},{12,... | collective-permute-start | bytes 1671176 | tf_op jit(solution)/shard_map/ppermute | solution.py:205
  34.9 15.0 %collective-permute-start.4 = (bf16[8,272,128]{2,1,0:T(8,128)(2,1)S(1)}, bf16[8,272,128]{2,1,0:T(8,128)(2,1)S(1)}, u32[]{:S(2)}, u32[]{:S(2)}) collective-permute-start(bf16[8,272,128]{2,1,0:T(8,128)(2,1)S(1)} %all-to-all-done.refs_0_), channel_id=1, source_target_pairs={{0,2},{2,4},{4,6},{6,0},{1,3},{3,5},{5,7},{7,1},{8,10},{10,12},{12... | collective-permute-start | bytes 1671176 | tf_op jit(solution)/shard_map/ppermute | solution.py:205
  34.9 1.0 copy-start.2
  42.1 8.2 %copy-start.3 = (bf16[2,1024,128]{2,1,0:T(8,128)(2,1)S(1)}, bf16[2,1024,128]{2,1,0:T(8,128)(2,1)}, u32[]{:S(2)}) copy-start(bf16[2,1024,128]{2,1,0:T(8,128)(2,1)} %join_keys.1.refs_1_) | copy-start | bytes 1572868
  46.4 18.3 %collective-permute-start.9 = (bf16[8,136,128]{2,1,0:T(8,128)(2,1)S(1)}, bf16[8,136,128]{2,1,0:T(8,128)(2,1)S(1)}, u32[]{:S(2)}, u32[]{:S(2)}) collective-permute-start(bf16[8,136,128]{2,1,0:T(8,128)(2,1)S(1)} %slice.9), channel_id=1, source_target_pairs={{0,6},{2,0},{4,2},{6,4},{1,7},{3,1},{5,3},{7,5},{8,14},{10,8},{12,... | collective-permute-start | bytes 835592 | tf_op jit(solution)/shard_map/ppermute | solution.py:205
  50.0 14.8 %collective-permute-start.8 = (bf16[8,136,128]{2,1,0:T(8,128)(2,1)S(1)}, bf16[8,136,128]{2,1,0:T(8,128)(2,1)S(1)}, u32[]{:S(2)}, u32[]{:S(2)}) collective-permute-start(bf16[8,136,128]{2,1,0:T(8,128)(2,1)S(1)} %slice.8), channel_id=1, source_target_pairs={{0,2},{2,4},{4,6},{6,0},{1,3},{3,5},{5,7},{7,1},{8,10},{10,12},{12... | collective-permute-start | bytes 835592 | tf_op jit(solution)/shard_map/ppermute | solution.py:205
  56.0 16.7 %collective-permute-start.5 = (bf16[8,128,128]{2,1,0:T(8,128)(2,1)S(1)}, bf16[8,128,128]{2,1,0:T(8,128)(2,1)S(1)}, u32[]{:S(2)}, u32[]{:S(2)}) collective-permute-start(bf16[8,128,128]{2,1,0:T(8,128)(2,1)S(1)} %get-tuple-element.22), channel_id=1, source_target_pairs={{0,6},{2,0},{4,2},{6,4},{1,7},{3,1},{5,3},{7,5},{8,14},{10,8},{12,... | collective-permute-start | bytes 786440 | tf_op jit(solution)/shard_map/ppermute | solution.py:205
  64.5 8.3 %collective-permute-start.7 = (bf16[8,128,128]{2,1,0:T(8,128)(2,1)S(1)}, bf16[8,128,128]{2,1,0:T(8,128)(2,1)S(1)}, u32[]{:S(2)}, u32[]{:S(2)}) collective-permute-start(bf16[8,128,128]{2,1,0:T(8,128)(2,1)S(1)} %get-tuple-element.25), channel_id=1, source_target_pairs={{0,2},{2,4},{4,6},{6,0},{1,3},{3,5},{5,7},{7,1},{8,10},{10,12},{12... | collective-permute-start | bytes 786440 | tf_op jit(solution)/shard_map/ppermute | solution.py:205
  70.6 1.0 copy-start.1
  71.5 12.5 %copy-start = (f32[2,1024,128]{2,1,0:T(8,128)}, f32[2,1024,128]{2,1,0:T(8,128)S(1)}, u32[]{:S(2)}) copy-start(f32[2,1024,128]{2,1,0:T(8,128)S(1)} %get-tuple-element.29.own_ref) | copy-start | bytes 3145732
  71.5 7.1 %collective-permute-start.10 = (bf16[8,128,128]{2,1,0:T(8,128)(2,1)S(1)}, bf16[8,128,128]{2,1,0:T(8,128)(2,1)S(1)}, u32[]{:S(2)}, u32[]{:S(2)}) collective-permute-start(bf16[8,128,128]{2,1,0:T(8,128)(2,1)S(1)} %get-tuple-element.28), channel_id=1, source_target_pairs={{0,4},{2,6},{4,0},{6,2},{1,5},{3,7},{5,1},{7,3},{8,12},{10,14},{12... | collective-permute-start | bytes 786440 | tf_op jit(solution)/shard_map/ppermute | solution.py:205
  79.5 14.0 %all-to-all-start.1 = ((bf16[8,128,128]{2,1,0:T(8,128)(2,1)}), bf16[8,128,128]{2,1,0:T(8,128)(2,1)S(1)}, u32[]{:S(2)}, u32[]{:S(2)}) async-start(bf16[8,128,128]{2,1,0:T(8,128)(2,1)} %add_queries.1), calls=%async_computation.1 | async-start | bytes 524288 | tf_op jit(solution)/shard_map/all_to_all | solution.py:261
  93.4 22.6 %all-to-all-start.2 = ((bf16[8,64,1024]{2,1,0:T(8,128)(2,1)}), bf16[8,64,1024]{2,1,0:T(8,128)(2,1)S(1)}, u32[]{:S(2)}, u32[]{:S(2)}) async-start(bf16[8,64,1024]{2,1,0:T(8,128)(2,1)} %pack_sums.1), calls=%async_computation.2 | async-start | bytes 2097152 | tf_op jit(solution)/shard_map/all_to_all | solution.py:257

commit v2 on v1

v2 whole, which is shorter than its diff:
```python
import functools
import math

import jax
import jax.numpy as jnp
from jax import lax
from jax.experimental import pallas as pl
from jax.experimental.pallas import tpu as pltpu
from jax.sharding import Mesh
from jax.sharding import PartitionSpec as P

F32 = jnp.float32
BF16 = jnp.bfloat16
HEAD_DIM = 128
ROWS = 128
KEYS = 1024
FEATS = 32
SIDE = 16
MSG = 2 * ROWS + SIDE
SCALING = HEAD_DIM ** (-0.5)
LOG2E = math.log2(math.e)
NT = (((1,), (1,)), ((), ()))
NN = (((1,), (0,)), ((), ()))
TN = (((0,), (0,)), ((), ()))
VMEM = pl.BlockSpec(memory_space=pltpu.VMEM)
SMEM = pl.BlockSpec(memory_space=pltpu.SMEM)


def dot(left, right, dims):
    return lax.dot_general(left, right, dims, preferred_element_type=F32)


def split3(value):
    high = value.astype(BF16).astype(F32)
    middle = (value - high).astype(BF16).astype(F32)
    return high, middle, value - high - middle


def call(body, out_shape, operands, name, flops=0, moved=1024, scratch=(), aliases=None, scalars=0, limit=8):
    return pl.pallas_call(
        body,
        out_shape=out_shape,
        in_specs=[SMEM] * scalars + [VMEM] * (len(operands) - scalars),
        out_specs=jax.tree.map(lambda _: VMEM, out_shape),
        scratch_shapes=list(scratch),
        input_output_aliases=aliases or {},
        compiler_params=pltpu.CompilerParams(vmem_limit_bytes=limit * 2**20),
        cost_estimate=pl.CostEstimate(flops=flops, bytes_accessed=moved, transcendentals=0),
        name=name,
    )(*operands)


def prepare(q_hbm, do_hbm, o_hbm, lse_hbm, k_hbm, v_hbm, msg_ref, kv_ref, q_s, do_s, o_s, lse_s, sems):
    copies = [
        pltpu.make_async_copy(do_hbm, do_s, sems.at[0]),
        pltpu.make_async_copy(o_hbm, o_s, sems.at[1]),
        pltpu.make_async_copy(lse_hbm, lse_s, sems.at[2]),
        pltpu.make_async_copy(q_hbm, q_s, sems.at[3]),
        pltpu.make_async_copy(k_hbm, kv_ref.at[pl.ds(0, FEATS)], sems.at[4]),
        pltpu.make_async_copy(v_hbm, kv_ref.at[pl.ds(FEATS, FEATS)], sems.at[5]),
    ]
    for copy in copies:
        copy.start()
    for copy in copies[:4]:
        copy.wait()
    product = do_s[...].astype(F32) * o_s[...].astype(F32)
    row = lax.broadcasted_iota(jnp.int32, (SIDE, ROWS), 0)
    for head in range(2):
        cols = pl.ds(head * HEAD_DIM, HEAD_DIM)
        part = product[:, head * HEAD_DIM : (head + 1) * HEAD_DIM]
        delta = jnp.sum(part.T, axis=0, keepdims=True)
        terms = split3(lse_s[head : head + 1, :] * LOG2E) + split3(delta)
        side = jnp.zeros((SIDE, ROWS), F32)
        for index, term in enumerate(terms):
            side = jnp.where(row == index, jnp.broadcast_to(term, (SIDE, ROWS)), side)
        side = side.astype(BF16)
        for place in range(4):
            target = head * 4 + place
            msg_ref[target, 0:ROWS, :] = q_s[:, cols]
            msg_ref[target, ROWS : 2 * ROWS, :] = do_s[:, cols]
            msg_ref[target, 2 * ROWS : MSG, :] = side
    for copy in copies[4:]:
        copy.wait()


def join_keys(y_ref, own_ref, next_ref, prev_ref, far_ref, k_ref, v_ref, kt, vt):
    y = y_ref[0]
    for shift, ref in ((0, own_ref), (3, prev_ref), (1, next_ref), (2, far_ref)):
        source = lax.rem(y + shift, 4)
        rows = pl.ds(pl.multiple_of(source * FEATS, FEATS), FEATS)
        kt[rows, :] = ref[0:FEATS, :]
        vt[rows, :] = ref[FEATS : 2 * FEATS, :]
    k_ref[...] = kt[...].T
    v_ref[...] = vt[...].T


def attend(first, last, blocks, *refs):
    refs = list(refs)
    core_ref = refs.pop(0) if last else None
    msg_refs = [refs.pop(0), refs.pop(0)]
    k_ref, v_ref = refs.pop(0), refs.pop(0)
    dq_in = None if first else refs.pop(0)
    dq_out = refs.pop(0)
    sums_ref, q_s, do_s, st_s, dk_s, dv_s = refs[:6]
    dq_s = refs[6] if last else dq_out
    for index in range(16):
        msg_ref, place = msg_refs[index // 8], index % 8
        span = pl.ds(index * ROWS, ROWS)
        q_s[span, :] = msg_ref[place, 0:ROWS, :]
        do_s[span, :] = msg_ref[place, ROWS : 2 * ROWS, :]
        side = msg_ref[place, 2 * ROWS : MSG, :].astype(F32)
        st_s[0:1, span] = side[0:1] + side[1:2] + side[2:3]
        st_s[1:2, span] = side[3:4] + side[4:5] + side[5:6]
    dk_s[...] = jnp.zeros_like(dk_s)
    dv_s[...] = jnp.zeros_like(dv_s)
    key, value = k_ref[...], v_ref[...]

    def step(index, _):
        for block in range(blocks):
            qs = pl.ds(pl.multiple_of(index * blocks * 256 + block * 256, 256), 256)
            query, grad = q_s[qs, :], do_s[qs, :]
            scores = dot(key, query, NT)
            probs = jnp.exp2(scores * (SCALING * LOG2E) - st_s[0:1, qs])
            grad_probs = dot(value, grad, NT)
            grad_scores = (probs * (grad_probs - st_s[1:2, qs])).astype(BF16)
            dv_s[...] += dot(probs.astype(BF16), grad, NN)
            dk_s[...] += dot(grad_scores, query, NN)
            dq = dot(grad_scores, key, TN)
            dq_s[qs, :] = dq if first else dq_in[qs, :] + dq
        return 0

    if blocks == 8:
        step(0, 0)
    else:
        lax.fori_loop(0, 8 // blocks, step, 0)
    if last:
        core = core_ref[0]
        for index in range(16):
            slot = 2 * (index % 8) + (core if index < 8 else 1 - core)
            dq_out[slot] = dq_s[pl.ds(index * ROWS, ROWS), :].astype(BF16)
    dk = (dk_s[...] * SCALING).astype(BF16).T
    dv = dv_s[...].astype(BF16).T
    for y in range(4):
        rows = slice(y * FEATS, (y + 1) * FEATS)
        sums_ref[2 * y * FEATS : (2 * y + 1) * FEATS, :] = dk[rows]
        sums_ref[(2 * y + 1) * FEATS : (2 * y + 2) * FEATS, :] = dv[rows]


def attend_call(msgs, chunk, dq_in, name, core=None, weight=0, blocks=4):
    sds = jax.ShapeDtypeStruct
    first = dq_in is None
    last = core is not None
    operands = ([core] if last else []) + list(msgs) + list(chunk) + ([] if first else [dq_in])
    if last:
        out = (sds((16, ROWS, HEAD_DIM), BF16),)
    else:
        out = (sds((16 * ROWS, HEAD_DIM), F32),)
    out += (sds((8 * FEATS, KEYS), BF16),)
    return call(
        functools.partial(attend, first, last, blocks),
        out,
        operands,
        name,
        flops=int(weight * 10 * 2**27),
        moved=int(weight * 2**23),
        scratch=[
            pltpu.VMEM((16 * ROWS, HEAD_DIM), BF16),
            pltpu.VMEM((16 * ROWS, HEAD_DIM), BF16),
            pltpu.VMEM((8, 16 * ROWS), F32),
            pltpu.VMEM((KEYS, HEAD_DIM), F32),
            pltpu.VMEM((KEYS, HEAD_DIM), F32),
        ]
        + [pltpu.VMEM((16 * ROWS, HEAD_DIM), F32)] * last,
        scalars=int(last),
        limit=30,
    )


def finish_queries(in_ref, out_ref):
    for head in range(2):
        total = in_ref[head * 8].astype(F32)
        for place in range(1, 8):
            total = total + in_ref[head * 8 + place].astype(F32)
        out_ref[:, head * HEAD_DIM : (head + 1) * HEAD_DIM] = (total * SCALING).astype(BF16)


def pack_sums(y_ref, own_ref, a_ref, b_ref, c_ref, mine_ref, next_ref, prev_ref, far_ref, total):
    y = y_ref[0]
    partial = own_ref[...].astype(F32) + a_ref[...].astype(F32)
    total[...] = partial + b_ref[...].astype(F32) + c_ref[...].astype(F32)
    for shift, ref in ((0, mine_ref), (1, next_ref), (3, prev_ref), (2, far_ref)):
        target = lax.rem(y + shift, 4)
        ref[...] = total[pl.ds(pl.multiple_of(target * 2 * FEATS, 2 * FEATS), 2 * FEATS), :].astype(BF16)


def finish_keys(a_ref, b_ref, c_ref, d_ref, dk_ref, dv_ref):
    total = a_ref[...].astype(F32) + b_ref[...].astype(F32)
    total = total + c_ref[...].astype(F32) + d_ref[...].astype(F32)
    dk_ref[...] = total[0:FEATS].astype(BF16)
    dv_ref[...] = total[FEATS : 2 * FEATS].astype(BF16)


def shift(value, axis, size, amount):
    return lax.ppermute(value, axis, [(i, (i + amount) % size) for i in range(size)])


X = ("xa", "xb")
Z = ("zh", "zl")


def per_device(queries, keys, values, outputs, d_out, lse):
    sds = jax.ShapeDtypeStruct
    y = lax.axis_index("y").astype(jnp.int32).reshape(1)
    core = lax.axis_index("c").astype(jnp.int32).reshape(1)

    msg, kvt = pl.pallas_call(
        prepare,
        out_shape=(sds((8, MSG, HEAD_DIM), BF16), sds((2 * FEATS, KEYS), BF16)),
        in_specs=[pl.BlockSpec(memory_space=pl.ANY)] * 6,
        out_specs=(VMEM, VMEM),
        scratch_shapes=[pltpu.VMEM((ROWS, 2 * HEAD_DIM), BF16)] * 3
        + [pltpu.VMEM((2, ROWS), F32), pltpu.SemaphoreType.DMA((6,))],
        cost_estimate=pl.CostEstimate(flops=0, bytes_accessed=2**20, transcendentals=0),
        name="prepare",
    )(queries, d_out, outputs, lse, keys.T, values.T)
    q_own = lax.all_to_all(msg, Z, 0, 0, tiled=True)
    kv_next = shift(kvt, "y", 4, 3)
    kv_prev = shift(kvt, "y", 4, 1)
    kv_far = shift(kvt, "y", 4, 2)
    k_own, v_own = call(
        join_keys,
        (sds((KEYS, HEAD_DIM), BF16),) * 2,
        [y, kvt, kv_next, kv_prev, kv_far],
        "join_keys",
        flops=20 * 2**30,
        scratch=[pltpu.VMEM((HEAD_DIM, KEYS), BF16)] * 2,
        scalars=1,
    )
    k_prev = shift(k_own, X, 4, 1)
    v_next = shift(v_own, X, 4, 3)
    v_prev = shift(v_own, X, 4, 1)
    k_next = shift(k_own, X, 4, 3)
    k_far = shift(k_prev, X, 4, 1)
    v_far = shift(v_next, X, 4, 3)
    q_own, k_prev, v_next, v_prev, k_next = lax.optimization_barrier(
        (q_own, k_prev, v_next, v_prev, k_next)
    )
    q_other = shift(q_own, "c", 2, 1)

    msgs = [q_own, q_other]
    dq, sums_prev = attend_call(msgs, [k_prev, v_prev], None, "attend_prev")
    back_prev = shift(sums_prev, X, 4, 3)
    dq, sums_far = attend_call(msgs, [k_far, v_far], dq, "attend_far")
    back_far = shift(sums_far, X, 4, 2)
    dq, sums_next = attend_call(msgs, [k_next, v_next], dq, "attend_next")
    back_next = shift(sums_next, X, 4, 1)
    dq, sums_own = attend_call(msgs, [k_own, v_own], dq, "attend_own", core=core, blocks=8)
    dq, back_far = lax.optimization_barrier((dq, back_far))
    dq = lax.all_to_all(dq, Z + ("c",), 0, 0, tiled=True)

    mine, to_next, to_prev, to_far = call(
        pack_sums,
        (sds((2 * FEATS, KEYS), BF16),) * 4,
        [y, sums_own, back_prev, back_far, back_next],
        "pack_sums",
        flops=100 * 2**30,
        scratch=[pltpu.VMEM((8 * FEATS, KEYS), F32)],
        scalars=1,
    )
    sums = [mine, shift(to_next, "y", 4, 1), shift(to_prev, "y", 4, 3), shift(to_far, "y", 4, 2)]
    d_queries = call(finish_queries, sds((ROWS, 2 * HEAD_DIM), BF16), [dq], "finish_queries")
    d_keys, d_values = call(
        finish_keys, (sds((FEATS, KEYS), BF16),) * 2, sums, "finish_keys"
    )
    return d_queries, d_keys.T, d_values.T


def solution(mesh):
    every = ("zh", "y", "zl", "xa", "xb", "c")
    fine = Mesh(mesh.devices.reshape(2, 4, 4, 2, 2, 2), every)
    blocks = P(("zl", "xa", "xb", "c"), ("zh", "y"))
    rows = P(every, None)
    return jax.shard_map(
        per_device,
        mesh=fine,
        in_specs=(rows, blocks, blocks, rows, rows, P(None, every)),
        out_specs=(rows, blocks, blocks),
        check_vma=False,
    )
```

time: 117 us -> 97.3 us (0.83)
  waiting for transfers between devices: 41.2 us -> 23.2 us
  local copies, waits for them, and re-layouts: 5.93 us -> 0.82 us
  starting transfers between devices: 37.3 us -> 39.3 us
  Pallas kernels: 31.5 us -> 32.9 us
    all_to_all x3 -> x2, waiting for transfers between devices: 24 us -> 6.48 us  [the longest x1 5.28 us: per_device(): dq = lax.all_to_all(dq, Z + ('c',), 0, 0, tiled=True)]
    ppermute x11 -> x16, starting transfers between devices: 16.2 us -> 24.1 us  [shift(): lax.ppermute(value, axis, [(i, (i + amount) % size) for i in range(size)])]
    all_to_all x3 -> x2, starting transfers between devices: 21.1 us -> 15.2 us  [the longest x1 8.32 us: per_device(): q_own = lax.all_to_all(msg, Z, 0, 0, tiled=True)]
    unnamed x28 -> x6, local copies, waits for them, and re-layouts: 5.88 us -> 0.82 us
    pallas_call x12 -> x9, Pallas kernels: 31.5 us -> 32.9 us  [the longest x8 30.9 us: call(): pl.pallas_call(body, out_shape=out_shape, in_specs=[SMEM] * scalars + [VM...]
    ppermute x11 -> x16, waiting for transfers between devices: 17.3 us -> 16.7 us  [shift(): lax.ppermute(value, axis, [(i, (i + amount) % size) for i in range(size)])]
  transfers between devices with their start and end apart: 14 -> 18, of which waited for: 7 -> 9; matrix products, arithmetic and copies ran while one was open for 0% -> 0% of each run, Pallas kernels for 25% -> 24%
where the time goes in v2:
time: 97.3 us; the launch traced here: 96.9 us
  starting transfers between devices  39.3 us (40%)
  Pallas kernels  32.9 us (34%)
  waiting for transfers between devices  23.2 us (24%)
    pallas_call x8, Pallas kernels, call(): pl.pallas_call(body, out_shape=out_shape, in_specs=[SMEM] * scalars + [VM...  30.9 us
    ppermute x16, starting transfers between devices, shift(): lax.ppermute(value, axis, [(i, (i + amount) % size) for i in range(size)])  24.1 us
    ppermute x16, waiting for transfers between devices, shift(): lax.ppermute(value, axis, [(i, (i + amount) % size) for i in range(size)])  16.7 us
    all_to_all x1, starting transfers between devices, per_device(): q_own = lax.all_to_all(msg, Z, 0, 0, tiled=True)  8.32 us
    all_to_all x1, starting transfers between devices, per_device(): dq = lax.all_to_all(dq, Z + ('c',), 0, 0, tiled=True)  6.9 us
    all_to_all x1, waiting for transfers between devices, per_device(): dq = lax.all_to_all(dq, Z + ('c',), 0, 0, tiled=True)  5.28 us
    pallas_call x1, Pallas kernels, per_device(): pl.pallas_call(prepare, out_shape=(sds((8, MSG, HEAD_DIM), BF16), sds((2...  1.99 us
  transfers between devices with their start and end apart: 18, of which 9 were waited for; matrix products, arithmetic and copies ran while one was open for 0% of the time, Pallas kernels for 24%

profile of v2, /device:TPU:1, one launch (start us, length us, event | category | flops | bytes accessed | tf_op | source)
XLA Modules:
  0.0 96.9 jit_solution(5974768319210574552)
XLA Ops:
  0.6 2.0 %prepare.1 = (bf16[8,272,128]{2,1,0:T(8,128)(2,1)}, bf16[64,1024]{1,0:T(8,128)(2,1)}) custom-call(bf16[128,256]{1,0:T(8,128)(2,1)} %q_hbm.1, bf16[128,256]{1,0:T(8,128)(2,1)} %do_hbm.1, bf16[128,256]{1,0:T(8,128)(2,1)} %o_hbm.1, f32[2,128]{1,0:T(2,128)} %lse_hbm.1, bf16[32,1024]{1,0:T(8,128)(2,1)} %bitcast.6, bf16[32,1024]{1,0:T(8,128)(2,1)} %bitcast.7), custom_call_target="tpu_custom_call" | custom-call | bytes 1048576 | tf_op jit(solution)/shard_map/prepare/pallas_call | solution.py:216
  2.6 3.8 %collective-permute-start.2 = (bf16[64,1024]{1,0:T(8,128)(2,1)}, bf16[64,1024]{1,0:T(8,128)(2,1)S(1)}, u32[]{:S(2)}, u32[]{:S(2)}) collective-permute-start(bf16[64,1024]{1,0:T(8,128)(2,1)} %get-tuple-element.29.own_ref), channel_id=1, source_target_pairs={{0,64},{32,96},{64,0},{96,32},{1,65},{33,97},{65,1},{97,33},{2,66}... | collective-permute-start | bytes 393224 | tf_op jit(solution)/shard_map/ppermute | solution.py:204
  6.5 0.4 collective-permute-start.1
  6.9 2.3 %collective-permute-start = (bf16[64,1024]{1,0:T(8,128)(2,1)}, bf16[64,1024]{1,0:T(8,128)(2,1)S(1)}, u32[]{:S(2)}, u32[]{:S(2)}) collective-permute-start(bf16[64,1024]{1,0:T(8,128)(2,1)} %get-tuple-element.29.own_ref), channel_id=1, source_target_pairs={{0,96},{32,0},{64,32},{96,64},{1,97},{33,1},{65,33},{97,65},{2,98}... | collective-permute-start | bytes 393224 | tf_op jit(solution)/shard_map/ppermute | solution.py:204
  9.1 8.3 %all-to-all-start = ((bf16[8,272,128]{2,1,0:T(8,128)(2,1)}), bf16[8,272,128]{2,1,0:T(8,128)(2,1)S(1)}, u32[]{:S(2)}, u32[]{:S(2)}) async-start(bf16[8,272,128]{2,1,0:T(8,128)(2,1)} %get-tuple-element.28), calls=%async_computation | async-start | bytes 1114112 | tf_op jit(solution)/shard_map/all_to_all | solution.py:226
  17.7 2.6 %collective-permute-start.6 = (bf16[1024,128]{1,0:T(8,128)(2,1)S(1)}, bf16[1024,128]{1,0:T(8,128)(2,1)S(1)}, u32[]{:S(2)}, u32[]{:S(2)}) collective-permute-start(bf16[1024,128]{1,0:T(8,128)(2,1)S(1)} %get-tuple-element.30.refs_3_), channel_id=1, source_target_pairs={{0,6},{2,0},{4,2},{6,4},{1,7},{3,1},{5,3},{7,5},{8,14},{10,8},{12,... | collective-permute-start | bytes 786440 | tf_op jit(solution)/shard_map/ppermute | solution.py:204
  20.5 2.5 %collective-permute-start.4 = (bf16[1024,128]{1,0:T(8,128)(2,1)S(1)}, bf16[1024,128]{1,0:T(8,128)(2,1)S(1)}, u32[]{:S(2)}, u32[]{:S(2)}) collective-permute-start(bf16[1024,128]{1,0:T(8,128)(2,1)S(1)} %get-tuple-element.31.refs_4_), channel_id=1, source_target_pairs={{0,6},{2,0},{4,2},{6,4},{1,7},{3,1},{5,3},{7,5},{8,14},{10,8},{12,... | collective-permute-start | bytes 786440 | tf_op jit(solution)/shard_map/ppermute | solution.py:204
  23.0 1.1 %collective-permute-done.6.refs_2_ = bf16[1024,128]{1,0:T(8,128)(2,1)S(1)} collective-permute-done((bf16[1024,128]{1,0:T(8,128)(2,1)S(1)}, bf16[1024,128]{1,0:T(8,128)(2,1)S(1)}, u32[]{:S(2)}, u32[]{:S(2)}) %collective-permute-start.6) | collective-permute-done | bytes 262176 | tf_op jit(solution)/shard_map/ppermute | solution.py:204
  24.1 3.1 %collective-permute-done.3.refs_2_ = bf16[1024,128]{1,0:T(8,128)(2,1)S(1)} collective-permute-done((bf16[1024,128]{1,0:T(8,128)(2,1)S(1)}, bf16[1024,128]{1,0:T(8,128)(2,1)S(1)}, u32[]{:S(2)}, u32[]{:S(2)}) %collective-permute-start.3) | collective-permute-done | bytes 262176 | tf_op jit(solution)/shard_map/ppermute | solution.py:204
  27.2 5.6 %collective-permute-done.5.refs_3_ = bf16[1024,128]{1,0:T(8,128)(2,1)S(1)} collective-permute-done((bf16[1024,128]{1,0:T(8,128)(2,1)S(1)}, bf16[1024,128]{1,0:T(8,128)(2,1)S(1)}, u32[]{:S(2)}, u32[]{:S(2)}) %collective-permute-start.5) | collective-permute-done | bytes 262176 | tf_op jit(solution)/shard_map/ppermute | solution.py:204
  32.8 1.2 %all-to-all-done.refs_0_.refs_1_ = bf16[8,272,128]{2,1,0:T(8,128)(2,1)S(1)} async-done(((bf16[8,272,128]{2,1,0:T(8,128)(2,1)}), bf16[8,272,128]{2,1,0:T(8,128)(2,1)S(1)}, u32[]{:S(2)}, u32[]{:S(2)}) %all-to-all-start) | async-done | bytes 557088 | tf_op jit(solution)/shard_map/all_to_all | solution.py:226
  34.0 2.6 %collective-permute-start.7 = (bf16[8,272,128]{2,1,0:T(8,128)(2,1)S(1)}, bf16[8,272,128]{2,1,0:T(8,128)(2,1)S(1)}, u32[]{:S(2)}, u32[]{:S(2)}) collective-permute-start(bf16[8,272,128]{2,1,0:T(8,128)(2,1)S(1)} %all-to-all-done.refs_0_.refs_1_), channel_id=1, source_target_pairs={{0,1},{1,0},{2,3},{3,2},{4,5},{5,4},{6,7},{7,6},{8,9},{9,8},{10,11... | collective-permute-start | bytes 1671176 | tf_op jit(solution)/shard_map/ppermute | solution.py:204
  36.6 1.2 %collective-permute-start.8 = (bf16[1024,128]{1,0:T(8,128)(2,1)S(1)}, bf16[1024,128]{1,0:T(8,128)(2,1)S(1)}, u32[]{:S(2)}, u32[]{:S(2)}) collective-permute-start(bf16[1024,128]{1,0:T(8,128)(2,1)S(1)} %collective-permute-done.3.refs_2_), channel_id=1, source_target_pairs={{0,2},{2,4},{4,6},{6,0},{1,3},{3,5},{5,7},{7,1},{8,10},{10,12},{12... | collective-permute-start | bytes 786440 | tf_op jit(solution)/shard_map/ppermute | solution.py:204
  37.8 1.5 %collective-permute-start.9 = (bf16[1024,128]{1,0:T(8,128)(2,1)S(1)}, bf16[1024,128]{1,0:T(8,128)(2,1)S(1)}, u32[]{:S(2)}, u32[]{:S(2)}) collective-permute-start(bf16[1024,128]{1,0:T(8,128)(2,1)S(1)} %collective-permute-done.4.refs_3_), channel_id=1, source_target_pairs={{0,6},{2,0},{4,2},{6,4},{1,7},{3,1},{5,3},{7,5},{8,14},{10,8},{12,... | collective-permute-start | bytes 786440 | tf_op jit(solution)/shard_map/ppermute | solution.py:204
  39.3 7.0 %attend_prev.1 = (f32[2048,128]{1,0:T(8,128)S(1)}, bf16[256,1024]{1,0:T(8,128)(2,1)}) custom-call(bf16[8,272,128]{2,1,0:T(8,128)(2,1)S(1)} %all-to-all-done.refs_0_.refs_1_, bf16[8,272,128]{2,1,0:T(8,128)(2,1)S(1)} %collective-permute-done.7.refs_1_.refs_2_, bf16[1024,128]{1,0:T(8,128)(2,1)S(1)} %collective-permute-done.3.refs_2_, ...), custom_call_target="tpu_custom_call" | custom-call | tf_op jit(solution)/shard_map/attend_prev/pallas_call | solution.py:40
  46.3 7.0 %attend_far.1 = (f32[2048,128]{1,0:T(8,128)S(1)}, bf16[256,1024]{1,0:T(8,128)(2,1)}) custom-call(bf16[8,272,128]{2,1,0:T(8,128)(2,1)S(1)} %all-to-all-done.refs_0_.refs_1_, bf16[8,272,128]{2,1,0:T(8,128)(2,1)S(1)} %collective-permute-done.7.refs_1_.refs_2_, bf16[1024,128]{1,0:T(8,128)(2,1)S(1)} %collective-permute-done.8.refs_2_, ...), custom_call_target="tpu_custom_call" | custom-call | tf_op jit(solution)/shard_map/attend_far/pallas_call | solution.py:40
  53.4 1.6 %collective-permute-start.10 = (bf16[256,1024]{1,0:T(8,128)(2,1)}, bf16[256,1024]{1,0:T(8,128)(2,1)}, u32[]{:S(2)}, u32[]{:S(2)}) collective-permute-start(bf16[256,1024]{1,0:T(8,128)(2,1)} %get-tuple-element.41), channel_id=1, source_target_pairs={{0,4},{2,6},{4,0},{6,2},{1,5},{3,7},{5,1},{7,3},{8,12},{10,14},{12... | collective-permute-start | bytes 1572872 | tf_op jit(solution)/shard_map/ppermute | solution.py:204
  55.0 7.0 %attend_next.1 = (f32[2048,128]{1,0:T(8,128)S(1)}, bf16[256,1024]{1,0:T(8,128)(2,1)}) custom-call(bf16[8,272,128]{2,1,0:T(8,128)(2,1)S(1)} %all-to-all-done.refs_0_.refs_1_, bf16[8,272,128]{2,1,0:T(8,128)(2,1)S(1)} %collective-permute-done.7.refs_1_.refs_2_, bf16[1024,128]{1,0:T(8,128)(2,1)S(1)} %collective-permute-done.6.refs_2_, ...), custom_call_target="tpu_custom_call" | custom-call | tf_op jit(solution)/shard_map/attend_next/pallas_call | solution.py:40
  62.0 0.7 collective-permute-start.12
  62.7 2.0 %collective-permute-start.11 = (bf16[256,1024]{1,0:T(8,128)(2,1)}, bf16[256,1024]{1,0:T(8,128)(2,1)}, u32[]{:S(2)}, u32[]{:S(2)}) collective-permute-start(bf16[256,1024]{1,0:T(8,128)(2,1)} %get-tuple-element.44), channel_id=1, source_target_pairs={{0,6},{2,0},{4,2},{6,4},{1,7},{3,1},{5,3},{7,5},{8,14},{10,8},{12,... | collective-permute-start | bytes 1572872 | tf_op jit(solution)/shard_map/ppermute | solution.py:204
  64.7 6.5 %attend_own.1 = (bf16[16,128,128]{2,1,0:T(8,128)(2,1)}, bf16[256,1024]{1,0:T(8,128)(2,1)S(1)}) custom-call(s32[1]{0:T(128)} %bitcast.refs_0_, bf16[8,272,128]{2,1,0:T(8,128)(2,1)S(1)} %all-to-all-done.refs_0_.refs_1_, bf16[8,272,128]{2,1,0:T(8,128)(2,1)S(1)} %collective-permute-done.7.refs_1_.refs_2_, bf16[1024,128]{1,0:T(8,128)(2,1)S(1)} %get-tuple-element.30.refs_3_, ...), custom_call_target="tpu_custom_call" | custom-call | tf_op jit(solution)/shard_map/attend_own/pallas_call | solution.py:40
  71.2 0.8 copy-done
  72.0 6.9 %all-to-all-start.1 = ((bf16[16,128,128]{2,1,0:T(8,128)(2,1)}), bf16[16,128,128]{2,1,0:T(8,128)(2,1)S(1)}, u32[]{:S(2)}, u32[]{:S(2)}) async-start(bf16[16,128,128]{2,1,0:T(8,128)(2,1)} %get-tuple-element.42), calls=%async_computation.1 | async-start | bytes 1048576 | tf_op jit(solution)/shard_map/all_to_all | solution.py:259
  78.9 1.3 %collective-permute-done.12.c_ref = bf16[256,1024]{1,0:T(8,128)(2,1)S(1)} collective-permute-done((bf16[256,1024]{1,0:T(8,128)(2,1)}, bf16[256,1024]{1,0:T(8,128)(2,1)S(1)}, u32[]{:S(2)}, u32[]{:S(2)}) %collective-permute-start.12) | collective-permute-done | bytes 524320 | tf_op jit(solution)/shard_map/ppermute | solution.py:204
  80.2 1.7 %pack_sums.1 = (bf16[64,1024]{1,0:T(8,128)(2,1)S(1)}, bf16[64,1024]{1,0:T(8,128)(2,1)S(1)}, bf16[64,1024]{1,0:T(8,128)(2,1)S(1)}, bf16[64,1024]{1,0:T(8,128)(2,1)S(1)}) custom-call(s32[1]{0:T(128)} %bitcast.3.y_ref, bf16[256,1024]{1,0:T(8,128)(2,1)S(1)} %copy-done.1, bf16[256,1024]{1,0:T(8,128)(2,1)} %collective-permute-done.11.a_ref, ...), custom_call_target="tpu_custom_call" | custom-call | flops 107374182400 | bytes 1024 | tf_op jit(solution)/shard_map/pack_sums/pallas_call | solution.py:40
  82.0 2.7 %collective-permute-start.14 = (bf16[64,1024]{1,0:T(8,128)(2,1)S(1)}, bf16[64,1024]{1,0:T(8,128)(2,1)S(1)}, u32[]{:S(2)}, u32[]{:S(2)}) collective-permute-start(bf16[64,1024]{1,0:T(8,128)(2,1)S(1)} %get-tuple-element.49), channel_id=1, source_target_pairs={{0,96},{32,0},{64,32},{96,64},{1,97},{33,1},{65,33},{97,65},{2,98}... | collective-permute-start | bytes 393224 | tf_op jit(solution)/shard_map/ppermute | solution.py:204
  84.6 3.1 %collective-permute-done.13.b_ref = bf16[64,1024]{1,0:T(8,128)(2,1)S(1)} collective-permute-done((bf16[64,1024]{1,0:T(8,128)(2,1)S(1)}, bf16[64,1024]{1,0:T(8,128)(2,1)S(1)}, u32[]{:S(2)}, u32[]{:S(2)}) %collective-permute-start.13) | collective-permute-done | bytes 131104 | tf_op jit(solution)/shard_map/ppermute | solution.py:204
  87.7 2.0 %collective-permute-done.14.c_ref = bf16[64,1024]{1,0:T(8,128)(2,1)S(1)} collective-permute-done((bf16[64,1024]{1,0:T(8,128)(2,1)S(1)}, bf16[64,1024]{1,0:T(8,128)(2,1)S(1)}, u32[]{:S(2)}, u32[]{:S(2)}) %collective-permute-start.14) | collective-permute-done | bytes 131104 | tf_op jit(solution)/shard_map/ppermute | solution.py:204
  89.7 0.5 collective-permute-done.15.d_ref
  90.2 0.7 finish_keys.1
  90.9 5.3 %all-to-all-done.1.in_ref = bf16[16,128,128]{2,1,0:T(8,128)(2,1)S(1)} async-done(((bf16[16,128,128]{2,1,0:T(8,128)(2,1)}), bf16[16,128,128]{2,1,0:T(8,128)(2,1)S(1)}, u32[]{:S(2)}, u32[]{:S(2)}) %all-to-all-start.1) | async-done | bytes 524320 | tf_op jit(solution)/shard_map/all_to_all | solution.py:259
  96.2 0.7 finish_queries.1
  (19 shorter events, 0.5 us)
Async XLA Ops:
  2.6 14.8 %collective-permute-start.2 = (bf16[64,1024]{1,0:T(8,128)(2,1)}, bf16[64,1024]{1,0:T(8,128)(2,1)S(1)}, u32[]{:S(2)}, u32[]{:S(2)}) collective-permute-start(bf16[64,1024]{1,0:T(8,128)(2,1)} %get-tuple-element.29.own_ref), channel_id=1, source_target_pairs={{0,64},{32,96},{64,0},{96,32},{1,65},{33,97},{65,1},{97,33},{2,66}... | collective-permute-start | bytes 393224 | tf_op jit(solution)/shard_map/ppermute | solution.py:204
  6.5 11.0 %collective-permute-start.1 = (bf16[64,1024]{1,0:T(8,128)(2,1)}, bf16[64,1024]{1,0:T(8,128)(2,1)S(1)}, u32[]{:S(2)}, u32[]{:S(2)}) collective-permute-start(bf16[64,1024]{1,0:T(8,128)(2,1)} %get-tuple-element.29.own_ref), channel_id=1, source_target_pairs={{0,32},{32,64},{64,96},{96,0},{1,33},{33,65},{65,97},{97,1},{2,34}... | collective-permute-start | bytes 393224 | tf_op jit(solution)/shard_map/ppermute | solution.py:204
  6.9 10.6 %collective-permute-start = (bf16[64,1024]{1,0:T(8,128)(2,1)}, bf16[64,1024]{1,0:T(8,128)(2,1)S(1)}, u32[]{:S(2)}, u32[]{:S(2)}) collective-permute-start(bf16[64,1024]{1,0:T(8,128)(2,1)} %get-tuple-element.29.own_ref), channel_id=1, source_target_pairs={{0,96},{32,0},{64,32},{96,64},{1,97},{33,1},{65,33},{97,65},{2,98}... | collective-permute-start | bytes 393224 | tf_op jit(solution)/shard_map/ppermute | solution.py:204
  9.1 8.3 %copy-start.2 = (bf16[64,1024]{1,0:T(8,128)(2,1)S(1)}, bf16[64,1024]{1,0:T(8,128)(2,1)}, u32[]{:S(2)}) copy-start(bf16[64,1024]{1,0:T(8,128)(2,1)} %get-tuple-element.29.own_ref) | copy-start | bytes 393220
  9.1 24.9 %all-to-all-start = ((bf16[8,272,128]{2,1,0:T(8,128)(2,1)}), bf16[8,272,128]{2,1,0:T(8,128)(2,1)S(1)}, u32[]{:S(2)}, u32[]{:S(2)}) async-start(bf16[8,272,128]{2,1,0:T(8,128)(2,1)} %get-tuple-element.28), calls=%async_computation | async-start | bytes 1114112 | tf_op jit(solution)/shard_map/all_to_all | solution.py:226
  17.7 6.4 %collective-permute-start.6 = (bf16[1024,128]{1,0:T(8,128)(2,1)S(1)}, bf16[1024,128]{1,0:T(8,128)(2,1)S(1)}, u32[]{:S(2)}, u32[]{:S(2)}) collective-permute-start(bf16[1024,128]{1,0:T(8,128)(2,1)S(1)} %get-tuple-element.30.refs_3_), channel_id=1, source_target_pairs={{0,6},{2,0},{4,2},{6,4},{1,7},{3,1},{5,3},{7,5},{8,14},{10,8},{12,... | collective-permute-start | bytes 786440 | tf_op jit(solution)/shard_map/ppermute | solution.py:204
  20.3 6.9 %collective-permute-start.3 = (bf16[1024,128]{1,0:T(8,128)(2,1)S(1)}, bf16[1024,128]{1,0:T(8,128)(2,1)S(1)}, u32[]{:S(2)}, u32[]{:S(2)}) collective-permute-start(bf16[1024,128]{1,0:T(8,128)(2,1)S(1)} %get-tuple-element.30.refs_3_), channel_id=1, source_target_pairs={{0,2},{2,4},{4,6},{6,0},{1,3},{3,5},{5,7},{7,1},{8,10},{10,12},{12... | collective-permute-start | bytes 786440 | tf_op jit(solution)/shard_map/ppermute | solution.py:204
  20.3 12.5 %collective-permute-start.5 = (bf16[1024,128]{1,0:T(8,128)(2,1)S(1)}, bf16[1024,128]{1,0:T(8,128)(2,1)S(1)}, u32[]{:S(2)}, u32[]{:S(2)}) collective-permute-start(bf16[1024,128]{1,0:T(8,128)(2,1)S(1)} %get-tuple-element.31.refs_4_), channel_id=1, source_target_pairs={{0,2},{2,4},{4,6},{6,0},{1,3},{3,5},{5,7},{7,1},{8,10},{10,12},{12... | collective-permute-start | bytes 786440 | tf_op jit(solution)/shard_map/ppermute | solution.py:204
  20.5 12.4 %collective-permute-start.4 = (bf16[1024,128]{1,0:T(8,128)(2,1)S(1)}, bf16[1024,128]{1,0:T(8,128)(2,1)S(1)}, u32[]{:S(2)}, u32[]{:S(2)}) collective-permute-start(bf16[1024,128]{1,0:T(8,128)(2,1)S(1)} %get-tuple-element.31.refs_4_), channel_id=1, source_target_pairs={{0,6},{2,0},{4,2},{6,4},{1,7},{3,1},{5,3},{7,5},{8,14},{10,8},{12,... | collective-permute-start | bytes 786440 | tf_op jit(solution)/shard_map/ppermute | solution.py:204
  34.0 5.3 %collective-permute-start.7 = (bf16[8,272,128]{2,1,0:T(8,128)(2,1)S(1)}, bf16[8,272,128]{2,1,0:T(8,128)(2,1)S(1)}, u32[]{:S(2)}, u32[]{:S(2)}) collective-permute-start(bf16[8,272,128]{2,1,0:T(8,128)(2,1)S(1)} %all-to-all-done.refs_0_.refs_1_), channel_id=1, source_target_pairs={{0,1},{1,0},{2,3},{3,2},{4,5},{5,4},{6,7},{7,6},{8,9},{9,8},{10,11... | collective-permute-start | bytes 1671176 | tf_op jit(solution)/shard_map/ppermute | solution.py:204
  36.6 9.7 %collective-permute-start.8 = (bf16[1024,128]{1,0:T(8,128)(2,1)S(1)}, bf16[1024,128]{1,0:T(8,128)(2,1)S(1)}, u32[]{:S(2)}, u32[]{:S(2)}) collective-permute-start(bf16[1024,128]{1,0:T(8,128)(2,1)S(1)} %collective-permute-done.3.refs_2_), channel_id=1, source_target_pairs={{0,2},{2,4},{4,6},{6,0},{1,3},{3,5},{5,7},{7,1},{8,10},{10,12},{12... | collective-permute-start | bytes 786440 | tf_op jit(solution)/shard_map/ppermute | solution.py:204
  37.8 8.5 %collective-permute-start.9 = (bf16[1024,128]{1,0:T(8,128)(2,1)S(1)}, bf16[1024,128]{1,0:T(8,128)(2,1)S(1)}, u32[]{:S(2)}, u32[]{:S(2)}) collective-permute-start(bf16[1024,128]{1,0:T(8,128)(2,1)S(1)} %collective-permute-done.4.refs_3_), channel_id=1, source_target_pairs={{0,6},{2,0},{4,2},{6,4},{1,7},{3,1},{5,3},{7,5},{8,14},{10,8},{12,... | collective-permute-start | bytes 786440 | tf_op jit(solution)/shard_map/ppermute | solution.py:204
  53.4 18.6 %collective-permute-start.10 = (bf16[256,1024]{1,0:T(8,128)(2,1)}, bf16[256,1024]{1,0:T(8,128)(2,1)}, u32[]{:S(2)}, u32[]{:S(2)}) collective-permute-start(bf16[256,1024]{1,0:T(8,128)(2,1)} %get-tuple-element.41), channel_id=1, source_target_pairs={{0,4},{2,6},{4,0},{6,2},{1,5},{3,7},{5,1},{7,3},{8,12},{10,14},{12... | collective-permute-start | bytes 1572872 | tf_op jit(solution)/shard_map/ppermute | solution.py:204
  62.0 18.1 %collective-permute-start.12 = (bf16[256,1024]{1,0:T(8,128)(2,1)}, bf16[256,1024]{1,0:T(8,128)(2,1)S(1)}, u32[]{:S(2)}, u32[]{:S(2)}) collective-permute-start(bf16[256,1024]{1,0:T(8,128)(2,1)} %get-tuple-element.46), channel_id=1, source_target_pairs={{0,2},{2,4},{4,6},{6,0},{1,3},{3,5},{5,7},{7,1},{8,10},{10,12},{12... | collective-permute-start | bytes 1572872 | tf_op jit(solution)/shard_map/ppermute | solution.py:204
  62.7 17.4 %collective-permute-start.11 = (bf16[256,1024]{1,0:T(8,128)(2,1)}, bf16[256,1024]{1,0:T(8,128)(2,1)}, u32[]{:S(2)}, u32[]{:S(2)}) collective-permute-start(bf16[256,1024]{1,0:T(8,128)(2,1)} %get-tuple-element.44), channel_id=1, source_target_pairs={{0,6},{2,0},{4,2},{6,4},{1,7},{3,1},{5,3},{7,5},{8,14},{10,8},{12,... | collective-permute-start | bytes 1572872 | tf_op jit(solution)/shard_map/ppermute | solution.py:204
  71.2 0.8 copy-start
  72.0 8.2 %copy-start.1 = (bf16[256,1024]{1,0:T(8,128)(2,1)S(1)}, bf16[256,1024]{1,0:T(8,128)(2,1)}, u32[]{:S(2)}) copy-start(bf16[256,1024]{1,0:T(8,128)(2,1)} %copy-done) | copy-start | bytes 1572868
  72.0 24.2 %all-to-all-start.1 = ((bf16[16,128,128]{2,1,0:T(8,128)(2,1)}), bf16[16,128,128]{2,1,0:T(8,128)(2,1)S(1)}, u32[]{:S(2)}, u32[]{:S(2)}) async-start(bf16[16,128,128]{2,1,0:T(8,128)(2,1)} %get-tuple-element.42), calls=%async_computation.1 | async-start | bytes 1048576 | tf_op jit(solution)/shard_map/all_to_all | solution.py:259
  81.9 5.9 %collective-permute-start.13 = (bf16[64,1024]{1,0:T(8,128)(2,1)S(1)}, bf16[64,1024]{1,0:T(8,128)(2,1)S(1)}, u32[]{:S(2)}, u32[]{:S(2)}) collective-permute-start(bf16[64,1024]{1,0:T(8,128)(2,1)S(1)} %get-tuple-element.48), channel_id=1, source_target_pairs={{0,32},{32,64},{64,96},{96,0},{1,33},{33,65},{65,97},{97,1},{2,34}... | collective-permute-start | bytes 393224 | tf_op jit(solution)/shard_map/ppermute | solution.py:204
  82.0 7.8 %collective-permute-start.14 = (bf16[64,1024]{1,0:T(8,128)(2,1)S(1)}, bf16[64,1024]{1,0:T(8,128)(2,1)S(1)}, u32[]{:S(2)}, u32[]{:S(2)}) collective-permute-start(bf16[64,1024]{1,0:T(8,128)(2,1)S(1)} %get-tuple-element.49), channel_id=1, source_target_pairs={{0,96},{32,0},{64,32},{96,64},{1,97},{33,1},{65,33},{97,65},{2,98}... | collective-permute-start | bytes 393224 | tf_op jit(solution)/shard_map/ppermute | solution.py:204
  84.6 5.6 %collective-permute-start.15 = (bf16[64,1024]{1,0:T(8,128)(2,1)S(1)}, bf16[64,1024]{1,0:T(8,128)(2,1)S(1)}, u32[]{:S(2)}, u32[]{:S(2)}) collective-permute-start(bf16[64,1024]{1,0:T(8,128)(2,1)S(1)} %get-tuple-element.50), channel_id=1, source_target_pairs={{0,64},{32,96},{64,0},{96,32},{1,65},{33,97},{65,1},{97,33},{2,66}... | collective-permute-start | bytes 393224 | tf_op jit(solution)/shard_map/ppermute | solution.py:204

commit v3 on v2

--- a/solution.py
+++ b/solution.py
@@ -15,7 +15,7 @@
 ROWS = 128
 KEYS = 1024
 FEATS = 32
-SIDE = 16
+SIDE = 8
 MSG = 2 * ROWS + SIDE
 SCALING = HEAD_DIM ** (-0.5)
 LOG2E = math.log2(math.e)
@@ -83,50 +83,54 @@
         copy.wait()
 
 
-def join_keys(y_ref, own_ref, next_ref, prev_ref, far_ref, k_ref, v_ref, kt, vt):
+def join_keys(y_ref, own_ref, next_ref, prev_ref, far_ref, kv_ref, kt, vt):
     y = y_ref[0]
     for shift, ref in ((0, own_ref), (3, prev_ref), (1, next_ref), (2, far_ref)):
         source = lax.rem(y + shift, 4)
         rows = pl.ds(pl.multiple_of(source * FEATS, FEATS), FEATS)
         kt[rows, :] = ref[0:FEATS, :]
         vt[rows, :] = ref[FEATS : 2 * FEATS, :]
-    k_ref[...] = kt[...].T
-    v_ref[...] = vt[...].T
+    kv_ref[0] = kt[...].T
+    kv_ref[1] = vt[...].T
 
 
 def attend(first, last, blocks, *refs):
     refs = list(refs)
     core_ref = refs.pop(0) if last else None
     msg_refs = [refs.pop(0), refs.pop(0)]
-    k_ref, v_ref = refs.pop(0), refs.pop(0)
+    kv_ref = refs.pop(0)
     dq_in = None if first else refs.pop(0)
     dq_out = refs.pop(0)
-    sums_ref, q_s, do_s, st_s, dk_s, dv_s = refs[:6]
-    dq_s = refs[6] if last else dq_out
-    for index in range(16):
-        msg_ref, place = msg_refs[index // 8], index % 8
-        span = pl.ds(index * ROWS, ROWS)
-        q_s[span, :] = msg_ref[place, 0:ROWS, :]
-        do_s[span, :] = msg_ref[place, ROWS : 2 * ROWS, :]
-        side = msg_ref[place, 2 * ROWS : MSG, :].astype(F32)
-        st_s[0:1, span] = side[0:1] + side[1:2] + side[2:3]
-        st_s[1:2, span] = side[3:4] + side[4:5] + side[5:6]
+    sums_ref, dk_s, dv_s = refs[:3]
+    dq_s = refs[3] if last else dq_out
     dk_s[...] = jnp.zeros_like(dk_s)
     dv_s[...] = jnp.zeros_like(dv_s)
-    key, value = k_ref[...], v_ref[...]
+    key, value = kv_ref[0], kv_ref[1]
+
+    def pair(msg_ref, place, start, size):
+        return jnp.concatenate(
+            [msg_ref[place, start : start + size, :], msg_ref[place + 1, start : start + size, :]],
+            axis=0 if size == ROWS else 1,
+        )
 
     def step(index, _):
         for block in range(blocks):
-            qs = pl.ds(pl.multiple_of(index * blocks * 256 + block * 256, 256), 256)
-            query, grad = q_s[qs, :], do_s[qs, :]
+            which = block % 2
+            place = index * blocks + block - which
+            msg_ref = msg_refs[which]
+            query, grad = pair(msg_ref, place, 0, ROWS), pair(msg_ref, place, ROWS, ROWS)
+            side = pair(msg_ref, place, 2 * ROWS, SIDE).astype(F32)
+            lse = side[0:1] + side[1:2] + side[2:3]
+            delta = side[3:4] + side[4:5] + side[5:6]
             scores = dot(key, query, NT)
-            probs = jnp.exp2(scores * (SCALING * LOG2E) - st_s[0:1, qs])
+            probs = jnp.exp2(scores * (SCALING * LOG2E) - lse)
             grad_probs = dot(value, grad, NT)
-            grad_scores = (probs * (grad_probs - st_s[1:2, qs])).astype(BF16)
+            grad_scores = (probs * (grad_probs - delta)).astype(BF16)
             dv_s[...] += dot(probs.astype(BF16), grad, NN)
             dk_s[...] += dot(grad_scores, query, NN)
             dq = dot(grad_scores, key, TN)
-            dq_s[qs, :] = dq if first else dq_in[qs, :] + dq
+            rows = pl.ds(pl.multiple_of(which * 8 * ROWS + place * ROWS, 256), 256)
+            dq_s[rows, :] = dq if first else dq_in[rows, :] + dq
         return 0
 
     if blocks == 8:
@@ -146,11 +150,11 @@
         sums_ref[(2 * y + 1) * FEATS : (2 * y + 2) * FEATS, :] = dv[rows]
 
 
-def attend_call(msgs, chunk, dq_in, name, core=None, weight=0, blocks=4):
+def attend_call(msgs, chunk, dq_in, name, core=None, weight=0, blocks=8):
     sds = jax.ShapeDtypeStruct
     first = dq_in is None
     last = core is not None
-    operands = ([core] if last else []) + list(msgs) + list(chunk) + ([] if first else [dq_in])
+    operands = ([core] if last else []) + list(msgs) + [chunk] + ([] if first else [dq_in])
     if last:
         out = (sds((16, ROWS, HEAD_DIM), BF16),)
     else:
@@ -164,9 +168,6 @@
         flops=int(weight * 10 * 2**27),
         moved=int(weight * 2**23),
         scratch=[
-            pltpu.VMEM((16 * ROWS, HEAD_DIM), BF16),
-            pltpu.VMEM((16 * ROWS, HEAD_DIM), BF16),
-            pltpu.VMEM((8, 16 * ROWS), F32),
             pltpu.VMEM((KEYS, HEAD_DIM), F32),
             pltpu.VMEM((KEYS, HEAD_DIM), F32),
         ]
@@ -184,10 +185,13 @@
         out_ref[:, head * HEAD_DIM : (head + 1) * HEAD_DIM] = (total * SCALING).astype(BF16)
 
 
-def pack_sums(y_ref, own_ref, a_ref, b_ref, c_ref, mine_ref, next_ref, prev_ref, far_ref, total):
+def add_sums(a_ref, b_ref, out_ref):
+    out_ref[...] = a_ref[...].astype(F32) + b_ref[...].astype(F32)
+
+
+def pack_sums(y_ref, near_ref, own_ref, back_ref, mine_ref, next_ref, prev_ref, far_ref, total):
     y = y_ref[0]
-    partial = own_ref[...].astype(F32) + a_ref[...].astype(F32)
-    total[...] = partial + b_ref[...].astype(F32) + c_ref[...].astype(F32)
+    total[...] = near_ref[...] + own_ref[...].astype(F32) + back_ref[...].astype(F32)
     for shift, ref in ((0, mine_ref), (1, next_ref), (3, prev_ref), (2, far_ref)):
         target = lax.rem(y + shift, 4)
         ref[...] = total[pl.ds(pl.multiple_of(target * 2 * FEATS, 2 * FEATS), 2 * FEATS), :].astype(BF16)
@@ -227,43 +231,44 @@
     kv_next = shift(kvt, "y", 4, 3)
     kv_prev = shift(kvt, "y", 4, 1)
     kv_far = shift(kvt, "y", 4, 2)
-    k_own, v_own = call(
+    kv_own = call(
         join_keys,
-        (sds((KEYS, HEAD_DIM), BF16),) * 2,
+        sds((2, KEYS, HEAD_DIM), BF16),
         [y, kvt, kv_next, kv_prev, kv_far],
         "join_keys",
         flops=20 * 2**30,
         scratch=[pltpu.VMEM((HEAD_DIM, KEYS), BF16)] * 2,
         scalars=1,
     )
-    k_prev = shift(k_own, X, 4, 1)
-    v_next = shift(v_own, X, 4, 3)
-    v_prev = shift(v_own, X, 4, 1)
-    k_next = shift(k_own, X, 4, 3)
-    k_far = shift(k_prev, X, 4, 1)
-    v_far = shift(v_next, X, 4, 3)
-    q_own, k_prev, v_next, v_prev, k_next = lax.optimization_barrier(
-        (q_own, k_prev, v_next, v_prev, k_next)
-    )
+    kv_x_prev = shift(kv_own, X, 4, 1)
+    kv_x_next = shift(kv_own, X, 4, 3)
+    kv_x_far = shift(kv_own, X, 4, 2)
+    q_own, kv_x_prev, kv_x_next = lax.optimization_barrier((q_own, kv_x_prev, kv_x_next))
     q_other = shift(q_own, "c", 2, 1)
 
     msgs = [q_own, q_other]
-    dq, sums_prev = attend_call(msgs, [k_prev, v_prev], None, "attend_prev")
+    dq, sums_prev = attend_call(msgs, kv_x_prev, None, "attend_prev")
     back_prev = shift(sums_prev, X, 4, 3)
-    dq, sums_far = attend_call(msgs, [k_far, v_far], dq, "attend_far")
+    dq, sums_next = attend_call(msgs, kv_x_next, dq, "attend_next")
+    back_next = shift(sums_next, X, 4, 1)
+    dq, sums_far = attend_call(msgs, kv_x_far, dq, "attend_far")
     back_far = shift(sums_far, X, 4, 2)
-    dq, sums_next = attend_call(msgs, [k_next, v_next], dq, "attend_next")
-    back_next = shift(sums_next, X, 4, 1)
-    dq, sums_own = attend_call(msgs, [k_own, v_own], dq, "attend_own", core=core, blocks=8)
-    dq, back_far = lax.optimization_barrier((dq, back_far))
+    dq, sums_own = attend_call(msgs, kv_own, dq, "attend_own", core=core)
+    dq, back_prev = lax.optimization_barrier((dq, back_prev))
     dq = lax.all_to_all(dq, Z + ("c",), 0, 0, tiled=True)
 
+    near = call(
+        add_sums,
+        sds((8 * FEATS, KEYS), F32),
+        [back_prev, back_next],
+        "add_sums",
+        flops=2**37,
+    )
     mine, to_next, to_prev, to_far = call(
         pack_sums,
         (sds((2 * FEATS, KEYS), BF16),) * 4,
-        [y, sums_own, back_prev, back_far, back_next],
+        [y, near, sums_own, back_far],
         "pack_sums",
-        flops=100 * 2**30,
         scratch=[pltpu.VMEM((8 * FEATS, KEYS), F32)],
         scalars=1,
     )

time: 97.3 us -> 93.5 us (0.961)
  starting transfers between devices: 39.3 us -> 34.7 us
  waiting for transfers between devices: 23.2 us -> 25.9 us
  Pallas kernels: 32.9 us -> 31.8 us
    ppermute x16 -> x13, starting transfers between devices: 24.1 us -> 20.1 us  [shift(): lax.ppermute(value, axis, [(i, (i + amount) % size) for i in range(size)])]
    ppermute x16 -> x13, waiting for transfers between devices: 16.7 us -> 20.6 us  [shift(): lax.ppermute(value, axis, [(i, (i + amount) % size) for i in range(size)])]
    pallas_call x8 -> x9, Pallas kernels: 30.9 us -> 29.8 us  [call(): pl.pallas_call(body, out_shape=out_shape, in_specs=[SMEM] * scalars + [VM...]
  transfers between devices with their start and end apart: 18 -> 15, of which waited for: 9 -> 8; matrix products, arithmetic and copies ran while one was open for 0% -> 0% of each run, Pallas kernels for 24% -> 31%
where the time goes in v3:
time: 93.5 us; the launch traced here: 93.1 us
  starting transfers between devices  34.7 us (37%)
  Pallas kernels  31.8 us (34%)
  waiting for transfers between devices  25.9 us (28%)
    pallas_call x9, Pallas kernels, call(): pl.pallas_call(body, out_shape=out_shape, in_specs=[SMEM] * scalars + [VM...  29.8 us
    ppermute x13, waiting for transfers between devices, shift(): lax.ppermute(value, axis, [(i, (i + amount) % size) for i in range(size)])  20.6 us
    ppermute x13, starting transfers between devices, shift(): lax.ppermute(value, axis, [(i, (i + amount) % size) for i in range(size)])  20.1 us
    all_to_all x1, starting transfers between devices, per_device(): q_own = lax.all_to_all(msg, Z, 0, 0, tiled=True)  8.32 us
    all_to_all x1, starting transfers between devices, per_device(): dq = lax.all_to_all(dq, Z + ('c',), 0, 0, tiled=True)  6.3 us
    all_to_all x1, waiting for transfers between devices, per_device(): dq = lax.all_to_all(dq, Z + ('c',), 0, 0, tiled=True)  4.33 us
    pallas_call x1, Pallas kernels, per_device(): pl.pallas_call(prepare, out_shape=(sds((8, MSG, HEAD_DIM), BF16), sds((2...  2.01 us
  transfers between devices with their start and end apart: 15, of which 8 were waited for; matrix products, arithmetic and copies ran while one was open for 0% of the time, Pallas kernels for 31%

profile of v3, /device:TPU:1, one launch (start us, length us, event | category | flops | bytes accessed | tf_op | source)
XLA Modules:
  0.0 93.1 jit_solution(16012706796820058996)
XLA Ops:
  0.6 2.0 %prepare.1 = (bf16[8,264,128]{2,1,0:T(8,128)(2,1)}, bf16[64,1024]{1,0:T(8,128)(2,1)}) custom-call(bf16[128,256]{1,0:T(8,128)(2,1)} %q_hbm.1, bf16[128,256]{1,0:T(8,128)(2,1)} %do_hbm.1, bf16[128,256]{1,0:T(8,128)(2,1)} %o_hbm.1, f32[2,128]{1,0:T(2,128)} %lse_hbm.1, bf16[32,1024]{1,0:T(8,128)(2,1)} %bitcast.6, bf16[32,1024]{1,0:T(8,128)(2,1)} %bitcast.7), custom_call_target="tpu_custom_call" | custom-call | bytes 1048576 | tf_op jit(solution)/shard_map/prepare/pallas_call | solution.py:220
  2.6 3.8 %collective-permute-start.2 = (bf16[64,1024]{1,0:T(8,128)(2,1)}, bf16[64,1024]{1,0:T(8,128)(2,1)S(1)}, u32[]{:S(2)}, u32[]{:S(2)}) collective-permute-start(bf16[64,1024]{1,0:T(8,128)(2,1)} %get-tuple-element.25.own_ref), channel_id=1, source_target_pairs={{0,64},{32,96},{64,0},{96,32},{1,65},{33,97},{65,1},{97,33},{2,66}... | collective-permute-start | bytes 393224 | tf_op jit(solution)/shard_map/ppermute | solution.py:208
  6.5 0.4 collective-permute-start.1
  6.9 2.3 %collective-permute-start = (bf16[64,1024]{1,0:T(8,128)(2,1)}, bf16[64,1024]{1,0:T(8,128)(2,1)S(1)}, u32[]{:S(2)}, u32[]{:S(2)}) collective-permute-start(bf16[64,1024]{1,0:T(8,128)(2,1)} %get-tuple-element.25.own_ref), channel_id=1, source_target_pairs={{0,96},{32,0},{64,32},{96,64},{1,97},{33,1},{65,33},{97,65},{2,98}... | collective-permute-start | bytes 393224 | tf_op jit(solution)/shard_map/ppermute | solution.py:208
  9.2 8.3 %all-to-all-start = ((bf16[8,264,128]{2,1,0:T(8,128)(2,1)}), bf16[8,264,128]{2,1,0:T(8,128)(2,1)S(1)}, u32[]{:S(2)}, u32[]{:S(2)}) async-start(bf16[8,264,128]{2,1,0:T(8,128)(2,1)} %get-tuple-element.24), calls=%async_computation | async-start | bytes 1081344 | tf_op jit(solution)/shard_map/all_to_all | solution.py:230
  17.5 0.0 collective-permute-done.1.prev_ref
  17.5 0.2 join_keys.1.refs_3_
  17.7 2.6 %collective-permute-start.4 = (bf16[2,1024,128]{2,1,0:T(8,128)(2,1)S(1)}, bf16[2,1024,128]{2,1,0:T(8,128)(2,1)S(1)}, u32[]{:S(2)}, u32[]{:S(2)}) collective-permute-start(bf16[2,1024,128]{2,1,0:T(8,128)(2,1)S(1)} %join_keys.1.refs_3_), channel_id=1, source_target_pairs={{0,6},{2,0},{4,2},{6,4},{1,7},{3,1},{5,3},{7,5},{8,14},{10,8},{12,... | collective-permute-start | bytes 1572872 | tf_op jit(solution)/shard_map/ppermute | solution.py:208
  20.3 9.4 %collective-permute-done.4.refs_2_ = bf16[2,1024,128]{2,1,0:T(8,128)(2,1)S(1)} collective-permute-done((bf16[2,1024,128]{2,1,0:T(8,128)(2,1)S(1)}, bf16[2,1024,128]{2,1,0:T(8,128)(2,1)S(1)}, u32[]{:S(2)}, u32[]{:S(2)}) %collective-permute-start.4) | collective-permute-done | bytes 524320 | tf_op jit(solution)/shard_map/ppermute | solution.py:208
  29.7 3.1 %collective-permute-done.3.refs_2_ = bf16[2,1024,128]{2,1,0:T(8,128)(2,1)S(1)} collective-permute-done((bf16[2,1024,128]{2,1,0:T(8,128)(2,1)S(1)}, bf16[2,1024,128]{2,1,0:T(8,128)(2,1)S(1)}, u32[]{:S(2)}, u32[]{:S(2)}) %collective-permute-start.3) | collective-permute-done | bytes 524320 | tf_op jit(solution)/shard_map/ppermute | solution.py:208
  32.8 0.9 all-to-all-done.refs_0_.refs_1_
  33.7 2.5 %collective-permute-start.5 = (bf16[8,264,128]{2,1,0:T(8,128)(2,1)S(1)}, bf16[8,264,128]{2,1,0:T(8,128)(2,1)S(1)}, u32[]{:S(2)}, u32[]{:S(2)}) collective-permute-start(bf16[8,264,128]{2,1,0:T(8,128)(2,1)S(1)} %all-to-all-done.refs_0_.refs_1_), channel_id=1, source_target_pairs={{0,1},{1,0},{2,3},{3,2},{4,5},{5,4},{6,7},{7,6},{8,9},{9,8},{10,11... | collective-permute-start | bytes 1622024 | tf_op jit(solution)/shard_map/ppermute | solution.py:208
  36.3 2.7 %collective-permute-start.6 = (bf16[2,1024,128]{2,1,0:T(8,128)(2,1)S(1)}, bf16[2,1024,128]{2,1,0:T(8,128)(2,1)}, u32[]{:S(2)}, u32[]{:S(2)}) collective-permute-start(bf16[2,1024,128]{2,1,0:T(8,128)(2,1)S(1)} %join_keys.1.refs_3_), channel_id=1, source_target_pairs={{0,4},{2,6},{4,0},{6,2},{1,5},{3,7},{5,1},{7,3},{8,12},{10,14},{12... | collective-permute-start | bytes 1572872 | tf_op jit(solution)/shard_map/ppermute | solution.py:208
  39.0 6.4 %attend_prev.1 = (f32[2048,128]{1,0:T(8,128)S(1)}, bf16[256,1024]{1,0:T(8,128)(2,1)}) custom-call(bf16[8,264,128]{2,1,0:T(8,128)(2,1)S(1)} %all-to-all-done.refs_0_.refs_1_, bf16[8,264,128]{2,1,0:T(8,128)(2,1)S(1)} %collective-permute-done.5.refs_1_.refs_2_, bf16[2,1024,128]{2,1,0:T(8,128)(2,1)S(1)} %collective-permute-done.3.refs_2_), custom_call_target="tpu_custom_call" | custom-call | tf_op jit(solution)/shard_map/attend_prev/pallas_call | solution.py:40
  45.4 1.3 %collective-permute-start.7 = (bf16[256,1024]{1,0:T(8,128)(2,1)}, bf16[256,1024]{1,0:T(8,128)(2,1)}, u32[]{:S(2)}, u32[]{:S(2)}) collective-permute-start(bf16[256,1024]{1,0:T(8,128)(2,1)} %get-tuple-element.33), channel_id=1, source_target_pairs={{0,6},{2,0},{4,2},{6,4},{1,7},{3,1},{5,3},{7,5},{8,14},{10,8},{12,... | collective-permute-start | bytes 1572872 | tf_op jit(solution)/shard_map/ppermute | solution.py:208
  46.7 6.4 %attend_next.1 = (f32[2048,128]{1,0:T(8,128)S(1)}, bf16[256,1024]{1,0:T(8,128)(2,1)}) custom-call(bf16[8,264,128]{2,1,0:T(8,128)(2,1)S(1)} %all-to-all-done.refs_0_.refs_1_, bf16[8,264,128]{2,1,0:T(8,128)(2,1)S(1)} %collective-permute-done.5.refs_1_.refs_2_, bf16[2,1024,128]{2,1,0:T(8,128)(2,1)S(1)} %collective-permute-done.4.refs_2_, ...), custom_call_target="tpu_custom_call" | custom-call | tf_op jit(solution)/shard_map/attend_next/pallas_call | solution.py:40
  53.1 0.2 collective-permute-start.8
  53.3 7.4 %attend_far.1 = (f32[2048,128]{1,0:T(8,128)S(1)}, bf16[256,1024]{1,0:T(8,128)(2,1)}) custom-call(bf16[8,264,128]{2,1,0:T(8,128)(2,1)S(1)} %all-to-all-done.refs_0_.refs_1_, bf16[8,264,128]{2,1,0:T(8,128)(2,1)S(1)} %collective-permute-done.5.refs_1_.refs_2_, bf16[2,1024,128]{2,1,0:T(8,128)(2,1)} %collective-permute-done.6.refs_2_, ...), custom_call_target="tpu_custom_call" | custom-call | tf_op jit(solution)/shard_map/attend_far/pallas_call | solution.py:40
  60.8 1.6 %collective-permute-start.9 = (bf16[256,1024]{1,0:T(8,128)(2,1)}, bf16[256,1024]{1,0:T(8,128)(2,1)S(1)}, u32[]{:S(2)}, u32[]{:S(2)}) collective-permute-start(bf16[256,1024]{1,0:T(8,128)(2,1)} %get-tuple-element.38), channel_id=1, source_target_pairs={{0,4},{2,6},{4,0},{6,2},{1,5},{3,7},{5,1},{7,3},{8,12},{10,14},{12... | collective-permute-start | bytes 1572872 | tf_op jit(solution)/shard_map/ppermute | solution.py:208
  62.3 6.5 %attend_own.1 = (bf16[16,128,128]{2,1,0:T(8,128)(2,1)}, bf16[256,1024]{1,0:T(8,128)(2,1)S(1)}) custom-call(s32[1]{0:T(128)} %bitcast.refs_0_, bf16[8,264,128]{2,1,0:T(8,128)(2,1)S(1)} %all-to-all-done.refs_0_.refs_1_, bf16[8,264,128]{2,1,0:T(8,128)(2,1)S(1)} %collective-permute-done.5.refs_1_.refs_2_, bf16[2,1024,128]{2,1,0:T(8,128)(2,1)S(1)} %join_keys.1.refs_3_, ...), custom_call_target="tpu_custom_call" | custom-call | tf_op jit(solution)/shard_map/attend_own/pallas_call | solution.py:40
  68.8 6.3 %all-to-all-start.1 = ((bf16[16,128,128]{2,1,0:T(8,128)(2,1)}), bf16[16,128,128]{2,1,0:T(8,128)(2,1)S(1)}, u32[]{:S(2)}, u32[]{:S(2)}) async-start(bf16[16,128,128]{2,1,0:T(8,128)(2,1)} %get-tuple-element.34), calls=%async_computation.1 | async-start | bytes 1048576 | tf_op jit(solution)/shard_map/all_to_all | solution.py:258
  75.1 1.1 %add_sums.1.near_ref = f32[256,1024]{1,0:T(8,128)S(1)} custom-call(bf16[256,1024]{1,0:T(8,128)(2,1)} %collective-permute-done.7.a_ref, bf16[256,1024]{1,0:T(8,128)(2,1)S(1)} %collective-permute-done.8.b_ref), custom_call_target="tpu_custom_call" | custom-call | flops 137438953472 | bytes 1024 | tf_op jit(solution)/shard_map/add_sums/pallas_call | solution.py:40
  76.2 1.5 %collective-permute-done.9.back_ref = bf16[256,1024]{1,0:T(8,128)(2,1)S(1)} collective-permute-done((bf16[256,1024]{1,0:T(8,128)(2,1)}, bf16[256,1024]{1,0:T(8,128)(2,1)S(1)}, u32[]{:S(2)}, u32[]{:S(2)}) %collective-permute-start.9) | collective-permute-done | bytes 524320 | tf_op jit(solution)/shard_map/ppermute | solution.py:208
  77.7 0.3 pack_sums.1
  78.0 0.1 collective-permute-start.10
  78.1 2.7 %collective-permute-start.11 = (bf16[64,1024]{1,0:T(8,128)(2,1)S(1)}, bf16[64,1024]{1,0:T(8,128)(2,1)S(1)}, u32[]{:S(2)}, u32[]{:S(2)}) collective-permute-start(bf16[64,1024]{1,0:T(8,128)(2,1)S(1)} %get-tuple-element.41), channel_id=1, source_target_pairs={{0,96},{32,0},{64,32},{96,64},{1,97},{33,1},{65,33},{97,65},{2,98}... | collective-permute-start | bytes 393224 | tf_op jit(solution)/shard_map/ppermute | solution.py:208
  80.8 2.6 %collective-permute-done.10.b_ref = bf16[64,1024]{1,0:T(8,128)(2,1)S(1)} collective-permute-done((bf16[64,1024]{1,0:T(8,128)(2,1)S(1)}, bf16[64,1024]{1,0:T(8,128)(2,1)S(1)}, u32[]{:S(2)}, u32[]{:S(2)}) %collective-permute-start.10) | collective-permute-done | bytes 131104 | tf_op jit(solution)/shard_map/ppermute | solution.py:208
  83.4 0.7 collective-permute-done.11.c_ref
  84.1 3.3 %collective-permute-done.12.d_ref = bf16[64,1024]{1,0:T(8,128)(2,1)S(1)} collective-permute-done((bf16[64,1024]{1,0:T(8,128)(2,1)S(1)}, bf16[64,1024]{1,0:T(8,128)(2,1)S(1)}, u32[]{:S(2)}, u32[]{:S(2)}) %collective-permute-start.12) | collective-permute-done | bytes 131104 | tf_op jit(solution)/shard_map/ppermute | solution.py:208
  87.4 0.7 finish_keys.1
  88.1 4.3 %all-to-all-done.1.in_ref = bf16[16,128,128]{2,1,0:T(8,128)(2,1)S(1)} async-done(((bf16[16,128,128]{2,1,0:T(8,128)(2,1)}), bf16[16,128,128]{2,1,0:T(8,128)(2,1)S(1)}, u32[]{:S(2)}, u32[]{:S(2)}) %all-to-all-start.1) | async-done | bytes 524320 | tf_op jit(solution)/shard_map/all_to_all | solution.py:258
  92.4 0.7 finish_queries.1
  (10 shorter events, 0.0 us)
Async XLA Ops:
  2.6 14.8 %collective-permute-start.2 = (bf16[64,1024]{1,0:T(8,128)(2,1)}, bf16[64,1024]{1,0:T(8,128)(2,1)S(1)}, u32[]{:S(2)}, u32[]{:S(2)}) collective-permute-start(bf16[64,1024]{1,0:T(8,128)(2,1)} %get-tuple-element.25.own_ref), channel_id=1, source_target_pairs={{0,64},{32,96},{64,0},{96,32},{1,65},{33,97},{65,1},{97,33},{2,66}... | collective-permute-start | bytes 393224 | tf_op jit(solution)/shard_map/ppermute | solution.py:208
  6.5 11.0 %collective-permute-start.1 = (bf16[64,1024]{1,0:T(8,128)(2,1)}, bf16[64,1024]{1,0:T(8,128)(2,1)S(1)}, u32[]{:S(2)}, u32[]{:S(2)}) collective-permute-start(bf16[64,1024]{1,0:T(8,128)(2,1)} %get-tuple-element.25.own_ref), channel_id=1, source_target_pairs={{0,32},{32,64},{64,96},{96,0},{1,33},{33,65},{65,97},{97,1},{2,34}... | collective-permute-start | bytes 393224 | tf_op jit(solution)/shard_map/ppermute | solution.py:208
  6.9 10.6 %collective-permute-start = (bf16[64,1024]{1,0:T(8,128)(2,1)}, bf16[64,1024]{1,0:T(8,128)(2,1)S(1)}, u32[]{:S(2)}, u32[]{:S(2)}) collective-permute-start(bf16[64,1024]{1,0:T(8,128)(2,1)} %get-tuple-element.25.own_ref), channel_id=1, source_target_pairs={{0,96},{32,0},{64,32},{96,64},{1,97},{33,1},{65,33},{97,65},{2,98}... | collective-permute-start | bytes 393224 | tf_op jit(solution)/shard_map/ppermute | solution.py:208
  9.2 8.3 %copy-start = (bf16[64,1024]{1,0:T(8,128)(2,1)S(1)}, bf16[64,1024]{1,0:T(8,128)(2,1)}, u32[]{:S(2)}) copy-start(bf16[64,1024]{1,0:T(8,128)(2,1)} %get-tuple-element.25.own_ref) | copy-start | bytes 393220
  9.2 24.6 %all-to-all-start = ((bf16[8,264,128]{2,1,0:T(8,128)(2,1)}), bf16[8,264,128]{2,1,0:T(8,128)(2,1)S(1)}, u32[]{:S(2)}, u32[]{:S(2)}) async-start(bf16[8,264,128]{2,1,0:T(8,128)(2,1)} %get-tuple-element.24), calls=%async_computation | async-start | bytes 1081344 | tf_op jit(solution)/shard_map/all_to_all | solution.py:230
  17.7 12.0 %collective-permute-start.4 = (bf16[2,1024,128]{2,1,0:T(8,128)(2,1)S(1)}, bf16[2,1024,128]{2,1,0:T(8,128)(2,1)S(1)}, u32[]{:S(2)}, u32[]{:S(2)}) collective-permute-start(bf16[2,1024,128]{2,1,0:T(8,128)(2,1)S(1)} %join_keys.1.refs_3_), channel_id=1, source_target_pairs={{0,6},{2,0},{4,2},{6,4},{1,7},{3,1},{5,3},{7,5},{8,14},{10,8},{12,... | collective-permute-start | bytes 1572872 | tf_op jit(solution)/shard_map/ppermute | solution.py:208
  20.3 12.5 %collective-permute-start.3 = (bf16[2,1024,128]{2,1,0:T(8,128)(2,1)S(1)}, bf16[2,1024,128]{2,1,0:T(8,128)(2,1)S(1)}, u32[]{:S(2)}, u32[]{:S(2)}) collective-permute-start(bf16[2,1024,128]{2,1,0:T(8,128)(2,1)S(1)} %join_keys.1.refs_3_), channel_id=1, source_target_pairs={{0,2},{2,4},{4,6},{6,0},{1,3},{3,5},{5,7},{7,1},{8,10},{10,12},{12... | collective-permute-start | bytes 1572872 | tf_op jit(solution)/shard_map/ppermute | solution.py:208
  33.7 5.3 %collective-permute-start.5 = (bf16[8,264,128]{2,1,0:T(8,128)(2,1)S(1)}, bf16[8,264,128]{2,1,0:T(8,128)(2,1)S(1)}, u32[]{:S(2)}, u32[]{:S(2)}) collective-permute-start(bf16[8,264,128]{2,1,0:T(8,128)(2,1)S(1)} %all-to-all-done.refs_0_.refs_1_), channel_id=1, source_target_pairs={{0,1},{1,0},{2,3},{3,2},{4,5},{5,4},{6,7},{7,6},{8,9},{9,8},{10,11... | collective-permute-start | bytes 1622024 | tf_op jit(solution)/shard_map/ppermute | solution.py:208
  36.3 17.0 %collective-permute-start.6 = (bf16[2,1024,128]{2,1,0:T(8,128)(2,1)S(1)}, bf16[2,1024,128]{2,1,0:T(8,128)(2,1)}, u32[]{:S(2)}, u32[]{:S(2)}) collective-permute-start(bf16[2,1024,128]{2,1,0:T(8,128)(2,1)S(1)} %join_keys.1.refs_3_), channel_id=1, source_target_pairs={{0,4},{2,6},{4,0},{6,2},{1,5},{3,7},{5,1},{7,3},{8,12},{10,14},{12... | collective-permute-start | bytes 1572872 | tf_op jit(solution)/shard_map/ppermute | solution.py:208
  45.4 23.3 %collective-permute-start.7 = (bf16[256,1024]{1,0:T(8,128)(2,1)}, bf16[256,1024]{1,0:T(8,128)(2,1)}, u32[]{:S(2)}, u32[]{:S(2)}) collective-permute-start(bf16[256,1024]{1,0:T(8,128)(2,1)} %get-tuple-element.33), channel_id=1, source_target_pairs={{0,6},{2,0},{4,2},{6,4},{1,7},{3,1},{5,3},{7,5},{8,14},{10,8},{12,... | collective-permute-start | bytes 1572872 | tf_op jit(solution)/shard_map/ppermute | solution.py:208
  53.1 21.9 %collective-permute-start.8 = (bf16[256,1024]{1,0:T(8,128)(2,1)}, bf16[256,1024]{1,0:T(8,128)(2,1)S(1)}, u32[]{:S(2)}, u32[]{:S(2)}) collective-permute-start(bf16[256,1024]{1,0:T(8,128)(2,1)} %get-tuple-element.36), channel_id=1, source_target_pairs={{0,2},{2,4},{4,6},{6,0},{1,3},{3,5},{5,7},{7,1},{8,10},{10,12},{12... | collective-permute-start | bytes 1572872 | tf_op jit(solution)/shard_map/ppermute | solution.py:208
  60.8 16.9 %collective-permute-start.9 = (bf16[256,1024]{1,0:T(8,128)(2,1)}, bf16[256,1024]{1,0:T(8,128)(2,1)S(1)}, u32[]{:S(2)}, u32[]{:S(2)}) collective-permute-start(bf16[256,1024]{1,0:T(8,128)(2,1)} %get-tuple-element.38), channel_id=1, source_target_pairs={{0,4},{2,6},{4,0},{6,2},{1,5},{3,7},{5,1},{7,3},{8,12},{10,14},{12... | collective-permute-start | bytes 1572872 | tf_op jit(solution)/shard_map/ppermute | solution.py:208
  68.8 23.6 %all-to-all-start.1 = ((bf16[16,128,128]{2,1,0:T(8,128)(2,1)}), bf16[16,128,128]{2,1,0:T(8,128)(2,1)S(1)}, u32[]{:S(2)}, u32[]{:S(2)}) async-start(bf16[16,128,128]{2,1,0:T(8,128)(2,1)} %get-tuple-element.34), calls=%async_computation.1 | async-start | bytes 1048576 | tf_op jit(solution)/shard_map/all_to_all | solution.py:258
  78.0 5.4 %collective-permute-start.10 = (bf16[64,1024]{1,0:T(8,128)(2,1)S(1)}, bf16[64,1024]{1,0:T(8,128)(2,1)S(1)}, u32[]{:S(2)}, u32[]{:S(2)}) collective-permute-start(bf16[64,1024]{1,0:T(8,128)(2,1)S(1)} %get-tuple-element.40), channel_id=1, source_target_pairs={{0,32},{32,64},{64,96},{96,0},{1,33},{33,65},{65,97},{97,1},{2,34}... | collective-permute-start | bytes 393224 | tf_op jit(solution)/shard_map/ppermute | solution.py:208
  78.1 6.0 %collective-permute-start.11 = (bf16[64,1024]{1,0:T(8,128)(2,1)S(1)}, bf16[64,1024]{1,0:T(8,128)(2,1)S(1)}, u32[]{:S(2)}, u32[]{:S(2)}) collective-permute-start(bf16[64,1024]{1,0:T(8,128)(2,1)S(1)} %get-tuple-element.41), channel_id=1, source_target_pairs={{0,96},{32,0},{64,32},{96,64},{1,97},{33,1},{65,33},{97,65},{2,98}... | collective-permute-start | bytes 393224 | tf_op jit(solution)/shard_map/ppermute | solution.py:208
  80.8 6.6 %collective-permute-start.12 = (bf16[64,1024]{1,0:T(8,128)(2,1)S(1)}, bf16[64,1024]{1,0:T(8,128)(2,1)S(1)}, u32[]{:S(2)}, u32[]{:S(2)}) collective-permute-start(bf16[64,1024]{1,0:T(8,128)(2,1)S(1)} %get-tuple-element.42), channel_id=1, source_target_pairs={{0,64},{32,96},{64,0},{96,32},{1,65},{33,97},{65,1},{97,33},{2,66}... | collective-permute-start | bytes 393224 | tf_op jit(solution)/shard_map/ppermute | solution.py:208

commit v4 on v3

--- a/solution.py
+++ b/solution.py
@@ -216,6 +216,7 @@
     sds = jax.ShapeDtypeStruct
     y = lax.axis_index("y").astype(jnp.int32).reshape(1)
     core = lax.axis_index("c").astype(jnp.int32).reshape(1)
+    y, core = lax.optimization_barrier((y, core))
 
     msg, kvt = pl.pallas_call(
         prepare,

time: 93.5 us -> 91.3 us (0.976)
  Pallas kernels: 31.8 us -> 29.2 us
    pallas_call x9, Pallas kernels: 29.8 us -> 27.2 us  [call(): pl.pallas_call(body, out_shape=out_shape, in_specs=[SMEM] * scalars + [VM...]
  transfers between devices with their start and end apart: 15 -> 15, of which waited for: 8 -> 8; matrix products, arithmetic and copies ran while one was open for 0% -> 0% of each run, Pallas kernels for 31% -> 29%
where the time goes in v4:
time: 91.3 us; the launch traced here: 90.9 us
  starting transfers between devices  35.1 us (38%)
  Pallas kernels  29.2 us (32%)
  waiting for transfers between devices  25.9 us (28%)
    pallas_call x9, Pallas kernels, call(): pl.pallas_call(body, out_shape=out_shape, in_specs=[SMEM] * scalars + [VM...  27.2 us
    ppermute x13, waiting for transfers between devices, shift(): lax.ppermute(value, axis, [(i, (i + amount) % size) for i in range(size)])  21.4 us
    ppermute x13, starting transfers between devices, shift(): lax.ppermute(value, axis, [(i, (i + amount) % size) for i in range(size)])  20.9 us
    all_to_all x1, starting transfers between devices, per_device(): q_own = lax.all_to_all(msg, Z, 0, 0, tiled=True)  8.32 us
    all_to_all x1, starting transfers between devices, per_device(): dq = lax.all_to_all(dq, Z + ('c',), 0, 0, tiled=True)  5.89 us
    all_to_all x1, waiting for transfers between devices, per_device(): dq = lax.all_to_all(dq, Z + ('c',), 0, 0, tiled=True)  3.61 us
    pallas_call x1, Pallas kernels, per_device(): pl.pallas_call(prepare, out_shape=(sds((8, MSG, HEAD_DIM), BF16), sds((2...  2.01 us
  transfers between devices with their start and end apart: 15, of which 8 were waited for; matrix products, arithmetic and copies ran while one was open for 0% of the time, Pallas kernels for 29%

profile of v4, /device:TPU:1, one launch (start us, length us, event | category | flops | bytes accessed | tf_op | source)
XLA Modules:
  0.0 90.9 jit_solution(12990187729122106786)
XLA Ops:
  0.6 2.0 %prepare.1 = (bf16[8,264,128]{2,1,0:T(8,128)(2,1)}, bf16[64,1024]{1,0:T(8,128)(2,1)}) custom-call(bf16[128,256]{1,0:T(8,128)(2,1)} %q_hbm.1, bf16[128,256]{1,0:T(8,128)(2,1)} %do_hbm.1, bf16[128,256]{1,0:T(8,128)(2,1)} %o_hbm.1, f32[2,128]{1,0:T(2,128)} %lse_hbm.1, bf16[32,1024]{1,0:T(8,128)(2,1)} %bitcast.6, bf16[32,1024]{1,0:T(8,128)(2,1)} %bitcast.7), custom_call_target="tpu_custom_call" | custom-call | bytes 1048576 | tf_op jit(solution)/shard_map/prepare/pallas_call | solution.py:221
  2.6 3.8 %collective-permute-start.2 = (bf16[64,1024]{1,0:T(8,128)(2,1)}, bf16[64,1024]{1,0:T(8,128)(2,1)S(1)}, u32[]{:S(2)}, u32[]{:S(2)}) collective-permute-start(bf16[64,1024]{1,0:T(8,128)(2,1)} %get-tuple-element.29.own_ref), channel_id=1, source_target_pairs={{0,64},{32,96},{64,0},{96,32},{1,65},{33,97},{65,1},{97,33},{2,66}... | collective-permute-start | bytes 393224 | tf_op jit(solution)/shard_map/ppermute | solution.py:208
  6.5 0.4 collective-permute-start.1
  6.9 2.3 %collective-permute-start = (bf16[64,1024]{1,0:T(8,128)(2,1)}, bf16[64,1024]{1,0:T(8,128)(2,1)S(1)}, u32[]{:S(2)}, u32[]{:S(2)}) collective-permute-start(bf16[64,1024]{1,0:T(8,128)(2,1)} %get-tuple-element.29.own_ref), channel_id=1, source_target_pairs={{0,96},{32,0},{64,32},{96,64},{1,97},{33,1},{65,33},{97,65},{2,98}... | collective-permute-start | bytes 393224 | tf_op jit(solution)/shard_map/ppermute | solution.py:208
  9.2 8.3 %all-to-all-start = ((bf16[8,264,128]{2,1,0:T(8,128)(2,1)}), bf16[8,264,128]{2,1,0:T(8,128)(2,1)S(1)}, u32[]{:S(2)}, u32[]{:S(2)}) async-start(bf16[8,264,128]{2,1,0:T(8,128)(2,1)} %get-tuple-element.27), calls=%async_computation | async-start | bytes 1081344 | tf_op jit(solution)/shard_map/all_to_all | solution.py:231
  17.5 0.0 collective-permute-done.1.prev_ref
  17.5 0.2 join_keys.1.refs_3_
  17.7 2.6 %collective-permute-start.4 = (bf16[2,1024,128]{2,1,0:T(8,128)(2,1)S(1)}, bf16[2,1024,128]{2,1,0:T(8,128)(2,1)S(1)}, u32[]{:S(2)}, u32[]{:S(2)}) collective-permute-start(bf16[2,1024,128]{2,1,0:T(8,128)(2,1)S(1)} %join_keys.1.refs_3_), channel_id=1, source_target_pairs={{0,6},{2,0},{4,2},{6,4},{1,7},{3,1},{5,3},{7,5},{8,14},{10,8},{12,... | collective-permute-start | bytes 1572872 | tf_op jit(solution)/shard_map/ppermute | solution.py:208
  20.3 9.4 %collective-permute-done.4.refs_2_ = bf16[2,1024,128]{2,1,0:T(8,128)(2,1)S(1)} collective-permute-done((bf16[2,1024,128]{2,1,0:T(8,128)(2,1)S(1)}, bf16[2,1024,128]{2,1,0:T(8,128)(2,1)S(1)}, u32[]{:S(2)}, u32[]{:S(2)}) %collective-permute-start.4) | collective-permute-done | bytes 524320 | tf_op jit(solution)/shard_map/ppermute | solution.py:208
  29.7 3.1 %collective-permute-done.3.refs_2_ = bf16[2,1024,128]{2,1,0:T(8,128)(2,1)S(1)} collective-permute-done((bf16[2,1024,128]{2,1,0:T(8,128)(2,1)S(1)}, bf16[2,1024,128]{2,1,0:T(8,128)(2,1)S(1)}, u32[]{:S(2)}, u32[]{:S(2)}) %collective-permute-start.3) | collective-permute-done | bytes 524320 | tf_op jit(solution)/shard_map/ppermute | solution.py:208
  32.8 0.9 all-to-all-done.refs_0_.refs_1_
  33.7 2.5 %collective-permute-start.5 = (bf16[8,264,128]{2,1,0:T(8,128)(2,1)S(1)}, bf16[8,264,128]{2,1,0:T(8,128)(2,1)S(1)}, u32[]{:S(2)}, u32[]{:S(2)}) collective-permute-start(bf16[8,264,128]{2,1,0:T(8,128)(2,1)S(1)} %all-to-all-done.refs_0_.refs_1_), channel_id=1, source_target_pairs={{0,1},{1,0},{2,3},{3,2},{4,5},{5,4},{6,7},{7,6},{8,9},{9,8},{10,11... | collective-permute-start | bytes 1622024 | tf_op jit(solution)/shard_map/ppermute | solution.py:208
  36.3 2.7 %collective-permute-start.6 = (bf16[2,1024,128]{2,1,0:T(8,128)(2,1)S(1)}, bf16[2,1024,128]{2,1,0:T(8,128)(2,1)S(1)}, u32[]{:S(2)}, u32[]{:S(2)}) collective-permute-start(bf16[2,1024,128]{2,1,0:T(8,128)(2,1)S(1)} %join_keys.1.refs_3_), channel_id=1, source_target_pairs={{0,4},{2,6},{4,0},{6,2},{1,5},{3,7},{5,1},{7,3},{8,12},{10,14},{12... | collective-permute-start | bytes 1572872 | tf_op jit(solution)/shard_map/ppermute | solution.py:208
  39.0 5.6 %attend_prev.1 = (f32[2048,128]{1,0:T(8,128)S(1)}, bf16[256,1024]{1,0:T(8,128)(2,1)S(1)}) custom-call(bf16[8,264,128]{2,1,0:T(8,128)(2,1)S(1)} %all-to-all-done.refs_0_.refs_1_, bf16[8,264,128]{2,1,0:T(8,128)(2,1)S(1)} %collective-permute-done.5.refs_1_.refs_2_, bf16[2,1024,128]{2,1,0:T(8,128)(2,1)S(1)} %collective-permute-done.3.refs_2_), custom_call_target="tpu_custom_call" | custom-call | tf_op jit(solution)/shard_map/attend_prev/pallas_call | solution.py:40
  44.7 1.5 %collective-permute-start.7 = (bf16[256,1024]{1,0:T(8,128)(2,1)S(1)}, bf16[256,1024]{1,0:T(8,128)(2,1)S(1)}, u32[]{:S(2)}, u32[]{:S(2)}) collective-permute-start(bf16[256,1024]{1,0:T(8,128)(2,1)S(1)} %get-tuple-element.37), channel_id=1, source_target_pairs={{0,6},{2,0},{4,2},{6,4},{1,7},{3,1},{5,3},{7,5},{8,14},{10,8},{12,... | collective-permute-start | bytes 1572872 | tf_op jit(solution)/shard_map/ppermute | solution.py:208
  46.2 5.6 %attend_next.1 = (f32[2048,128]{1,0:T(8,128)S(1)}, bf16[256,1024]{1,0:T(8,128)(2,1)S(1)}) custom-call(bf16[8,264,128]{2,1,0:T(8,128)(2,1)S(1)} %all-to-all-done.refs_0_.refs_1_, bf16[8,264,128]{2,1,0:T(8,128)(2,1)S(1)} %collective-permute-done.5.refs_1_.refs_2_, bf16[2,1024,128]{2,1,0:T(8,128)(2,1)S(1)} %collective-permute-done.4.refs_2_, ...), custom_call_target="tpu_custom_call" | custom-call | tf_op jit(solution)/shard_map/attend_next/pallas_call | solution.py:40
  51.9 0.3 collective-permute-start.8
  52.1 6.4 %attend_far.1 = (f32[2048,128]{1,0:T(8,128)S(1)}, bf16[256,1024]{1,0:T(8,128)(2,1)}) custom-call(bf16[8,264,128]{2,1,0:T(8,128)(2,1)S(1)} %all-to-all-done.refs_0_.refs_1_, bf16[8,264,128]{2,1,0:T(8,128)(2,1)S(1)} %collective-permute-done.5.refs_1_.refs_2_, bf16[2,1024,128]{2,1,0:T(8,128)(2,1)S(1)} %collective-permute-done.6.refs_2_, ...), custom_call_target="tpu_custom_call" | custom-call | tf_op jit(solution)/shard_map/attend_far/pallas_call | solution.py:40
  58.5 2.0 %collective-permute-start.9 = (bf16[256,1024]{1,0:T(8,128)(2,1)}, bf16[256,1024]{1,0:T(8,128)(2,1)S(1)}, u32[]{:S(2)}, u32[]{:S(2)}) collective-permute-start(bf16[256,1024]{1,0:T(8,128)(2,1)} %get-tuple-element.42), channel_id=1, source_target_pairs={{0,4},{2,6},{4,0},{6,2},{1,5},{3,7},{5,1},{7,3},{8,12},{10,14},{12... | collective-permute-start | bytes 1572872 | tf_op jit(solution)/shard_map/ppermute | solution.py:208
  60.5 6.5 %attend_own.1 = (bf16[16,128,128]{2,1,0:T(8,128)(2,1)}, bf16[256,1024]{1,0:T(8,128)(2,1)S(1)}) custom-call(s32[1]{0:T(128)} %bitcast.1.refs_0_, bf16[8,264,128]{2,1,0:T(8,128)(2,1)S(1)} %all-to-all-done.refs_0_.refs_1_, bf16[8,264,128]{2,1,0:T(8,128)(2,1)S(1)} %collective-permute-done.5.refs_1_.refs_2_, bf16[2,1024,128]{2,1,0:T(8,128)(2,1)S(1)} %join_keys.1.refs_3_, ...), custom_call_target="tpu_custom_call" | custom-call | tf_op jit(solution)/shard_map/attend_own/pallas_call | solution.py:40
  67.0 5.9 %all-to-all-start.1 = ((bf16[16,128,128]{2,1,0:T(8,128)(2,1)}), bf16[16,128,128]{2,1,0:T(8,128)(2,1)S(1)}, u32[]{:S(2)}, u32[]{:S(2)}) async-start(bf16[16,128,128]{2,1,0:T(8,128)(2,1)} %get-tuple-element.38), calls=%async_computation.1 | async-start | bytes 1048576 | tf_op jit(solution)/shard_map/all_to_all | solution.py:259
  72.9 1.1 %add_sums.1.near_ref = f32[256,1024]{1,0:T(8,128)S(1)} custom-call(bf16[256,1024]{1,0:T(8,128)(2,1)S(1)} %collective-permute-done.7.a_ref, bf16[256,1024]{1,0:T(8,128)(2,1)} %collective-permute-done.8.b_ref), custom_call_target="tpu_custom_call" | custom-call | flops 137438953472 | bytes 1024 | tf_op jit(solution)/shard_map/add_sums/pallas_call | solution.py:40
  74.0 2.3 %collective-permute-done.9.back_ref = bf16[256,1024]{1,0:T(8,128)(2,1)S(1)} collective-permute-done((bf16[256,1024]{1,0:T(8,128)(2,1)}, bf16[256,1024]{1,0:T(8,128)(2,1)S(1)}, u32[]{:S(2)}, u32[]{:S(2)}) %collective-permute-start.9) | collective-permute-done | bytes 524320 | tf_op jit(solution)/shard_map/ppermute | solution.py:208
  76.3 0.3 pack_sums.1
  76.6 0.1 collective-permute-start.10
  76.7 2.7 %collective-permute-start.11 = (bf16[64,1024]{1,0:T(8,128)(2,1)S(1)}, bf16[64,1024]{1,0:T(8,128)(2,1)S(1)}, u32[]{:S(2)}, u32[]{:S(2)}) collective-permute-start(bf16[64,1024]{1,0:T(8,128)(2,1)S(1)} %get-tuple-element.45), channel_id=1, source_target_pairs={{0,96},{32,0},{64,32},{96,64},{1,97},{33,1},{65,33},{97,65},{2,98}... | collective-permute-start | bytes 393224 | tf_op jit(solution)/shard_map/ppermute | solution.py:208
  79.3 2.6 %collective-permute-done.10.b_ref = bf16[64,1024]{1,0:T(8,128)(2,1)S(1)} collective-permute-done((bf16[64,1024]{1,0:T(8,128)(2,1)S(1)}, bf16[64,1024]{1,0:T(8,128)(2,1)S(1)}, u32[]{:S(2)}, u32[]{:S(2)}) %collective-permute-start.10) | collective-permute-done | bytes 131104 | tf_op jit(solution)/shard_map/ppermute | solution.py:208
  82.0 0.7 collective-permute-done.11.c_ref
  82.7 3.2 %collective-permute-done.12.d_ref = bf16[64,1024]{1,0:T(8,128)(2,1)S(1)} collective-permute-done((bf16[64,1024]{1,0:T(8,128)(2,1)S(1)}, bf16[64,1024]{1,0:T(8,128)(2,1)S(1)}, u32[]{:S(2)}, u32[]{:S(2)}) %collective-permute-start.12) | collective-permute-done | bytes 131104 | tf_op jit(solution)/shard_map/ppermute | solution.py:208
  85.9 0.7 finish_keys.1
  86.6 3.6 %all-to-all-done.1.in_ref = bf16[16,128,128]{2,1,0:T(8,128)(2,1)S(1)} async-done(((bf16[16,128,128]{2,1,0:T(8,128)(2,1)}), bf16[16,128,128]{2,1,0:T(8,128)(2,1)S(1)}, u32[]{:S(2)}, u32[]{:S(2)}) %all-to-all-start.1) | async-done | bytes 524320 | tf_op jit(solution)/shard_map/all_to_all | solution.py:259
  90.2 0.7 finish_queries.1
  (10 shorter events, 0.0 us)
Async XLA Ops:
  2.6 14.8 %collective-permute-start.2 = (bf16[64,1024]{1,0:T(8,128)(2,1)}, bf16[64,1024]{1,0:T(8,128)(2,1)S(1)}, u32[]{:S(2)}, u32[]{:S(2)}) collective-permute-start(bf16[64,1024]{1,0:T(8,128)(2,1)} %get-tuple-element.29.own_ref), channel_id=1, source_target_pairs={{0,64},{32,96},{64,0},{96,32},{1,65},{33,97},{65,1},{97,33},{2,66}... | collective-permute-start | bytes 393224 | tf_op jit(solution)/shard_map/ppermute | solution.py:208
  6.5 11.0 %collective-permute-start.1 = (bf16[64,1024]{1,0:T(8,128)(2,1)}, bf16[64,1024]{1,0:T(8,128)(2,1)S(1)}, u32[]{:S(2)}, u32[]{:S(2)}) collective-permute-start(bf16[64,1024]{1,0:T(8,128)(2,1)} %get-tuple-element.29.own_ref), channel_id=1, source_target_pairs={{0,32},{32,64},{64,96},{96,0},{1,33},{33,65},{65,97},{97,1},{2,34}... | collective-permute-start | bytes 393224 | tf_op jit(solution)/shard_map/ppermute | solution.py:208
  6.9 10.6 %collective-permute-start = (bf16[64,1024]{1,0:T(8,128)(2,1)}, bf16[64,1024]{1,0:T(8,128)(2,1)S(1)}, u32[]{:S(2)}, u32[]{:S(2)}) collective-permute-start(bf16[64,1024]{1,0:T(8,128)(2,1)} %get-tuple-element.29.own_ref), channel_id=1, source_target_pairs={{0,96},{32,0},{64,32},{96,64},{1,97},{33,1},{65,33},{97,65},{2,98}... | collective-permute-start | bytes 393224 | tf_op jit(solution)/shard_map/ppermute | solution.py:208
  9.2 8.3 %copy-start = (bf16[64,1024]{1,0:T(8,128)(2,1)S(1)}, bf16[64,1024]{1,0:T(8,128)(2,1)}, u32[]{:S(2)}) copy-start(bf16[64,1024]{1,0:T(8,128)(2,1)} %get-tuple-element.29.own_ref) | copy-start | bytes 393220
  9.2 24.6 %all-to-all-start = ((bf16[8,264,128]{2,1,0:T(8,128)(2,1)}), bf16[8,264,128]{2,1,0:T(8,128)(2,1)S(1)}, u32[]{:S(2)}, u32[]{:S(2)}) async-start(bf16[8,264,128]{2,1,0:T(8,128)(2,1)} %get-tuple-element.27), calls=%async_computation | async-start | bytes 1081344 | tf_op jit(solution)/shard_map/all_to_all | solution.py:231
  17.7 12.0 %collective-permute-start.4 = (bf16[2,1024,128]{2,1,0:T(8,128)(2,1)S(1)}, bf16[2,1024,128]{2,1,0:T(8,128)(2,1)S(1)}, u32[]{:S(2)}, u32[]{:S(2)}) collective-permute-start(bf16[2,1024,128]{2,1,0:T(8,128)(2,1)S(1)} %join_keys.1.refs_3_), channel_id=1, source_target_pairs={{0,6},{2,0},{4,2},{6,4},{1,7},{3,1},{5,3},{7,5},{8,14},{10,8},{12,... | collective-permute-start | bytes 1572872 | tf_op jit(solution)/shard_map/ppermute | solution.py:208
  20.3 12.5 %collective-permute-start.3 = (bf16[2,1024,128]{2,1,0:T(8,128)(2,1)S(1)}, bf16[2,1024,128]{2,1,0:T(8,128)(2,1)S(1)}, u32[]{:S(2)}, u32[]{:S(2)}) collective-permute-start(bf16[2,1024,128]{2,1,0:T(8,128)(2,1)S(1)} %join_keys.1.refs_3_), channel_id=1, source_target_pairs={{0,2},{2,4},{4,6},{6,0},{1,3},{3,5},{5,7},{7,1},{8,10},{10,12},{12... | collective-permute-start | bytes 1572872 | tf_op jit(solution)/shard_map/ppermute | solution.py:208
  33.7 5.3 %collective-permute-start.5 = (bf16[8,264,128]{2,1,0:T(8,128)(2,1)S(1)}, bf16[8,264,128]{2,1,0:T(8,128)(2,1)S(1)}, u32[]{:S(2)}, u32[]{:S(2)}) collective-permute-start(bf16[8,264,128]{2,1,0:T(8,128)(2,1)S(1)} %all-to-all-done.refs_0_.refs_1_), channel_id=1, source_target_pairs={{0,1},{1,0},{2,3},{3,2},{4,5},{5,4},{6,7},{7,6},{8,9},{9,8},{10,11... | collective-permute-start | bytes 1622024 | tf_op jit(solution)/shard_map/ppermute | solution.py:208
  36.3 15.8 %collective-permute-start.6 = (bf16[2,1024,128]{2,1,0:T(8,128)(2,1)S(1)}, bf16[2,1024,128]{2,1,0:T(8,128)(2,1)S(1)}, u32[]{:S(2)}, u32[]{:S(2)}) collective-permute-start(bf16[2,1024,128]{2,1,0:T(8,128)(2,1)S(1)} %join_keys.1.refs_3_), channel_id=1, source_target_pairs={{0,4},{2,6},{4,0},{6,2},{1,5},{3,7},{5,1},{7,3},{8,12},{10,14},{12... | collective-permute-start | bytes 1572872 | tf_op jit(solution)/shard_map/ppermute | solution.py:208
  44.7 22.3 %collective-permute-start.7 = (bf16[256,1024]{1,0:T(8,128)(2,1)S(1)}, bf16[256,1024]{1,0:T(8,128)(2,1)S(1)}, u32[]{:S(2)}, u32[]{:S(2)}) collective-permute-start(bf16[256,1024]{1,0:T(8,128)(2,1)S(1)} %get-tuple-element.37), channel_id=1, source_target_pairs={{0,6},{2,0},{4,2},{6,4},{1,7},{3,1},{5,3},{7,5},{8,14},{10,8},{12,... | collective-permute-start | bytes 1572872 | tf_op jit(solution)/shard_map/ppermute | solution.py:208
  51.9 21.0 %collective-permute-start.8 = (bf16[256,1024]{1,0:T(8,128)(2,1)S(1)}, bf16[256,1024]{1,0:T(8,128)(2,1)}, u32[]{:S(2)}, u32[]{:S(2)}) collective-permute-start(bf16[256,1024]{1,0:T(8,128)(2,1)S(1)} %get-tuple-element.40), channel_id=1, source_target_pairs={{0,2},{2,4},{4,6},{6,0},{1,3},{3,5},{5,7},{7,1},{8,10},{10,12},{12... | collective-permute-start | bytes 1572872 | tf_op jit(solution)/shard_map/ppermute | solution.py:208
  58.5 17.8 %collective-permute-start.9 = (bf16[256,1024]{1,0:T(8,128)(2,1)}, bf16[256,1024]{1,0:T(8,128)(2,1)S(1)}, u32[]{:S(2)}, u32[]{:S(2)}) collective-permute-start(bf16[256,1024]{1,0:T(8,128)(2,1)} %get-tuple-element.42), channel_id=1, source_target_pairs={{0,4},{2,6},{4,0},{6,2},{1,5},{3,7},{5,1},{7,3},{8,12},{10,14},{12... | collective-permute-start | bytes 1572872 | tf_op jit(solution)/shard_map/ppermute | solution.py:208
  67.0 23.2 %all-to-all-start.1 = ((bf16[16,128,128]{2,1,0:T(8,128)(2,1)}), bf16[16,128,128]{2,1,0:T(8,128)(2,1)S(1)}, u32[]{:S(2)}, u32[]{:S(2)}) async-start(bf16[16,128,128]{2,1,0:T(8,128)(2,1)} %get-tuple-element.38), calls=%async_computation.1 | async-start | bytes 1048576 | tf_op jit(solution)/shard_map/all_to_all | solution.py:259
  76.6 5.4 %collective-permute-start.10 = (bf16[64,1024]{1,0:T(8,128)(2,1)S(1)}, bf16[64,1024]{1,0:T(8,128)(2,1)S(1)}, u32[]{:S(2)}, u32[]{:S(2)}) collective-permute-start(bf16[64,1024]{1,0:T(8,128)(2,1)S(1)} %get-tuple-element.44), channel_id=1, source_target_pairs={{0,32},{32,64},{64,96},{96,0},{1,33},{33,65},{65,97},{97,1},{2,34}... | collective-permute-start | bytes 393224 | tf_op jit(solution)/shard_map/ppermute | solution.py:208
  76.7 6.0 %collective-permute-start.11 = (bf16[64,1024]{1,0:T(8,128)(2,1)S(1)}, bf16[64,1024]{1,0:T(8,128)(2,1)S(1)}, u32[]{:S(2)}, u32[]{:S(2)}) collective-permute-start(bf16[64,1024]{1,0:T(8,128)(2,1)S(1)} %get-tuple-element.45), channel_id=1, source_target_pairs={{0,96},{32,0},{64,32},{96,64},{1,97},{33,1},{65,33},{97,65},{2,98}... | collective-permute-start | bytes 393224 | tf_op jit(solution)/shard_map/ppermute | solution.py:208
  79.3 6.5 %collective-permute-start.12 = (bf16[64,1024]{1,0:T(8,128)(2,1)S(1)}, bf16[64,1024]{1,0:T(8,128)(2,1)S(1)}, u32[]{:S(2)}, u32[]{:S(2)}) collective-permute-start(bf16[64,1024]{1,0:T(8,128)(2,1)S(1)} %get-tuple-element.46), channel_id=1, source_target_pairs={{0,64},{32,96},{64,0},{96,32},{1,65},{33,97},{65,1},{97,33},{2,66}... | collective-permute-start | bytes 393224 | tf_op jit(solution)/shard_map/ppermute | solution.py:208

commit v5 on v4

--- a/solution.py
+++ b/solution.py
@@ -94,17 +94,15 @@
     kv_ref[1] = vt[...].T
 
 
-def attend(first, last, blocks, *refs):
+def attend(first, last, *refs):
     refs = list(refs)
     core_ref = refs.pop(0) if last else None
     msg_refs = [refs.pop(0), refs.pop(0)]
     kv_ref = refs.pop(0)
     dq_in = None if first else refs.pop(0)
     dq_out = refs.pop(0)
-    sums_ref, dk_s, dv_s = refs[:3]
-    dq_s = refs[3] if last else dq_out
-    dk_s[...] = jnp.zeros_like(dk_s)
-    dv_s[...] = jnp.zeros_like(dv_s)
+    sums_ref, dk_s, dv_s = refs
+    core = core_ref[0] if last else None
     key, value = kv_ref[0], kv_ref[1]
 
     def pair(msg_ref, place, start, size):
@@ -113,35 +111,31 @@
             axis=0 if size == ROWS else 1,
         )
 
-    def step(index, _):
-        for block in range(blocks):
-            which = block % 2
-            place = index * blocks + block - which
-            msg_ref = msg_refs[which]
-            query, grad = pair(msg_ref, place, 0, ROWS), pair(msg_ref, place, ROWS, ROWS)
-            side = pair(msg_ref, place, 2 * ROWS, SIDE).astype(F32)
-            lse = side[0:1] + side[1:2] + side[2:3]
-            delta = side[3:4] + side[4:5] + side[5:6]
-            scores = dot(key, query, NT)
-            probs = jnp.exp2(scores * (SCALING * LOG2E) - lse)
-            grad_probs = dot(value, grad, NT)
-            grad_scores = (probs * (grad_probs - delta)).astype(BF16)
-            dv_s[...] += dot(probs.astype(BF16), grad, NN)
-            dk_s[...] += dot(grad_scores, query, NN)
-            dq = dot(grad_scores, key, TN)
-            rows = pl.ds(pl.multiple_of(which * 8 * ROWS + place * ROWS, 256), 256)
-            dq_s[rows, :] = dq if first else dq_in[rows, :] + dq
-        return 0
-
-    if blocks == 8:
-        step(0, 0)
-    else:
-        lax.fori_loop(0, 8 // blocks, step, 0)
-    if last:
-        core = core_ref[0]
-        for index in range(16):
-            slot = 2 * (index % 8) + (core if index < 8 else 1 - core)
-            dq_out[slot] = dq_s[pl.ds(index * ROWS, ROWS), :].astype(BF16)
+    for block in range(8):
+        which, place = block % 2, block - block % 2
+        msg_ref = msg_refs[which]
+        query, grad = pair(msg_ref, place, 0, ROWS), pair(msg_ref, place, ROWS, ROWS)
+        side = pair(msg_ref, place, 2 * ROWS, SIDE).astype(F32)
+        lse = side[0:1] + side[1:2] + side[2:3]
+        delta = side[3:4] + side[4:5] + side[5:6]
+        scores = dot(key, query, NT)
+        probs = jnp.exp2(scores * (SCALING * LOG2E) - lse)
+        grad_probs = dot(value, grad, NT)
+        grad_scores = (probs * (grad_probs - delta)).astype(BF16)
+        dv = dot(probs.astype(BF16), grad, NN)
+        dk = dot(grad_scores, query, NN)
+        dv_s[...] = dv if block == 0 else dv_s[...] + dv
+        dk_s[...] = dk if block == 0 else dk_s[...] + dk
+        start = (which * 8 + place) * ROWS
+        dq = dot(grad_scores, key, TN)
+        if not first:
+            dq = dq_in[start : start + 2 * ROWS, :] + dq
+        if last:
+            side_core = core if which == 0 else 1 - core
+            dq_out[2 * place + side_core] = dq[:ROWS].astype(BF16)
+            dq_out[2 * place + 2 + side_core] = dq[ROWS:].astype(BF16)
+        else:
+            dq_out[start : start + 2 * ROWS, :] = dq
     dk = (dk_s[...] * SCALING).astype(BF16).T
     dv = dv_s[...].astype(BF16).T
     for y in range(4):
@@ -150,7 +144,7 @@
         sums_ref[(2 * y + 1) * FEATS : (2 * y + 2) * FEATS, :] = dv[rows]
 
 
-def attend_call(msgs, chunk, dq_in, name, core=None, weight=0, blocks=8):
+def attend_call(msgs, chunk, dq_in, name, core=None):
     sds = jax.ShapeDtypeStruct
     first = dq_in is None
     last = core is not None
@@ -161,17 +155,12 @@
         out = (sds((16 * ROWS, HEAD_DIM), F32),)
     out += (sds((8 * FEATS, KEYS), BF16),)
     return call(
-        functools.partial(attend, first, last, blocks),
+        functools.partial(attend, first, last),
         out,
         operands,
         name,
-        flops=int(weight * 10 * 2**27),
-        moved=int(weight * 2**23),
-        scratch=[
-            pltpu.VMEM((KEYS, HEAD_DIM), F32),
-            pltpu.VMEM((KEYS, HEAD_DIM), F32),
-        ]
-        + [pltpu.VMEM((16 * ROWS, HEAD_DIM), F32)] * last,
+        moved=0,
+        scratch=[pltpu.VMEM((KEYS, HEAD_DIM), F32)] * 2,
         scalars=int(last),
         limit=30,
     )

time: 91.3 us -> 91.2 us (level)
  no operation moved by 1% of the time
where the time goes in v5:
time: 91.2 us; the launch traced here: 90.9 us
  starting transfers between devices  35.1 us (38%)
  Pallas kernels  29.2 us (32%)
  waiting for transfers between devices  25.9 us (28%)
    pallas_call x9, Pallas kernels, call(): pl.pallas_call(body, out_shape=out_shape, in_specs=[SMEM] * scalars + [VM...  27.2 us
    ppermute x13, waiting for transfers between devices, shift(): lax.ppermute(value, axis, [(i, (i + amount) % size) for i in range(size)])  21.4 us
    ppermute x13, starting transfers between devices, shift(): lax.ppermute(value, axis, [(i, (i + amount) % size) for i in range(size)])  20.9 us
    all_to_all x1, starting transfers between devices, per_device(): q_own = lax.all_to_all(msg, Z, 0, 0, tiled=True)  8.32 us
    all_to_all x1, starting transfers between devices, per_device(): dq = lax.all_to_all(dq, Z + ('c',), 0, 0, tiled=True)  5.89 us
    all_to_all x1, waiting for transfers between devices, per_device(): dq = lax.all_to_all(dq, Z + ('c',), 0, 0, tiled=True)  3.6 us
    pallas_call x1, Pallas kernels, per_device(): pl.pallas_call(prepare, out_shape=(sds((8, MSG, HEAD_DIM), BF16), sds((2...  2.01 us
  transfers between devices with their start and end apart: 15, of which 8 were waited for; matrix products, arithmetic and copies ran while one was open for 0% of the time, Pallas kernels for 29%

profile of v5, /device:TPU:1, one launch (start us, length us, event | category | flops | bytes accessed | tf_op | source)
XLA Modules:
  0.0 90.9 jit_solution(12551099360414142777)
XLA Ops:
  0.6 2.0 %prepare.1 = (bf16[8,264,128]{2,1,0:T(8,128)(2,1)}, bf16[64,1024]{1,0:T(8,128)(2,1)}) custom-call(bf16[128,256]{1,0:T(8,128)(2,1)} %q_hbm.1, bf16[128,256]{1,0:T(8,128)(2,1)} %do_hbm.1, bf16[128,256]{1,0:T(8,128)(2,1)} %o_hbm.1, f32[2,128]{1,0:T(2,128)} %lse_hbm.1, bf16[32,1024]{1,0:T(8,128)(2,1)} %bitcast.6, bf16[32,1024]{1,0:T(8,128)(2,1)} %bitcast.7), custom_call_target="tpu_custom_call" | custom-call | bytes 1048576 | tf_op jit(solution)/shard_map/prepare/pallas_call | solution.py:210
  2.6 3.8 %collective-permute-start.2 = (bf16[64,1024]{1,0:T(8,128)(2,1)}, bf16[64,1024]{1,0:T(8,128)(2,1)S(1)}, u32[]{:S(2)}, u32[]{:S(2)}) collective-permute-start(bf16[64,1024]{1,0:T(8,128)(2,1)} %get-tuple-element.29.own_ref), channel_id=1, source_target_pairs={{0,64},{32,96},{64,0},{96,32},{1,65},{33,97},{65,1},{97,33},{2,66}... | collective-permute-start | bytes 393224 | tf_op jit(solution)/shard_map/ppermute | solution.py:197
  6.5 0.4 collective-permute-start.1
  6.9 2.3 %collective-permute-start = (bf16[64,1024]{1,0:T(8,128)(2,1)}, bf16[64,1024]{1,0:T(8,128)(2,1)S(1)}, u32[]{:S(2)}, u32[]{:S(2)}) collective-permute-start(bf16[64,1024]{1,0:T(8,128)(2,1)} %get-tuple-element.29.own_ref), channel_id=1, source_target_pairs={{0,96},{32,0},{64,32},{96,64},{1,97},{33,1},{65,33},{97,65},{2,98}... | collective-permute-start | bytes 393224 | tf_op jit(solution)/shard_map/ppermute | solution.py:197
  9.2 8.3 %all-to-all-start = ((bf16[8,264,128]{2,1,0:T(8,128)(2,1)}), bf16[8,264,128]{2,1,0:T(8,128)(2,1)S(1)}, u32[]{:S(2)}, u32[]{:S(2)}) async-start(bf16[8,264,128]{2,1,0:T(8,128)(2,1)} %get-tuple-element.27), calls=%async_computation | async-start | bytes 1081344 | tf_op jit(solution)/shard_map/all_to_all | solution.py:220
  17.5 0.0 collective-permute-done.1.prev_ref
  17.5 0.2 join_keys.1.refs_3_
  17.7 2.6 %collective-permute-start.4 = (bf16[2,1024,128]{2,1,0:T(8,128)(2,1)S(1)}, bf16[2,1024,128]{2,1,0:T(8,128)(2,1)S(1)}, u32[]{:S(2)}, u32[]{:S(2)}) collective-permute-start(bf16[2,1024,128]{2,1,0:T(8,128)(2,1)S(1)} %join_keys.1.refs_3_), channel_id=1, source_target_pairs={{0,6},{2,0},{4,2},{6,4},{1,7},{3,1},{5,3},{7,5},{8,14},{10,8},{12,... | collective-permute-start | bytes 1572872 | tf_op jit(solution)/shard_map/ppermute | solution.py:197
  20.3 9.4 %collective-permute-done.4.refs_2_ = bf16[2,1024,128]{2,1,0:T(8,128)(2,1)S(1)} collective-permute-done((bf16[2,1024,128]{2,1,0:T(8,128)(2,1)S(1)}, bf16[2,1024,128]{2,1,0:T(8,128)(2,1)S(1)}, u32[]{:S(2)}, u32[]{:S(2)}) %collective-permute-start.4) | collective-permute-done | bytes 524320 | tf_op jit(solution)/shard_map/ppermute | solution.py:197
  29.7 3.1 %collective-permute-done.3.refs_2_ = bf16[2,1024,128]{2,1,0:T(8,128)(2,1)S(1)} collective-permute-done((bf16[2,1024,128]{2,1,0:T(8,128)(2,1)S(1)}, bf16[2,1024,128]{2,1,0:T(8,128)(2,1)S(1)}, u32[]{:S(2)}, u32[]{:S(2)}) %collective-permute-start.3) | collective-permute-done | bytes 524320 | tf_op jit(solution)/shard_map/ppermute | solution.py:197
  32.8 0.9 all-to-all-done.refs_0_.refs_1_
  33.7 2.5 %collective-permute-start.5 = (bf16[8,264,128]{2,1,0:T(8,128)(2,1)S(1)}, bf16[8,264,128]{2,1,0:T(8,128)(2,1)S(1)}, u32[]{:S(2)}, u32[]{:S(2)}) collective-permute-start(bf16[8,264,128]{2,1,0:T(8,128)(2,1)S(1)} %all-to-all-done.refs_0_.refs_1_), channel_id=1, source_target_pairs={{0,1},{1,0},{2,3},{3,2},{4,5},{5,4},{6,7},{7,6},{8,9},{9,8},{10,11... | collective-permute-start | bytes 1622024 | tf_op jit(solution)/shard_map/ppermute | solution.py:197
  36.3 2.7 %collective-permute-start.6 = (bf16[2,1024,128]{2,1,0:T(8,128)(2,1)S(1)}, bf16[2,1024,128]{2,1,0:T(8,128)(2,1)S(1)}, u32[]{:S(2)}, u32[]{:S(2)}) collective-permute-start(bf16[2,1024,128]{2,1,0:T(8,128)(2,1)S(1)} %join_keys.1.refs_3_), channel_id=1, source_target_pairs={{0,4},{2,6},{4,0},{6,2},{1,5},{3,7},{5,1},{7,3},{8,12},{10,14},{12... | collective-permute-start | bytes 1572872 | tf_op jit(solution)/shard_map/ppermute | solution.py:197
  39.0 5.6 %attend_prev.1 = (f32[2048,128]{1,0:T(8,128)S(1)}, bf16[256,1024]{1,0:T(8,128)(2,1)S(1)}) custom-call(bf16[8,264,128]{2,1,0:T(8,128)(2,1)S(1)} %all-to-all-done.refs_0_.refs_1_, bf16[8,264,128]{2,1,0:T(8,128)(2,1)S(1)} %collective-permute-done.5.refs_1_.refs_2_, bf16[2,1024,128]{2,1,0:T(8,128)(2,1)S(1)} %collective-permute-done.3.refs_2_), custom_call_target="tpu_custom_call" | custom-call | tf_op jit(solution)/shard_map/attend_prev/pallas_call | solution.py:40
  44.7 1.5 %collective-permute-start.7 = (bf16[256,1024]{1,0:T(8,128)(2,1)S(1)}, bf16[256,1024]{1,0:T(8,128)(2,1)S(1)}, u32[]{:S(2)}, u32[]{:S(2)}) collective-permute-start(bf16[256,1024]{1,0:T(8,128)(2,1)S(1)} %get-tuple-element.37), channel_id=1, source_target_pairs={{0,6},{2,0},{4,2},{6,4},{1,7},{3,1},{5,3},{7,5},{8,14},{10,8},{12,... | collective-permute-start | bytes 1572872 | tf_op jit(solution)/shard_map/ppermute | solution.py:197
  46.2 5.6 %attend_next.1 = (f32[2048,128]{1,0:T(8,128)S(1)}, bf16[256,1024]{1,0:T(8,128)(2,1)S(1)}) custom-call(bf16[8,264,128]{2,1,0:T(8,128)(2,1)S(1)} %all-to-all-done.refs_0_.refs_1_, bf16[8,264,128]{2,1,0:T(8,128)(2,1)S(1)} %collective-permute-done.5.refs_1_.refs_2_, bf16[2,1024,128]{2,1,0:T(8,128)(2,1)S(1)} %collective-permute-done.4.refs_2_, ...), custom_call_target="tpu_custom_call" | custom-call | tf_op jit(solution)/shard_map/attend_next/pallas_call | solution.py:40
  51.9 0.3 collective-permute-start.8
  52.1 6.4 %attend_far.1 = (f32[2048,128]{1,0:T(8,128)S(1)}, bf16[256,1024]{1,0:T(8,128)(2,1)}) custom-call(bf16[8,264,128]{2,1,0:T(8,128)(2,1)S(1)} %all-to-all-done.refs_0_.refs_1_, bf16[8,264,128]{2,1,0:T(8,128)(2,1)S(1)} %collective-permute-done.5.refs_1_.refs_2_, bf16[2,1024,128]{2,1,0:T(8,128)(2,1)S(1)} %collective-permute-done.6.refs_2_, ...), custom_call_target="tpu_custom_call" | custom-call | tf_op jit(solution)/shard_map/attend_far/pallas_call | solution.py:40
  58.5 2.0 %collective-permute-start.9 = (bf16[256,1024]{1,0:T(8,128)(2,1)}, bf16[256,1024]{1,0:T(8,128)(2,1)S(1)}, u32[]{:S(2)}, u32[]{:S(2)}) collective-permute-start(bf16[256,1024]{1,0:T(8,128)(2,1)} %get-tuple-element.42), channel_id=1, source_target_pairs={{0,4},{2,6},{4,0},{6,2},{1,5},{3,7},{5,1},{7,3},{8,12},{10,14},{12... | collective-permute-start | bytes 1572872 | tf_op jit(solution)/shard_map/ppermute | solution.py:197
  60.5 6.5 %attend_own.1 = (bf16[16,128,128]{2,1,0:T(8,128)(2,1)}, bf16[256,1024]{1,0:T(8,128)(2,1)S(1)}) custom-call(s32[1]{0:T(128)} %bitcast.1.refs_0_, bf16[8,264,128]{2,1,0:T(8,128)(2,1)S(1)} %all-to-all-done.refs_0_.refs_1_, bf16[8,264,128]{2,1,0:T(8,128)(2,1)S(1)} %collective-permute-done.5.refs_1_.refs_2_, bf16[2,1024,128]{2,1,0:T(8,128)(2,1)S(1)} %join_keys.1.refs_3_, ...), custom_call_target="tpu_custom_call" | custom-call | tf_op jit(solution)/shard_map/attend_own/pallas_call | solution.py:40
  67.0 5.9 %all-to-all-start.1 = ((bf16[16,128,128]{2,1,0:T(8,128)(2,1)}), bf16[16,128,128]{2,1,0:T(8,128)(2,1)S(1)}, u32[]{:S(2)}, u32[]{:S(2)}) async-start(bf16[16,128,128]{2,1,0:T(8,128)(2,1)} %get-tuple-element.38), calls=%async_computation.1 | async-start | bytes 1048576 | tf_op jit(solution)/shard_map/all_to_all | solution.py:248
  72.8 1.1 %add_sums.1.near_ref = f32[256,1024]{1,0:T(8,128)S(1)} custom-call(bf16[256,1024]{1,0:T(8,128)(2,1)S(1)} %collective-permute-done.7.a_ref, bf16[256,1024]{1,0:T(8,128)(2,1)} %collective-permute-done.8.b_ref), custom_call_target="tpu_custom_call" | custom-call | flops 137438953472 | bytes 1024 | tf_op jit(solution)/shard_map/add_sums/pallas_call | solution.py:40
  74.0 2.3 %collective-permute-done.9.back_ref = bf16[256,1024]{1,0:T(8,128)(2,1)S(1)} collective-permute-done((bf16[256,1024]{1,0:T(8,128)(2,1)}, bf16[256,1024]{1,0:T(8,128)(2,1)S(1)}, u32[]{:S(2)}, u32[]{:S(2)}) %collective-permute-start.9) | collective-permute-done | bytes 524320 | tf_op jit(solution)/shard_map/ppermute | solution.py:197
  76.3 0.3 pack_sums.1
  76.6 0.1 collective-permute-start.10
  76.7 2.7 %collective-permute-start.11 = (bf16[64,1024]{1,0:T(8,128)(2,1)S(1)}, bf16[64,1024]{1,0:T(8,128)(2,1)S(1)}, u32[]{:S(2)}, u32[]{:S(2)}) collective-permute-start(bf16[64,1024]{1,0:T(8,128)(2,1)S(1)} %get-tuple-element.45), channel_id=1, source_target_pairs={{0,96},{32,0},{64,32},{96,64},{1,97},{33,1},{65,33},{97,65},{2,98}... | collective-permute-start | bytes 393224 | tf_op jit(solution)/shard_map/ppermute | solution.py:197
  79.3 2.6 %collective-permute-done.10.b_ref = bf16[64,1024]{1,0:T(8,128)(2,1)S(1)} collective-permute-done((bf16[64,1024]{1,0:T(8,128)(2,1)S(1)}, bf16[64,1024]{1,0:T(8,128)(2,1)S(1)}, u32[]{:S(2)}, u32[]{:S(2)}) %collective-permute-start.10) | collective-permute-done | bytes 131104 | tf_op jit(solution)/shard_map/ppermute | solution.py:197
  82.0 0.7 collective-permute-done.11.c_ref
  82.7 3.2 %collective-permute-done.12.d_ref = bf16[64,1024]{1,0:T(8,128)(2,1)S(1)} collective-permute-done((bf16[64,1024]{1,0:T(8,128)(2,1)S(1)}, bf16[64,1024]{1,0:T(8,128)(2,1)S(1)}, u32[]{:S(2)}, u32[]{:S(2)}) %collective-permute-start.12) | collective-permute-done | bytes 131104 | tf_op jit(solution)/shard_map/ppermute | solution.py:197
  85.9 0.7 finish_keys.1
  86.6 3.6 %all-to-all-done.1.in_ref = bf16[16,128,128]{2,1,0:T(8,128)(2,1)S(1)} async-done(((bf16[16,128,128]{2,1,0:T(8,128)(2,1)}), bf16[16,128,128]{2,1,0:T(8,128)(2,1)S(1)}, u32[]{:S(2)}, u32[]{:S(2)}) %all-to-all-start.1) | async-done | bytes 524320 | tf_op jit(solution)/shard_map/all_to_all | solution.py:248
  90.2 0.7 finish_queries.1
  (10 shorter events, 0.0 us)
Async XLA Ops:
  2.6 14.8 %collective-permute-start.2 = (bf16[64,1024]{1,0:T(8,128)(2,1)}, bf16[64,1024]{1,0:T(8,128)(2,1)S(1)}, u32[]{:S(2)}, u32[]{:S(2)}) collective-permute-start(bf16[64,1024]{1,0:T(8,128)(2,1)} %get-tuple-element.29.own_ref), channel_id=1, source_target_pairs={{0,64},{32,96},{64,0},{96,32},{1,65},{33,97},{65,1},{97,33},{2,66}... | collective-permute-start | bytes 393224 | tf_op jit(solution)/shard_map/ppermute | solution.py:197
  6.5 11.0 %collective-permute-start.1 = (bf16[64,1024]{1,0:T(8,128)(2,1)}, bf16[64,1024]{1,0:T(8,128)(2,1)S(1)}, u32[]{:S(2)}, u32[]{:S(2)}) collective-permute-start(bf16[64,1024]{1,0:T(8,128)(2,1)} %get-tuple-element.29.own_ref), channel_id=1, source_target_pairs={{0,32},{32,64},{64,96},{96,0},{1,33},{33,65},{65,97},{97,1},{2,34}... | collective-permute-start | bytes 393224 | tf_op jit(solution)/shard_map/ppermute | solution.py:197
  6.9 10.6 %collective-permute-start = (bf16[64,1024]{1,0:T(8,128)(2,1)}, bf16[64,1024]{1,0:T(8,128)(2,1)S(1)}, u32[]{:S(2)}, u32[]{:S(2)}) collective-permute-start(bf16[64,1024]{1,0:T(8,128)(2,1)} %get-tuple-element.29.own_ref), channel_id=1, source_target_pairs={{0,96},{32,0},{64,32},{96,64},{1,97},{33,1},{65,33},{97,65},{2,98}... | collective-permute-start | bytes 393224 | tf_op jit(solution)/shard_map/ppermute | solution.py:197
  9.2 8.3 %copy-start = (bf16[64,1024]{1,0:T(8,128)(2,1)S(1)}, bf16[64,1024]{1,0:T(8,128)(2,1)}, u32[]{:S(2)}) copy-start(bf16[64,1024]{1,0:T(8,128)(2,1)} %get-tuple-element.29.own_ref) | copy-start | bytes 393220
  9.2 24.6 %all-to-all-start = ((bf16[8,264,128]{2,1,0:T(8,128)(2,1)}), bf16[8,264,128]{2,1,0:T(8,128)(2,1)S(1)}, u32[]{:S(2)}, u32[]{:S(2)}) async-start(bf16[8,264,128]{2,1,0:T(8,128)(2,1)} %get-tuple-element.27), calls=%async_computation | async-start | bytes 1081344 | tf_op jit(solution)/shard_map/all_to_all | solution.py:220
  17.7 12.0 %collective-permute-start.4 = (bf16[2,1024,128]{2,1,0:T(8,128)(2,1)S(1)}, bf16[2,1024,128]{2,1,0:T(8,128)(2,1)S(1)}, u32[]{:S(2)}, u32[]{:S(2)}) collective-permute-start(bf16[2,1024,128]{2,1,0:T(8,128)(2,1)S(1)} %join_keys.1.refs_3_), channel_id=1, source_target_pairs={{0,6},{2,0},{4,2},{6,4},{1,7},{3,1},{5,3},{7,5},{8,14},{10,8},{12,... | collective-permute-start | bytes 1572872 | tf_op jit(solution)/shard_map/ppermute | solution.py:197
  20.3 12.5 %collective-permute-start.3 = (bf16[2,1024,128]{2,1,0:T(8,128)(2,1)S(1)}, bf16[2,1024,128]{2,1,0:T(8,128)(2,1)S(1)}, u32[]{:S(2)}, u32[]{:S(2)}) collective-permute-start(bf16[2,1024,128]{2,1,0:T(8,128)(2,1)S(1)} %join_keys.1.refs_3_), channel_id=1, source_target_pairs={{0,2},{2,4},{4,6},{6,0},{1,3},{3,5},{5,7},{7,1},{8,10},{10,12},{12... | collective-permute-start | bytes 1572872 | tf_op jit(solution)/shard_map/ppermute | solution.py:197
  33.7 5.3 %collective-permute-start.5 = (bf16[8,264,128]{2,1,0:T(8,128)(2,1)S(1)}, bf16[8,264,128]{2,1,0:T(8,128)(2,1)S(1)}, u32[]{:S(2)}, u32[]{:S(2)}) collective-permute-start(bf16[8,264,128]{2,1,0:T(8,128)(2,1)S(1)} %all-to-all-done.refs_0_.refs_1_), channel_id=1, source_target_pairs={{0,1},{1,0},{2,3},{3,2},{4,5},{5,4},{6,7},{7,6},{8,9},{9,8},{10,11... | collective-permute-start | bytes 1622024 | tf_op jit(solution)/shard_map/ppermute | solution.py:197
  36.3 15.8 %collective-permute-start.6 = (bf16[2,1024,128]{2,1,0:T(8,128)(2,1)S(1)}, bf16[2,1024,128]{2,1,0:T(8,128)(2,1)S(1)}, u32[]{:S(2)}, u32[]{:S(2)}) collective-permute-start(bf16[2,1024,128]{2,1,0:T(8,128)(2,1)S(1)} %join_keys.1.refs_3_), channel_id=1, source_target_pairs={{0,4},{2,6},{4,0},{6,2},{1,5},{3,7},{5,1},{7,3},{8,12},{10,14},{12... | collective-permute-start | bytes 1572872 | tf_op jit(solution)/shard_map/ppermute | solution.py:197
  44.7 22.3 %collective-permute-start.7 = (bf16[256,1024]{1,0:T(8,128)(2,1)S(1)}, bf16[256,1024]{1,0:T(8,128)(2,1)S(1)}, u32[]{:S(2)}, u32[]{:S(2)}) collective-permute-start(bf16[256,1024]{1,0:T(8,128)(2,1)S(1)} %get-tuple-element.37), channel_id=1, source_target_pairs={{0,6},{2,0},{4,2},{6,4},{1,7},{3,1},{5,3},{7,5},{8,14},{10,8},{12,... | collective-permute-start | bytes 1572872 | tf_op jit(solution)/shard_map/ppermute | solution.py:197
  51.9 21.0 %collective-permute-start.8 = (bf16[256,1024]{1,0:T(8,128)(2,1)S(1)}, bf16[256,1024]{1,0:T(8,128)(2,1)}, u32[]{:S(2)}, u32[]{:S(2)}) collective-permute-start(bf16[256,1024]{1,0:T(8,128)(2,1)S(1)} %get-tuple-element.40), channel_id=1, source_target_pairs={{0,2},{2,4},{4,6},{6,0},{1,3},{3,5},{5,7},{7,1},{8,10},{10,12},{12... | collective-permute-start | bytes 1572872 | tf_op jit(solution)/shard_map/ppermute | solution.py:197
  58.5 17.8 %collective-permute-start.9 = (bf16[256,1024]{1,0:T(8,128)(2,1)}, bf16[256,1024]{1,0:T(8,128)(2,1)S(1)}, u32[]{:S(2)}, u32[]{:S(2)}) collective-permute-start(bf16[256,1024]{1,0:T(8,128)(2,1)} %get-tuple-element.42), channel_id=1, source_target_pairs={{0,4},{2,6},{4,0},{6,2},{1,5},{3,7},{5,1},{7,3},{8,12},{10,14},{12... | collective-permute-start | bytes 1572872 | tf_op jit(solution)/shard_map/ppermute | solution.py:197
  67.0 23.2 %all-to-all-start.1 = ((bf16[16,128,128]{2,1,0:T(8,128)(2,1)}), bf16[16,128,128]{2,1,0:T(8,128)(2,1)S(1)}, u32[]{:S(2)}, u32[]{:S(2)}) async-start(bf16[16,128,128]{2,1,0:T(8,128)(2,1)} %get-tuple-element.38), calls=%async_computation.1 | async-start | bytes 1048576 | tf_op jit(solution)/shard_map/all_to_all | solution.py:248
  76.6 5.4 %collective-permute-start.10 = (bf16[64,1024]{1,0:T(8,128)(2,1)S(1)}, bf16[64,1024]{1,0:T(8,128)(2,1)S(1)}, u32[]{:S(2)}, u32[]{:S(2)}) collective-permute-start(bf16[64,1024]{1,0:T(8,128)(2,1)S(1)} %get-tuple-element.44), channel_id=1, source_target_pairs={{0,32},{32,64},{64,96},{96,0},{1,33},{33,65},{65,97},{97,1},{2,34}... | collective-permute-start | bytes 393224 | tf_op jit(solution)/shard_map/ppermute | solution.py:197
  76.7 6.0 %collective-permute-start.11 = (bf16[64,1024]{1,0:T(8,128)(2,1)S(1)}, bf16[64,1024]{1,0:T(8,128)(2,1)S(1)}, u32[]{:S(2)}, u32[]{:S(2)}) collective-permute-start(bf16[64,1024]{1,0:T(8,128)(2,1)S(1)} %get-tuple-element.45), channel_id=1, source_target_pairs={{0,96},{32,0},{64,32},{96,64},{1,97},{33,1},{65,33},{97,65},{2,98}... | collective-permute-start | bytes 393224 | tf_op jit(solution)/shard_map/ppermute | solution.py:197
  79.3 6.5 %collective-permute-start.12 = (bf16[64,1024]{1,0:T(8,128)(2,1)S(1)}, bf16[64,1024]{1,0:T(8,128)(2,1)S(1)}, u32[]{:S(2)}, u32[]{:S(2)}) collective-permute-start(bf16[64,1024]{1,0:T(8,128)(2,1)S(1)} %get-tuple-element.46), channel_id=1, source_target_pairs={{0,64},{32,96},{64,0},{96,32},{1,65},{33,97},{65,1},{97,33},{2,66}... | collective-permute-start | bytes 393224 | tf_op jit(solution)/shard_map/ppermute | solution.py:197

commit v6 on v5

--- a/solution.py
+++ b/solution.py
@@ -262,7 +262,7 @@
         scratch=[pltpu.VMEM((8 * FEATS, KEYS), F32)],
         scalars=1,
     )
-    sums = [mine, shift(to_next, "y", 4, 1), shift(to_prev, "y", 4, 3), shift(to_far, "y", 4, 2)]
+    sums = [mine, shift(to_far, "y", 4, 2), shift(to_next, "y", 4, 1), shift(to_prev, "y", 4, 3)]
     d_queries = call(finish_queries, sds((ROWS, 2 * HEAD_DIM), BF16), [dq], "finish_queries")
     d_keys, d_values = call(
         finish_keys, (sds((FEATS, KEYS), BF16),) * 2, sums, "finish_keys"

time: 91.2 us -> 91.2 us (level)
    ppermute x13, waiting for transfers between devices: 21.4 us -> 18.9 us  [shift(): lax.ppermute(value, axis, [(i, (i + amount) % size) for i in range(size)])]
    all_to_all x1, waiting for transfers between devices: 3.6 us -> 5.98 us  [per_device(): dq = lax.all_to_all(dq, Z + ('c',), 0, 0, tiled=True)]
  transfers between devices with their start and end apart: 15 -> 15, of which waited for: 8 -> 7; matrix products, arithmetic and copies ran while one was open for 0% -> 0% of each run, Pallas kernels for 29% -> 29%
where the time goes in v6:
time: 91.2 us; the launch traced here: 90.9 us
  starting transfers between devices  35.2 us (39%)
  Pallas kernels  29.2 us (32%)
  waiting for transfers between devices  25.8 us (28%)
    pallas_call x9, Pallas kernels, call(): pl.pallas_call(body, out_shape=out_shape, in_specs=[SMEM] * scalars + [VM...  27.2 us
    ppermute x13, starting transfers between devices, shift(): lax.ppermute(value, axis, [(i, (i + amount) % size) for i in range(size)])  20.9 us
    ppermute x13, waiting for transfers between devices, shift(): lax.ppermute(value, axis, [(i, (i + amount) % size) for i in range(size)])  18.9 us
    all_to_all x1, starting transfers between devices, per_device(): q_own = lax.all_to_all(msg, Z, 0, 0, tiled=True)  8.32 us
    all_to_all x1, waiting for transfers between devices, per_device(): dq = lax.all_to_all(dq, Z + ('c',), 0, 0, tiled=True)  5.98 us
    all_to_all x1, starting transfers between devices, per_device(): dq = lax.all_to_all(dq, Z + ('c',), 0, 0, tiled=True)  5.89 us
    pallas_call x1, Pallas kernels, per_device(): pl.pallas_call(prepare, out_shape=(sds((8, MSG, HEAD_DIM), BF16), sds((2...  2.01 us
  transfers between devices with their start and end apart: 15, of which 7 were waited for; matrix products, arithmetic and copies ran while one was open for 0% of the time, Pallas kernels for 29%

profile of v6, /device:TPU:1, one launch (start us, length us, event | category | flops | bytes accessed | tf_op | source)
XLA Modules:
  0.0 90.9 jit_solution(16847307731630644005)
XLA Ops:
  0.6 2.0 %prepare.1 = (bf16[8,264,128]{2,1,0:T(8,128)(2,1)}, bf16[64,1024]{1,0:T(8,128)(2,1)}) custom-call(bf16[128,256]{1,0:T(8,128)(2,1)} %q_hbm.1, bf16[128,256]{1,0:T(8,128)(2,1)} %do_hbm.1, bf16[128,256]{1,0:T(8,128)(2,1)} %o_hbm.1, f32[2,128]{1,0:T(2,128)} %lse_hbm.1, bf16[32,1024]{1,0:T(8,128)(2,1)} %bitcast.6, bf16[32,1024]{1,0:T(8,128)(2,1)} %bitcast.7), custom_call_target="tpu_custom_call" | custom-call | bytes 1048576 | tf_op jit(solution)/shard_map/prepare/pallas_call | solution.py:210
  2.6 3.8 %collective-permute-start.2 = (bf16[64,1024]{1,0:T(8,128)(2,1)}, bf16[64,1024]{1,0:T(8,128)(2,1)S(1)}, u32[]{:S(2)}, u32[]{:S(2)}) collective-permute-start(bf16[64,1024]{1,0:T(8,128)(2,1)} %get-tuple-element.29.own_ref), channel_id=1, source_target_pairs={{0,64},{32,96},{64,0},{96,32},{1,65},{33,97},{65,1},{97,33},{2,66}... | collective-permute-start | bytes 393224 | tf_op jit(solution)/shard_map/ppermute | solution.py:197
  6.5 0.4 collective-permute-start.1
  6.9 2.3 %collective-permute-start = (bf16[64,1024]{1,0:T(8,128)(2,1)}, bf16[64,1024]{1,0:T(8,128)(2,1)S(1)}, u32[]{:S(2)}, u32[]{:S(2)}) collective-permute-start(bf16[64,1024]{1,0:T(8,128)(2,1)} %get-tuple-element.29.own_ref), channel_id=1, source_target_pairs={{0,96},{32,0},{64,32},{96,64},{1,97},{33,1},{65,33},{97,65},{2,98}... | collective-permute-start | bytes 393224 | tf_op jit(solution)/shard_map/ppermute | solution.py:197
  9.2 8.3 %all-to-all-start = ((bf16[8,264,128]{2,1,0:T(8,128)(2,1)}), bf16[8,264,128]{2,1,0:T(8,128)(2,1)S(1)}, u32[]{:S(2)}, u32[]{:S(2)}) async-start(bf16[8,264,128]{2,1,0:T(8,128)(2,1)} %get-tuple-element.27), calls=%async_computation | async-start | bytes 1081344 | tf_op jit(solution)/shard_map/all_to_all | solution.py:220
  17.5 0.0 collective-permute-done.2.far_ref
  17.5 0.2 join_keys.1.refs_3_
  17.7 2.6 %collective-permute-start.4 = (bf16[2,1024,128]{2,1,0:T(8,128)(2,1)S(1)}, bf16[2,1024,128]{2,1,0:T(8,128)(2,1)S(1)}, u32[]{:S(2)}, u32[]{:S(2)}) collective-permute-start(bf16[2,1024,128]{2,1,0:T(8,128)(2,1)S(1)} %join_keys.1.refs_3_), channel_id=1, source_target_pairs={{0,6},{2,0},{4,2},{6,4},{1,7},{3,1},{5,3},{7,5},{8,14},{10,8},{12,... | collective-permute-start | bytes 1572872 | tf_op jit(solution)/shard_map/ppermute | solution.py:197
  20.3 9.4 %collective-permute-done.4.refs_2_ = bf16[2,1024,128]{2,1,0:T(8,128)(2,1)S(1)} collective-permute-done((bf16[2,1024,128]{2,1,0:T(8,128)(2,1)S(1)}, bf16[2,1024,128]{2,1,0:T(8,128)(2,1)S(1)}, u32[]{:S(2)}, u32[]{:S(2)}) %collective-permute-start.4) | collective-permute-done | bytes 524320 | tf_op jit(solution)/shard_map/ppermute | solution.py:197
  29.7 3.1 %collective-permute-done.3.refs_2_ = bf16[2,1024,128]{2,1,0:T(8,128)(2,1)S(1)} collective-permute-done((bf16[2,1024,128]{2,1,0:T(8,128)(2,1)S(1)}, bf16[2,1024,128]{2,1,0:T(8,128)(2,1)S(1)}, u32[]{:S(2)}, u32[]{:S(2)}) %collective-permute-start.3) | collective-permute-done | bytes 524320 | tf_op jit(solution)/shard_map/ppermute | solution.py:197
  32.8 0.9 all-to-all-done.refs_0_.refs_1_
  33.7 2.5 %collective-permute-start.5 = (bf16[8,264,128]{2,1,0:T(8,128)(2,1)S(1)}, bf16[8,264,128]{2,1,0:T(8,128)(2,1)S(1)}, u32[]{:S(2)}, u32[]{:S(2)}) collective-permute-start(bf16[8,264,128]{2,1,0:T(8,128)(2,1)S(1)} %all-to-all-done.refs_0_.refs_1_), channel_id=1, source_target_pairs={{0,1},{1,0},{2,3},{3,2},{4,5},{5,4},{6,7},{7,6},{8,9},{9,8},{10,11... | collective-permute-start | bytes 1622024 | tf_op jit(solution)/shard_map/ppermute | solution.py:197
  36.3 2.7 %collective-permute-start.6 = (bf16[2,1024,128]{2,1,0:T(8,128)(2,1)S(1)}, bf16[2,1024,128]{2,1,0:T(8,128)(2,1)S(1)}, u32[]{:S(2)}, u32[]{:S(2)}) collective-permute-start(bf16[2,1024,128]{2,1,0:T(8,128)(2,1)S(1)} %join_keys.1.refs_3_), channel_id=1, source_target_pairs={{0,4},{2,6},{4,0},{6,2},{1,5},{3,7},{5,1},{7,3},{8,12},{10,14},{12... | collective-permute-start | bytes 1572872 | tf_op jit(solution)/shard_map/ppermute | solution.py:197
  39.0 5.6 %attend_prev.1 = (f32[2048,128]{1,0:T(8,128)S(1)}, bf16[256,1024]{1,0:T(8,128)(2,1)S(1)}) custom-call(bf16[8,264,128]{2,1,0:T(8,128)(2,1)S(1)} %all-to-all-done.refs_0_.refs_1_, bf16[8,264,128]{2,1,0:T(8,128)(2,1)S(1)} %collective-permute-done.5.refs_1_.refs_2_, bf16[2,1024,128]{2,1,0:T(8,128)(2,1)S(1)} %collective-permute-done.3.refs_2_), custom_call_target="tpu_custom_call" | custom-call | tf_op jit(solution)/shard_map/attend_prev/pallas_call | solution.py:40
  44.7 1.5 %collective-permute-start.7 = (bf16[256,1024]{1,0:T(8,128)(2,1)S(1)}, bf16[256,1024]{1,0:T(8,128)(2,1)S(1)}, u32[]{:S(2)}, u32[]{:S(2)}) collective-permute-start(bf16[256,1024]{1,0:T(8,128)(2,1)S(1)} %get-tuple-element.37), channel_id=1, source_target_pairs={{0,6},{2,0},{4,2},{6,4},{1,7},{3,1},{5,3},{7,5},{8,14},{10,8},{12,... | collective-permute-start | bytes 1572872 | tf_op jit(solution)/shard_map/ppermute | solution.py:197
  46.2 5.6 %attend_next.1 = (f32[2048,128]{1,0:T(8,128)S(1)}, bf16[256,1024]{1,0:T(8,128)(2,1)S(1)}) custom-call(bf16[8,264,128]{2,1,0:T(8,128)(2,1)S(1)} %all-to-all-done.refs_0_.refs_1_, bf16[8,264,128]{2,1,0:T(8,128)(2,1)S(1)} %collective-permute-done.5.refs_1_.refs_2_, bf16[2,1024,128]{2,1,0:T(8,128)(2,1)S(1)} %collective-permute-done.4.refs_2_, ...), custom_call_target="tpu_custom_call" | custom-call | tf_op jit(solution)/shard_map/attend_next/pallas_call | solution.py:40
  51.9 0.3 collective-permute-start.8
  52.1 6.4 %attend_far.1 = (f32[2048,128]{1,0:T(8,128)S(1)}, bf16[256,1024]{1,0:T(8,128)(2,1)}) custom-call(bf16[8,264,128]{2,1,0:T(8,128)(2,1)S(1)} %all-to-all-done.refs_0_.refs_1_, bf16[8,264,128]{2,1,0:T(8,128)(2,1)S(1)} %collective-permute-done.5.refs_1_.refs_2_, bf16[2,1024,128]{2,1,0:T(8,128)(2,1)S(1)} %collective-permute-done.6.refs_2_, ...), custom_call_target="tpu_custom_call" | custom-call | tf_op jit(solution)/shard_map/attend_far/pallas_call | solution.py:40
  58.5 2.0 %collective-permute-start.9 = (bf16[256,1024]{1,0:T(8,128)(2,1)}, bf16[256,1024]{1,0:T(8,128)(2,1)S(1)}, u32[]{:S(2)}, u32[]{:S(2)}) collective-permute-start(bf16[256,1024]{1,0:T(8,128)(2,1)} %get-tuple-element.42), channel_id=1, source_target_pairs={{0,4},{2,6},{4,0},{6,2},{1,5},{3,7},{5,1},{7,3},{8,12},{10,14},{12... | collective-permute-start | bytes 1572872 | tf_op jit(solution)/shard_map/ppermute | solution.py:197
  60.5 6.5 %attend_own.1 = (bf16[16,128,128]{2,1,0:T(8,128)(2,1)}, bf16[256,1024]{1,0:T(8,128)(2,1)S(1)}) custom-call(s32[1]{0:T(128)} %bitcast.1.refs_0_, bf16[8,264,128]{2,1,0:T(8,128)(2,1)S(1)} %all-to-all-done.refs_0_.refs_1_, bf16[8,264,128]{2,1,0:T(8,128)(2,1)S(1)} %collective-permute-done.5.refs_1_.refs_2_, bf16[2,1024,128]{2,1,0:T(8,128)(2,1)S(1)} %join_keys.1.refs_3_, ...), custom_call_target="tpu_custom_call" | custom-call | tf_op jit(solution)/shard_map/attend_own/pallas_call | solution.py:40
  67.0 5.9 %all-to-all-start.1 = ((bf16[16,128,128]{2,1,0:T(8,128)(2,1)}), bf16[16,128,128]{2,1,0:T(8,128)(2,1)S(1)}, u32[]{:S(2)}, u32[]{:S(2)}) async-start(bf16[16,128,128]{2,1,0:T(8,128)(2,1)} %get-tuple-element.38), calls=%async_computation.1 | async-start | bytes 1048576 | tf_op jit(solution)/shard_map/all_to_all | solution.py:248
  72.8 1.1 %add_sums.1.near_ref = f32[256,1024]{1,0:T(8,128)S(1)} custom-call(bf16[256,1024]{1,0:T(8,128)(2,1)S(1)} %collective-permute-done.7.a_ref, bf16[256,1024]{1,0:T(8,128)(2,1)} %collective-permute-done.8.b_ref), custom_call_target="tpu_custom_call" | custom-call | flops 137438953472 | bytes 1024 | tf_op jit(solution)/shard_map/add_sums/pallas_call | solution.py:40
  74.0 2.3 %collective-permute-done.9.back_ref = bf16[256,1024]{1,0:T(8,128)(2,1)S(1)} collective-permute-done((bf16[256,1024]{1,0:T(8,128)(2,1)}, bf16[256,1024]{1,0:T(8,128)(2,1)S(1)}, u32[]{:S(2)}, u32[]{:S(2)}) %collective-permute-start.9) | collective-permute-done | bytes 524320 | tf_op jit(solution)/shard_map/ppermute | solution.py:197
  76.3 0.3 pack_sums.1
  76.6 0.1 collective-permute-start.10
  76.7 0.6 collective-permute-start.11
  77.3 2.2 %collective-permute-start.12 = (bf16[64,1024]{1,0:T(8,128)(2,1)S(1)}, bf16[64,1024]{1,0:T(8,128)(2,1)S(1)}, u32[]{:S(2)}, u32[]{:S(2)}) collective-permute-start(bf16[64,1024]{1,0:T(8,128)(2,1)S(1)} %get-tuple-element.46), channel_id=1, source_target_pairs={{0,96},{32,0},{64,32},{96,64},{1,97},{33,1},{65,33},{97,65},{2,98}... | collective-permute-start | bytes 393224 | tf_op jit(solution)/shard_map/ppermute | solution.py:197
  79.4 2.9 %collective-permute-done.10.b_ref = bf16[64,1024]{1,0:T(8,128)(2,1)S(1)} collective-permute-done((bf16[64,1024]{1,0:T(8,128)(2,1)S(1)}, bf16[64,1024]{1,0:T(8,128)(2,1)S(1)}, u32[]{:S(2)}, u32[]{:S(2)}) %collective-permute-start.10) | collective-permute-done | bytes 131104 | tf_op jit(solution)/shard_map/ppermute | solution.py:197
  82.3 1.2 %collective-permute-done.11.c_ref = bf16[64,1024]{1,0:T(8,128)(2,1)S(1)} collective-permute-done((bf16[64,1024]{1,0:T(8,128)(2,1)S(1)}, bf16[64,1024]{1,0:T(8,128)(2,1)S(1)}, u32[]{:S(2)}, u32[]{:S(2)}) %collective-permute-start.11) | collective-permute-done | bytes 131104 | tf_op jit(solution)/shard_map/ppermute | solution.py:197
  83.5 0.7 finish_keys.1
  84.2 6.0 %all-to-all-done.1.in_ref = bf16[16,128,128]{2,1,0:T(8,128)(2,1)S(1)} async-done(((bf16[16,128,128]{2,1,0:T(8,128)(2,1)}), bf16[16,128,128]{2,1,0:T(8,128)(2,1)S(1)}, u32[]{:S(2)}, u32[]{:S(2)}) %all-to-all-start.1) | async-done | bytes 524320 | tf_op jit(solution)/shard_map/all_to_all | solution.py:248
  90.2 0.7 finish_queries.1
  (10 shorter events, 0.0 us)
Async XLA Ops:
  2.6 14.8 %collective-permute-start.2 = (bf16[64,1024]{1,0:T(8,128)(2,1)}, bf16[64,1024]{1,0:T(8,128)(2,1)S(1)}, u32[]{:S(2)}, u32[]{:S(2)}) collective-permute-start(bf16[64,1024]{1,0:T(8,128)(2,1)} %get-tuple-element.29.own_ref), channel_id=1, source_target_pairs={{0,64},{32,96},{64,0},{96,32},{1,65},{33,97},{65,1},{97,33},{2,66}... | collective-permute-start | bytes 393224 | tf_op jit(solution)/shard_map/ppermute | solution.py:197
  6.5 11.0 %collective-permute-start.1 = (bf16[64,1024]{1,0:T(8,128)(2,1)}, bf16[64,1024]{1,0:T(8,128)(2,1)S(1)}, u32[]{:S(2)}, u32[]{:S(2)}) collective-permute-start(bf16[64,1024]{1,0:T(8,128)(2,1)} %get-tuple-element.29.own_ref), channel_id=1, source_target_pairs={{0,32},{32,64},{64,96},{96,0},{1,33},{33,65},{65,97},{97,1},{2,34}... | collective-permute-start | bytes 393224 | tf_op jit(solution)/shard_map/ppermute | solution.py:197
  6.9 10.6 %collective-permute-start = (bf16[64,1024]{1,0:T(8,128)(2,1)}, bf16[64,1024]{1,0:T(8,128)(2,1)S(1)}, u32[]{:S(2)}, u32[]{:S(2)}) collective-permute-start(bf16[64,1024]{1,0:T(8,128)(2,1)} %get-tuple-element.29.own_ref), channel_id=1, source_target_pairs={{0,96},{32,0},{64,32},{96,64},{1,97},{33,1},{65,33},{97,65},{2,98}... | collective-permute-start | bytes 393224 | tf_op jit(solution)/shard_map/ppermute | solution.py:197
  9.2 8.3 %copy-start = (bf16[64,1024]{1,0:T(8,128)(2,1)S(1)}, bf16[64,1024]{1,0:T(8,128)(2,1)}, u32[]{:S(2)}) copy-start(bf16[64,1024]{1,0:T(8,128)(2,1)} %get-tuple-element.29.own_ref) | copy-start | bytes 393220
  9.2 24.6 %all-to-all-start = ((bf16[8,264,128]{2,1,0:T(8,128)(2,1)}), bf16[8,264,128]{2,1,0:T(8,128)(2,1)S(1)}, u32[]{:S(2)}, u32[]{:S(2)}) async-start(bf16[8,264,128]{2,1,0:T(8,128)(2,1)} %get-tuple-element.27), calls=%async_computation | async-start | bytes 1081344 | tf_op jit(solution)/shard_map/all_to_all | solution.py:220
  17.7 12.0 %collective-permute-start.4 = (bf16[2,1024,128]{2,1,0:T(8,128)(2,1)S(1)}, bf16[2,1024,128]{2,1,0:T(8,128)(2,1)S(1)}, u32[]{:S(2)}, u32[]{:S(2)}) collective-permute-start(bf16[2,1024,128]{2,1,0:T(8,128)(2,1)S(1)} %join_keys.1.refs_3_), channel_id=1, source_target_pairs={{0,6},{2,0},{4,2},{6,4},{1,7},{3,1},{5,3},{7,5},{8,14},{10,8},{12,... | collective-permute-start | bytes 1572872 | tf_op jit(solution)/shard_map/ppermute | solution.py:197
  20.3 12.5 %collective-permute-start.3 = (bf16[2,1024,128]{2,1,0:T(8,128)(2,1)S(1)}, bf16[2,1024,128]{2,1,0:T(8,128)(2,1)S(1)}, u32[]{:S(2)}, u32[]{:S(2)}) collective-permute-start(bf16[2,1024,128]{2,1,0:T(8,128)(2,1)S(1)} %join_keys.1.refs_3_), channel_id=1, source_target_pairs={{0,2},{2,4},{4,6},{6,0},{1,3},{3,5},{5,7},{7,1},{8,10},{10,12},{12... | collective-permute-start | bytes 1572872 | tf_op jit(solution)/shard_map/ppermute | solution.py:197
  33.7 5.3 %collective-permute-start.5 = (bf16[8,264,128]{2,1,0:T(8,128)(2,1)S(1)}, bf16[8,264,128]{2,1,0:T(8,128)(2,1)S(1)}, u32[]{:S(2)}, u32[]{:S(2)}) collective-permute-start(bf16[8,264,128]{2,1,0:T(8,128)(2,1)S(1)} %all-to-all-done.refs_0_.refs_1_), channel_id=1, source_target_pairs={{0,1},{1,0},{2,3},{3,2},{4,5},{5,4},{6,7},{7,6},{8,9},{9,8},{10,11... | collective-permute-start | bytes 1622024 | tf_op jit(solution)/shard_map/ppermute | solution.py:197
  36.3 15.8 %collective-permute-start.6 = (bf16[2,1024,128]{2,1,0:T(8,128)(2,1)S(1)}, bf16[2,1024,128]{2,1,0:T(8,128)(2,1)S(1)}, u32[]{:S(2)}, u32[]{:S(2)}) collective-permute-start(bf16[2,1024,128]{2,1,0:T(8,128)(2,1)S(1)} %join_keys.1.refs_3_), channel_id=1, source_target_pairs={{0,4},{2,6},{4,0},{6,2},{1,5},{3,7},{5,1},{7,3},{8,12},{10,14},{12... | collective-permute-start | bytes 1572872 | tf_op jit(solution)/shard_map/ppermute | solution.py:197
  44.7 22.3 %collective-permute-start.7 = (bf16[256,1024]{1,0:T(8,128)(2,1)S(1)}, bf16[256,1024]{1,0:T(8,128)(2,1)S(1)}, u32[]{:S(2)}, u32[]{:S(2)}) collective-permute-start(bf16[256,1024]{1,0:T(8,128)(2,1)S(1)} %get-tuple-element.37), channel_id=1, source_target_pairs={{0,6},{2,0},{4,2},{6,4},{1,7},{3,1},{5,3},{7,5},{8,14},{10,8},{12,... | collective-permute-start | bytes 1572872 | tf_op jit(solution)/shard_map/ppermute | solution.py:197
  51.9 21.0 %collective-permute-start.8 = (bf16[256,1024]{1,0:T(8,128)(2,1)S(1)}, bf16[256,1024]{1,0:T(8,128)(2,1)}, u32[]{:S(2)}, u32[]{:S(2)}) collective-permute-start(bf16[256,1024]{1,0:T(8,128)(2,1)S(1)} %get-tuple-element.40), channel_id=1, source_target_pairs={{0,2},{2,4},{4,6},{6,0},{1,3},{3,5},{5,7},{7,1},{8,10},{10,12},{12... | collective-permute-start | bytes 1572872 | tf_op jit(solution)/shard_map/ppermute | solution.py:197
  58.5 17.8 %collective-permute-start.9 = (bf16[256,1024]{1,0:T(8,128)(2,1)}, bf16[256,1024]{1,0:T(8,128)(2,1)S(1)}, u32[]{:S(2)}, u32[]{:S(2)}) collective-permute-start(bf16[256,1024]{1,0:T(8,128)(2,1)} %get-tuple-element.42), channel_id=1, source_target_pairs={{0,4},{2,6},{4,0},{6,2},{1,5},{3,7},{5,1},{7,3},{8,12},{10,14},{12... | collective-permute-start | bytes 1572872 | tf_op jit(solution)/shard_map/ppermute | solution.py:197
  67.0 23.2 %all-to-all-start.1 = ((bf16[16,128,128]{2,1,0:T(8,128)(2,1)}), bf16[16,128,128]{2,1,0:T(8,128)(2,1)S(1)}, u32[]{:S(2)}, u32[]{:S(2)}) async-start(bf16[16,128,128]{2,1,0:T(8,128)(2,1)} %get-tuple-element.38), calls=%async_computation.1 | async-start | bytes 1048576 | tf_op jit(solution)/shard_map/all_to_all | solution.py:248
  76.6 5.7 %collective-permute-start.10 = (bf16[64,1024]{1,0:T(8,128)(2,1)S(1)}, bf16[64,1024]{1,0:T(8,128)(2,1)S(1)}, u32[]{:S(2)}, u32[]{:S(2)}) collective-permute-start(bf16[64,1024]{1,0:T(8,128)(2,1)S(1)} %get-tuple-element.44), channel_id=1, source_target_pairs={{0,64},{32,96},{64,0},{96,32},{1,65},{33,97},{65,1},{97,33},{2,66}... | collective-permute-start | bytes 393224 | tf_op jit(solution)/shard_map/ppermute | solution.py:197
  76.7 6.8 %collective-permute-start.11 = (bf16[64,1024]{1,0:T(8,128)(2,1)S(1)}, bf16[64,1024]{1,0:T(8,128)(2,1)S(1)}, u32[]{:S(2)}, u32[]{:S(2)}) collective-permute-start(bf16[64,1024]{1,0:T(8,128)(2,1)S(1)} %get-tuple-element.45), channel_id=1, source_target_pairs={{0,32},{32,64},{64,96},{96,0},{1,33},{33,65},{65,97},{97,1},{2,34}... | collective-permute-start | bytes 393224 | tf_op jit(solution)/shard_map/ppermute | solution.py:197
  77.3 6.2 %collective-permute-start.12 = (bf16[64,1024]{1,0:T(8,128)(2,1)S(1)}, bf16[64,1024]{1,0:T(8,128)(2,1)S(1)}, u32[]{:S(2)}, u32[]{:S(2)}) collective-permute-start(bf16[64,1024]{1,0:T(8,128)(2,1)S(1)} %get-tuple-element.46), channel_id=1, source_target_pairs={{0,96},{32,0},{64,32},{96,64},{1,97},{33,1},{65,33},{97,65},{2,98}... | collective-permute-start | bytes 393224 | tf_op jit(solution)/shard_map/ppermute | solution.py:197
